TPU v7x, 32 devices: a whole 2x2x4 slice. The times are simulated.
32 devices in a mesh: row: 8 (over y, x, core), col: 4 (over z).
Axes of the slice: x: 2, y: 2, z: 4, core: 2. Of those that a mesh axis runs over, the one named last changes fastest.
Arguments:
- tokens: bfloat16 [32768, 768], P(('row', 'col')), may hold values from -6 to 6
- segment: int32 [32, 1024], replicated, may hold values from 0 to 63, never falling along the last dimension, each value on 1 to 512 neighbouring positions
- w_qkv: bfloat16 [768, 2304], P('row', 'col'), may hold values from -0.21875 to 0.21875
- w_out: bfloat16 [768, 768], P('row', 'col'), may hold values from -0.875 to 0.875
- w_up: bfloat16 [768, 3072], P('row', 'col'), may hold values from -0.21875 to 0.21875
- w_down: bfloat16 [3072, 768], P('row', 'col'), may hold values from -0.109375 to 0.109375
- bias_query: float32 [768], replicated, may hold values from -3 to 3
- bias_value: float32 [768], replicated, may hold values from -3 to 3
- bias_out: float32 [768], replicated, may hold values from -3 to 3
- gain_attn: float32 [768], replicated, may hold values from 0.25 to 1.75
- shift_attn: float32 [768], replicated, may hold values from -3 to 3
- bias_up: float32 [3072], replicated, may hold values from -3 to 3
- bias_down: float32 [768], replicated, may hold values from -3 to 3
- gain_ffn: float32 [768], replicated, may hold values from 0.25 to 1.75
- shift_ffn: float32 [768], replicated, may hold values from -3 to 3
- cotangent: bfloat16 [32768, 768], P(('row', 'col')), may hold values from -6 to 6
Outputs:
- layer_out: bfloat16 [32768, 768], P(('row', 'col'))
- grad_tokens: float32 [32768, 768], P(('row', 'col'))
- grad_qkv: float32 [768, 2304], P('row', 'col')
- grad_out: float32 [768, 768], P('row', 'col')
- grad_up: float32 [768, 3072], P('row', 'col')
- grad_down: float32 [3072, 768], P('row', 'col')
- grad_bias_query: float32 [768], replicated
- grad_bias_value: float32 [768], replicated
- grad_bias_out: float32 [768], replicated
- grad_gain_attn: float32 [768], replicated
- grad_shift_attn: float32 [768], replicated
- grad_bias_up: float32 [3072], replicated
- grad_bias_down: float32 [768], replicated
- grad_gain_ffn: float32 [768], replicated
- grad_shift_ffn: float32 [768], replicated
Inputs may be any that keep to these rules, and one draw needn't show every extreme that they name: `segment`: within each packed sequence the document numbers never fall; a document is a run of equal numbers, and some document has 512 tokens.
All inputs are finite; a program needn't handle non-finite values.
Results may differ from a plain program's by a relative error of at most 0.019.
Values may be sent and summed in bfloat16 or wider, within the bound.
A program may use at most 192 MiB of HBM per device.

v0:
```python
import jax
import jax.numpy as jnp
from jax import lax
from jax.sharding import PartitionSpec as P

HEADS = 12
HEAD_DIM = 64
LEN = 1024


norm_eps = 1e-05
masked_score = -1e30


def gather_block(blocks):
    widened = (
        lax.all_gather(blocks[0], "col", axis=1, tiled=True),
        lax.all_gather(blocks[1], "col", axis=1, tiled=True),
    )
    return (
        lax.all_gather(widened[0], "row", axis=0, tiled=True),
        lax.all_gather(widened[1], "row", axis=0, tiled=True),
    )


def reduce_grads(grads):
    narrowed = (
        lax.psum_scatter(
            grads[0].astype(jnp.bfloat16), "col", scatter_dimension=1, tiled=True
        ).astype(jnp.float32),
        lax.psum_scatter(
            grads[1].astype(jnp.bfloat16), "col", scatter_dimension=1, tiled=True
        ).astype(jnp.float32),
    )
    return (
        lax.psum_scatter(
            narrowed[0].astype(jnp.bfloat16), "row", scatter_dimension=0, tiled=True
        ).astype(jnp.float32),
        lax.psum_scatter(
            narrowed[1].astype(jnp.bfloat16), "row", scatter_dimension=0, tiled=True
        ).astype(jnp.float32),
    )


def dot_rows(left, right):
    return lax.dot_general(
        left, right, (((0,), (0,)), ((), ())), preferred_element_type=jnp.float32
    )


def dot_back(left, right):
    return lax.dot_general(
        left, right, (((1,), (1,)), ((), ())), preferred_element_type=jnp.float32
    )


def norm_rows(resid, gain, shift):
    centre = resid - jnp.mean(resid, axis=1, keepdims=True)
    factor = lax.rsqrt(jnp.mean(centre * centre, axis=1, keepdims=True) + norm_eps)
    normed = centre * factor
    return (normed * gain + shift, normed, factor)


def norm_back(grad_result, normed, factor, gain):
    grad_normed = grad_result * gain
    grad_resid = factor * (
        grad_normed
        - jnp.mean(grad_normed, axis=1, keepdims=True)
        - normed * jnp.mean(grad_normed * normed, axis=1, keepdims=True)
    )
    return (grad_resid, jnp.sum(grad_result * normed, axis=0), jnp.sum(grad_result, axis=0))


def gelu_exact(value):
    return jax.nn.gelu(value, approximate=False)


def pair_scores(query_part, key_part, seg_query, seg_key):
    query_heads = query_part.reshape(query_part.shape[0], 2, HEAD_DIM)
    key_heads = key_part.reshape(key_part.shape[0], 2, HEAD_DIM)
    raw = jnp.einsum("qhd,khd->hqk", query_heads, key_heads, preferred_element_type=jnp.float32)
    same = seg_query[:, None] == seg_key[None, :]
    return jnp.where(same[None], raw * HEAD_DIM ** (-0.5), masked_score)


def per_device(
    tokens,
    segment,
    w_qkv,
    w_out,
    w_up,
    w_down,
    bias_query,
    bias_value,
    bias_out,
    gain_attn,
    shift_attn,
    bias_up,
    bias_down,
    gain_ffn,
    shift_ffn,
    cotangent,
):
    model = tokens.shape[1]
    tok_rows = tokens.shape[0]
    pairs = HEADS // 2
    width = 2 * HEAD_DIM
    qlen = min(tok_rows, LEN)
    local_seqs = tok_rows // qlen
    item_count = local_seqs * pairs
    device_at = lax.axis_index("row") * lax.axis_size("col") + lax.axis_index("col")
    seq_first = device_at * tok_rows // LEN
    attn_qkv, attn_out = gather_block((w_qkv, w_out))
    ffn_up, ffn_down = gather_block((w_up, w_down))
    projected = jnp.dot(tokens, attn_qkv, preferred_element_type=jnp.float32)
    queries = (projected[:, :model] + bias_query).astype(jnp.bfloat16)
    keys_values = jnp.concatenate(
        [projected[:, model : 2 * model], projected[:, 2 * model :] + bias_value], axis=1
    ).astype(jnp.bfloat16)

    def item_place(item):
        seq_at = item // pairs
        pair_at = item % pairs
        return (seq_at, seq_at * qlen, seq_at * LEN, pair_at * width)

    def item_segments(seq_at):
        segrow = lax.dynamic_index_in_dim(segment, seq_first + seq_at, 0, keepdims=False)
        return (segrow, segrow)

    def attend_step(item, carried):
        context, logsum = carried
        seq_at, query_row, key_row, start_col = item_place(item)
        query_part = lax.dynamic_slice(queries, (query_row, start_col), (qlen, width))
        key_part = lax.dynamic_slice(keys_values, (key_row, start_col), (LEN, width))
        value_part = lax.dynamic_slice(keys_values, (key_row, model + start_col), (LEN, width))
        seg_query, seg_key = item_segments(seq_at)
        scores = pair_scores(query_part, key_part, seg_query, seg_key)
        peak = jnp.max(scores, axis=2, keepdims=True)
        expo = jnp.exp(scores - peak)
        total = jnp.sum(expo, axis=2, keepdims=True)
        prob = (expo / total).astype(jnp.bfloat16)
        result = jnp.einsum(
            "hqk,khd->qhd",
            prob,
            value_part.reshape(LEN, 2, HEAD_DIM),
            preferred_element_type=jnp.float32,
        )
        context = lax.dynamic_update_slice(
            context, result.reshape(qlen, width).astype(jnp.bfloat16), (query_row, start_col)
        )
        logsum = lax.dynamic_update_slice(
            logsum, (peak + jnp.log(total))[None, :, :, 0], (item, 0, 0)
        )
        return (context, logsum)

    context, logsum = lax.fori_loop(
        0,
        item_count,
        attend_step,
        (jnp.zeros((tok_rows, model), jnp.bfloat16), jnp.zeros((item_count, 2, qlen), jnp.float32)),
    )
    attended = jnp.dot(context, attn_out, preferred_element_type=jnp.float32) + bias_out
    hidden, normed_one, factor_one = norm_rows(
        tokens.astype(jnp.float32) + attended, gain_attn, shift_attn
    )
    hidden_low = hidden.astype(jnp.bfloat16)
    upward = jnp.dot(hidden_low, ffn_up, preferred_element_type=jnp.float32) + bias_up
    active_low = gelu_exact(upward).astype(jnp.bfloat16)
    ffn_result = jnp.dot(active_low, ffn_down, preferred_element_type=jnp.float32) + bias_down
    output, normed_two, factor_two = norm_rows(hidden + ffn_result, gain_ffn, shift_ffn)
    grad_two, grad_gain_ffn, grad_shift_ffn = norm_back(
        cotangent.astype(jnp.float32), normed_two, factor_two, gain_ffn
    )
    grad_bias_down = jnp.sum(grad_two, axis=0)
    grad_two_low = grad_two.astype(jnp.bfloat16)
    grad_down_full = dot_rows(active_low, grad_two_low)
    grad_active = dot_back(grad_two_low, ffn_down)
    grad_upward = jax.vjp(gelu_exact, upward)[1](grad_active)[0]
    grad_bias_up = jnp.sum(grad_upward, axis=0)
    grad_up_low = grad_upward.astype(jnp.bfloat16)
    grad_up_full = dot_rows(hidden_low, grad_up_low)
    grad_hidden = grad_two + dot_back(grad_up_low, ffn_up)
    block_up, block_down = reduce_grads((grad_up_full, grad_down_full))
    grad_one, grad_gain_attn, grad_shift_attn = norm_back(
        grad_hidden, normed_one, factor_one, gain_attn
    )
    grad_bias_out = jnp.sum(grad_one, axis=0)
    grad_one_low = grad_one.astype(jnp.bfloat16)
    grad_out_full = dot_rows(context, grad_one_low)
    grad_context = dot_back(grad_one_low, attn_out).astype(jnp.bfloat16)

    def back_step(item, carried):
        grad_queries, grad_kv = carried
        seq_at, query_row, key_row, start_col = item_place(item)
        query_part = lax.dynamic_slice(queries, (query_row, start_col), (qlen, width))
        key_part = lax.dynamic_slice(keys_values, (key_row, start_col), (LEN, width))
        value_part = lax.dynamic_slice(keys_values, (key_row, model + start_col), (LEN, width))
        grad_part = lax.dynamic_slice(grad_context, (query_row, start_col), (qlen, width))
        seg_query, seg_key = item_segments(seq_at)
        lse_now = lax.dynamic_index_in_dim(logsum, item, 0, keepdims=False)
        scores = pair_scores(query_part, key_part, seg_query, seg_key)
        prob = jnp.exp(scores - lse_now[:, :, None])
        grad_heads = grad_part.reshape(qlen, 2, HEAD_DIM)
        value_heads = value_part.reshape(LEN, 2, HEAD_DIM)
        grad_prob = jnp.einsum(
            "qhd,khd->hqk", grad_heads, value_heads, preferred_element_type=jnp.float32
        )
        grad_value = jnp.einsum(
            "hqk,qhd->khd",
            prob.astype(jnp.bfloat16),
            grad_heads,
            preferred_element_type=jnp.float32,
        )
        inner = jnp.sum(prob * grad_prob, axis=2, keepdims=True)
        grad_raw = (prob * (grad_prob - inner) * HEAD_DIM ** (-0.5)).astype(jnp.bfloat16)
        grad_query = jnp.einsum(
            "hqk,khd->qhd",
            grad_raw,
            key_part.reshape(LEN, 2, HEAD_DIM),
            preferred_element_type=jnp.float32,
        )
        grad_key = jnp.einsum(
            "hqk,qhd->khd",
            grad_raw,
            query_part.reshape(qlen, 2, HEAD_DIM),
            preferred_element_type=jnp.float32,
        )
        grad_queries = lax.dynamic_update_slice(
            grad_queries, grad_query.reshape(qlen, width), (query_row, start_col)
        )
        grad_kv = lax.dynamic_update_slice(
            grad_kv, grad_key.reshape(LEN, width), (key_row, start_col)
        )
        grad_kv = lax.dynamic_update_slice(
            grad_kv, grad_value.reshape(LEN, width), (key_row, model + start_col)
        )
        return (grad_queries, grad_kv)

    grad_queries, grad_kv_whole = lax.fori_loop(
        0,
        item_count,
        back_step,
        (
            jnp.zeros((tok_rows, model), jnp.float32),
            jnp.zeros((keys_values.shape[0], 2 * model), jnp.float32),
        ),
    )
    grad_kv = grad_kv_whole
    grad_bias_query = jnp.sum(grad_queries, axis=0)
    grad_bias_value = jnp.sum(grad_kv[:, model:], axis=0)
    grad_proj_low = jnp.concatenate([grad_queries, grad_kv], axis=1).astype(jnp.bfloat16)
    grad_qkv_full = dot_rows(tokens, grad_proj_low)
    grad_tokens = grad_one + dot_back(grad_proj_low, attn_qkv)
    block_qkv, block_out = reduce_grads((grad_qkv_full, grad_out_full))
    (
        sum_query,
        sum_value,
        sum_out,
        sum_gain_attn,
        sum_shift_attn,
        sum_up,
        sum_down,
        sum_gain_ffn,
        sum_shift_ffn,
    ) = lax.psum(
        (
            grad_bias_query,
            grad_bias_value,
            grad_bias_out,
            grad_gain_attn,
            grad_shift_attn,
            grad_bias_up,
            grad_bias_down,
            grad_gain_ffn,
            grad_shift_ffn,
        ),
        ("row", "col"),
    )
    return (
        output.astype(jnp.bfloat16),
        grad_tokens,
        block_qkv,
        block_out,
        block_up,
        block_down,
        sum_query,
        sum_value,
        sum_out,
        sum_gain_attn,
        sum_shift_attn,
        sum_up,
        sum_down,
        sum_gain_ffn,
        sum_shift_ffn,
    )


def solution(mesh):
    return jax.shard_map(
        per_device,
        mesh=mesh,
        in_specs=(
            P(("row", "col"), None),
            P(),
            P("row", "col"),
            P("row", "col"),
            P("row", "col"),
            P("row", "col"),
            P(),
            P(),
            P(),
            P(),
            P(),
            P(),
            P(),
            P(),
            P(),
            P(("row", "col"), None),
        ),
        out_specs=(
            P(("row", "col"), None),
            P(("row", "col"), None),
            P("row", "col"),
            P("row", "col"),
            P("row", "col"),
            P("row", "col"),
            P(),
            P(),
            P(),
            P(),
            P(),
            P(),
            P(),
            P(),
            P(),
        ),
        check_vma=False,
    )
```

profile of v0, /device:TPU:0, one launch (start us, length us, event | category | flops | bytes accessed | tf_op | source)
XLA Modules:
  0.0 1040.2 jit_solution(14863380718797404151)
XLA Ops:
  7.2 17.5 %all-gather = bf16[4,576,96]{1,2,0:T(8,128)(2,1)S(1)} all-gather(bf16[1,576,96]{1,2,0:T(8,128)(2,1)} %bitcast.129), channel_id=1, replica_groups=mesh['row'=8,'col'=4] {'col'}, dimensions={0}, use_global_device_ids=true | all-gather | bytes 552960 | tf_op jit(solution)/shard_map/all_gather | solution.py:17
  27.1 14.3 %all_gather.26 = bf16[96,768]{0,1:T(8,128)(2,1)S(1)} all-gather(bf16[96,192]{0,1:T(8,128)(2,1)S(1)} %copy.96), channel_id=1, replica_groups=mesh['row'=8,'col'=4] {'col'}, dimensions={1}, use_global_device_ids=true | all-gather | bytes 184320 | tf_op jit(solution)/shard_map/all_gather | solution.py:18
  42.3 18.1 %all_gather.28 = bf16[96,3072]{1,0:T(8,128)(2,1)} all-gather(bf16[96,768]{1,0:T(8,128)(2,1)} %param.24), channel_id=1, replica_groups=mesh['row'=8,'col'=4] {'col'}, dimensions={1}, use_global_device_ids=true | all-gather | bytes 737280 | tf_op jit(solution)/shard_map/all_gather | solution.py:17
  60.5 15.7 %all_gather.30 = bf16[384,768]{0,1:T(8,128)(2,1)} all-gather(bf16[384,192]{0,1:T(8,128)(2,1)S(1)} %copy-done.12), channel_id=1, replica_groups=mesh['row'=8,'col'=4] {'col'}, dimensions={1}, use_global_device_ids=true | all-gather | bytes 737280 | tf_op jit(solution)/shard_map/all_gather | solution.py:18
  80.5 6.5 fusion.93
  95.2 60.3 %while.34 = (s32[]{:T(128)}, bf16[1024,768]{0,1:T(8,128)(2,1)}, f32[6,2,1024]{2,1,0:T(2,128)S(1)}, bf16[1024,1536]{0,1:T(8,128)(2,1)}, s32[]{:T(128)}, /*index=5...) while((s32[]{:T(128)}, bf16[1024,768]{0,1:T(8,128)(2,1)}, ...), condition=%wide.region_3.4_spmd, body=%wide.region_0.3_spmd.sunk | while | flops 563214336 | bytes 32584120 | solution.py:156
  161.1 38.2 %multiply_convert_fusion.1 = (bf16[1024,3072]{1,0:T(8,128)(2,1)}, f32[1024,3072]{1,0:T(8,128)}, f32[1024,3072]{1,0:T(8,128)}) fusion(f32[3072]{0:T(1024)S(1)} %copy-done.23, bf16[768,3072]{1,0:T(8,128)(2,1)} %all-gather.10.cloned.1.call-done, f32[1024,768]{0,1:T(8,128)S(1)} %get-tuple-element.618, f32[768]{0:T(1024)S(1)} %copy-done.26, ...), kind=kOutput, calls=%fused_computation.55 | convolution fusion | flops 5043388416 | bytes 39348224 | tf_op jit(solution)/shard_map/dot_general | solution.py:167
  199.3 9.7 fusion.89
  211.2 19.2 %fusion.90 = (f32[3072]{0:T(1024)}, bf16[1024,3072]{1,0:T(8,128)(2,1)}) fusion(f32[1024,3072]{1,0:T(8,128)} %get-tuple-element.602, bf16[3072,768]{0,1:T(8,128)(2,1)} %all-gather.12.cloned.1.call-done, f32[1024]{0:T(1024)S(1)} %get-tuple-element.625, f32[1024,768]{0,1:T(8,128)S(1)} %get-tuple-element.621, f32[1024]{0:T(1024)S(1)} %broadcast_multiply_fusion.4, ...), kind=kOutput, calls=%fused_computation.132 | convolution fusion | flops 4889244672 | bytes 40938496 | tf_op jit(solution)/shard_map/dot_general | solution.py:52
  230.4 11.6 %multiply_reduce_fusion.1 = (f32[768]{0:T(1024)}, f32[1024]{0:T(1024)S(1)}, f32[1024]{0:T(1024)S(1)}, f32[768]{0:T(1024)}, f32[1024,768]{0,1:T(8,128)S(1)}) fusion(f32[1024,768]{0,1:T(8,128)} %copy-done.3, f32[1024]{0:T(1024)S(1)} %add_rsqrt_fusion.1, f32[1024]{0:T(1024)S(1)} %broadcast_multiply_fusion.5, f32[768]{0:T(1024)S(1)} %copy-done.19, ...), kind=kOutput, calls=%fused_computation.90 | convolution fusion | flops 4845989888 | bytes 22065152 | tf_op jit(solution)/shard_map/dot_general | solution.py:52
  249.3 4.8 convolution_convert_fusion.3
  259.6 356.7 %while.35 = (s32[]{:T(128)}, f32[1024,768]{0,1:T(8,128)}, f32[1024,1536]{0,1:T(8,128)}, bf16[1024,1536]{0,1:T(8,128)(2,1)}, s32[]{:T(128)}, /*index=5*/s32[32,10...) while((s32[]{:T(128)}, f32[1024,768]{0,1:T(8,128)}, ...), condition=%wide.region_14.15_spmd, body=%wide.region_12.14_spmd.sunk | while | flops 1397757952 | bytes 74240520 | solution.py:239
  265.1 5.5 fusion.157
  272.3 4.5 fusion.158
  279.9 15.0 %fusion.160 = f32[2,64,1024]{2,1,0:T(8,128)} fusion(bf16[1024,2,64]{0,2,1:T(8,128)(2,1)S(1)} %bitcast.113, f32[2,1024,1024]{1,2,0:T(8,128)} %fusion.157, f32[2,1024,1024]{1,2,0:T(8,128)} %fusion.158, f32[2,1024]{1,0:T(2,128)S(1)} %dynamic-slice_bitcast_fusion.2, pred[1024,1024]{0,1:T(8,128)(4,1)} %broadcast_compare_fusion.5), kind=kOutput, calls=%fused_computation.23.clone.1 | convolution fusion | flops 291507200 | bytes 18620416 | tf_op jit(solution)/shard_map/while/body/eval_jaxpr/hqk,khd->qhd/dot_general | solution.py:216
  294.9 15.2 %fusion.159 = f32[2,64,1024]{2,1,0:T(8,128)} fusion(bf16[1024,2,64]{0,2,1:T(8,128)(2,1)} %bitcast.115, f32[2,1024,1024]{1,2,0:T(8,128)} %fusion.157, f32[2,1024,1024]{1,2,0:T(8,128)} %fusion.158, f32[2,1024]{1,0:T(2,128)S(1)} %dynamic-slice_bitcast_fusion.2, pred[1024,1024]{0,1:T(8,128)(4,1)} %broadcast_compare_fusion.5), kind=kOutput, calls=%fused_computation.22.clone.1 | convolution fusion | flops 291507200 | bytes 18620416 | tf_op jit(solution)/shard_map/while/body/eval_jaxpr/hqk,qhd->khd/dot_general | solution.py:222
  312.3 6.0 fusion.161
  324.4 5.5 fusion.157
  339.2 15.0 %fusion.160 = f32[2,64,1024]{2,1,0:T(8,128)} fusion(bf16[1024,2,64]{0,2,1:T(8,128)(2,1)S(1)} %bitcast.113, f32[2,1024,1024]{1,2,0:T(8,128)} %fusion.157, f32[2,1024,1024]{1,2,0:T(8,128)} %fusion.158, f32[2,1024]{1,0:T(2,128)S(1)} %dynamic-slice_bitcast_fusion.2, pred[1024,1024]{0,1:T(8,128)(4,1)} %broadcast_compare_fusion.5), kind=kOutput, calls=%fused_computation.23.clone.1 | convolution fusion | flops 291507200 | bytes 18620416 | tf_op jit(solution)/shard_map/while/body/eval_jaxpr/hqk,khd->qhd/dot_general | solution.py:216
  354.2 15.2 %fusion.159 = f32[2,64,1024]{2,1,0:T(8,128)} fusion(bf16[1024,2,64]{0,2,1:T(8,128)(2,1)} %bitcast.115, f32[2,1024,1024]{1,2,0:T(8,128)} %fusion.157, f32[2,1024,1024]{1,2,0:T(8,128)} %fusion.158, f32[2,1024]{1,0:T(2,128)S(1)} %dynamic-slice_bitcast_fusion.2, pred[1024,1024]{0,1:T(8,128)(4,1)} %broadcast_compare_fusion.5), kind=kOutput, calls=%fused_computation.22.clone.1 | convolution fusion | flops 291507200 | bytes 18620416 | tf_op jit(solution)/shard_map/while/body/eval_jaxpr/hqk,qhd->khd/dot_general | solution.py:222
  371.7 6.0 fusion.161
  383.8 5.5 fusion.157
  398.6 15.0 %fusion.160 = f32[2,64,1024]{2,1,0:T(8,128)} fusion(bf16[1024,2,64]{0,2,1:T(8,128)(2,1)S(1)} %bitcast.113, f32[2,1024,1024]{1,2,0:T(8,128)} %fusion.157, f32[2,1024,1024]{1,2,0:T(8,128)} %fusion.158, f32[2,1024]{1,0:T(2,128)S(1)} %dynamic-slice_bitcast_fusion.2, pred[1024,1024]{0,1:T(8,128)(4,1)} %broadcast_compare_fusion.5), kind=kOutput, calls=%fused_computation.23.clone.1 | convolution fusion | flops 291507200 | bytes 18620416 | tf_op jit(solution)/shard_map/while/body/eval_jaxpr/hqk,khd->qhd/dot_general | solution.py:216
  413.6 15.2 %fusion.159 = f32[2,64,1024]{2,1,0:T(8,128)} fusion(bf16[1024,2,64]{0,2,1:T(8,128)(2,1)} %bitcast.115, f32[2,1024,1024]{1,2,0:T(8,128)} %fusion.157, f32[2,1024,1024]{1,2,0:T(8,128)} %fusion.158, f32[2,1024]{1,0:T(2,128)S(1)} %dynamic-slice_bitcast_fusion.2, pred[1024,1024]{0,1:T(8,128)(4,1)} %broadcast_compare_fusion.5), kind=kOutput, calls=%fused_computation.22.clone.1 | convolution fusion | flops 291507200 | bytes 18620416 | tf_op jit(solution)/shard_map/while/body/eval_jaxpr/hqk,qhd->khd/dot_general | solution.py:222
  431.1 6.0 fusion.161
  443.2 5.5 fusion.157
  458.0 15.0 %fusion.160 = f32[2,64,1024]{2,1,0:T(8,128)} fusion(bf16[1024,2,64]{0,2,1:T(8,128)(2,1)S(1)} %bitcast.113, f32[2,1024,1024]{1,2,0:T(8,128)} %fusion.157, f32[2,1024,1024]{1,2,0:T(8,128)} %fusion.158, f32[2,1024]{1,0:T(2,128)S(1)} %dynamic-slice_bitcast_fusion.2, pred[1024,1024]{0,1:T(8,128)(4,1)} %broadcast_compare_fusion.5), kind=kOutput, calls=%fused_computation.23.clone.1 | convolution fusion | flops 291507200 | bytes 18620416 | tf_op jit(solution)/shard_map/while/body/eval_jaxpr/hqk,khd->qhd/dot_general | solution.py:216
  473.0 15.2 %fusion.159 = f32[2,64,1024]{2,1,0:T(8,128)} fusion(bf16[1024,2,64]{0,2,1:T(8,128)(2,1)} %bitcast.115, f32[2,1024,1024]{1,2,0:T(8,128)} %fusion.157, f32[2,1024,1024]{1,2,0:T(8,128)} %fusion.158, f32[2,1024]{1,0:T(2,128)S(1)} %dynamic-slice_bitcast_fusion.2, pred[1024,1024]{0,1:T(8,128)(4,1)} %broadcast_compare_fusion.5), kind=kOutput, calls=%fused_computation.22.clone.1 | convolution fusion | flops 291507200 | bytes 18620416 | tf_op jit(solution)/shard_map/while/body/eval_jaxpr/hqk,qhd->khd/dot_general | solution.py:222
  490.5 6.0 fusion.161
  502.6 5.5 fusion.157
  517.4 15.0 %fusion.160 = f32[2,64,1024]{2,1,0:T(8,128)} fusion(bf16[1024,2,64]{0,2,1:T(8,128)(2,1)S(1)} %bitcast.113, f32[2,1024,1024]{1,2,0:T(8,128)} %fusion.157, f32[2,1024,1024]{1,2,0:T(8,128)} %fusion.158, f32[2,1024]{1,0:T(2,128)S(1)} %dynamic-slice_bitcast_fusion.2, pred[1024,1024]{0,1:T(8,128)(4,1)} %broadcast_compare_fusion.5), kind=kOutput, calls=%fused_computation.23.clone.1 | convolution fusion | flops 291507200 | bytes 18620416 | tf_op jit(solution)/shard_map/while/body/eval_jaxpr/hqk,khd->qhd/dot_general | solution.py:216
  532.4 15.2 %fusion.159 = f32[2,64,1024]{2,1,0:T(8,128)} fusion(bf16[1024,2,64]{0,2,1:T(8,128)(2,1)} %bitcast.115, f32[2,1024,1024]{1,2,0:T(8,128)} %fusion.157, f32[2,1024,1024]{1,2,0:T(8,128)} %fusion.158, f32[2,1024]{1,0:T(2,128)S(1)} %dynamic-slice_bitcast_fusion.2, pred[1024,1024]{0,1:T(8,128)(4,1)} %broadcast_compare_fusion.5), kind=kOutput, calls=%fused_computation.22.clone.1 | convolution fusion | flops 291507200 | bytes 18620416 | tf_op jit(solution)/shard_map/while/body/eval_jaxpr/hqk,qhd->khd/dot_general | solution.py:222
  549.9 6.0 fusion.161
  562.0 5.5 fusion.157
  576.8 15.0 %fusion.160 = f32[2,64,1024]{2,1,0:T(8,128)} fusion(bf16[1024,2,64]{0,2,1:T(8,128)(2,1)S(1)} %bitcast.113, f32[2,1024,1024]{1,2,0:T(8,128)} %fusion.157, f32[2,1024,1024]{1,2,0:T(8,128)} %fusion.158, f32[2,1024]{1,0:T(2,128)S(1)} %dynamic-slice_bitcast_fusion.2, pred[1024,1024]{0,1:T(8,128)(4,1)} %broadcast_compare_fusion.5), kind=kOutput, calls=%fused_computation.23.clone.1 | convolution fusion | flops 291507200 | bytes 18620416 | tf_op jit(solution)/shard_map/while/body/eval_jaxpr/hqk,khd->qhd/dot_general | solution.py:216
  591.7 15.2 %fusion.159 = f32[2,64,1024]{2,1,0:T(8,128)} fusion(bf16[1024,2,64]{0,2,1:T(8,128)(2,1)} %bitcast.115, f32[2,1024,1024]{1,2,0:T(8,128)} %fusion.157, f32[2,1024,1024]{1,2,0:T(8,128)} %fusion.158, f32[2,1024]{1,0:T(2,128)S(1)} %dynamic-slice_bitcast_fusion.2, pred[1024,1024]{0,1:T(8,128)(4,1)} %broadcast_compare_fusion.5), kind=kOutput, calls=%fused_computation.22.clone.1 | convolution fusion | flops 291507200 | bytes 18620416 | tf_op jit(solution)/shard_map/while/body/eval_jaxpr/hqk,qhd->khd/dot_general | solution.py:222
  609.2 6.0 fusion.161
  622.5 6.5 fusion.54
  629.1 9.6 convolution_convert_fusion
  639.4 9.8 convolution_convert_fusion.1
  651.3 46.1 %reduce-scatter.15.cloned.1.call-done = bf16[768,576]{0,1:T(8,128)(2,1)} async-done(((bf16[768,2304]{0,1:T(8,128)(2,1)}), bf16[768,576]{0,1:T(8,128)(2,1)}) %reduce-scatter.15.cloned.1.call-update) | async-done | bytes 884752 | tf_op jit(solution)/shard_map/reduce_scatter | solution.py:28
  699.6 85.5 %reduce-scatter.23.cloned.1.call-done = bf16[3072,192]{0,1:T(8,128)(2,1)} async-done(((bf16[3072,768]{0,1:T(8,128)(2,1)}), bf16[3072,192]{0,1:T(8,128)(2,1)}) %reduce-scatter.23.cloned.1.call-update) | async-done | bytes 1179664 | tf_op jit(solution)/shard_map/reduce_scatter | solution.py:31
  787.7 85.6 %reduce-scatter.19.cloned.1.call-done = bf16[768,768]{1,0:T(8,128)(2,1)} async-done(((bf16[768,3072]{1,0:T(8,128)(2,1)}), bf16[768,768]{1,0:T(8,128)(2,1)}) %reduce-scatter.19.cloned.1.call-update) | async-done | bytes 1179664 | tf_op jit(solution)/shard_map/reduce_scatter | solution.py:28
  873.3 9.8 fusion.69
  895.8 42.1 %all-reduce = (f32[768]{0:T(1024)}, f32[768]{0:T(1024)}, f32[768]{0:T(1024)}, f32[768]{0:T(1024)}, f32[768]{0:T(1024)}, /*index=5*/f32[3072]{0:T(1024)}, f32[768]{0:T(1024)}, f32[768]{0:T(1024)}, f32[768]{0:T(1024)}) all-reduce(f32[768]{0:T(1024)S(1)} %get-tuple-element.615, ...), channel_id=1, replica_groups=mesh['row'=8,'col'=4] {'row','col'}, use_global_device_ids=true, to_apply=%region_24.25 | all-reduce | flops 9216 | bytes 73728 | tf_op jit(solution)/shard_map/psum | solution.py:265
  939.6 10.1 reduce-scatter.25.cloned.1.call-done
  951.6 39.7 %reduce-scatter.29.cloned.1.call-done = bf16[384,192]{1,0:T(8,128)(2,1)} async-done(((bf16[3072,192]{1,0:T(8,128)(2,1)}), bf16[384,192]{1,0:T(8,128)(2,1)}) %reduce-scatter.29.cloned.1.call-update) | async-done | bytes 147472
  993.2 38.0 %reduce-scatter.21.cloned.1.call-done = bf16[96,768]{1,0:T(8,128)(2,1)} async-done(((bf16[768,768]{1,0:T(8,128)(2,1)}), bf16[96,768]{1,0:T(8,128)(2,1)}) %reduce-scatter.21.cloned.1.call-update) | async-done | bytes 147472 | tf_op jit(solution)/shard_map/reduce_scatter | solution.py:36
  (257 shorter events, 230.6 us)
Async XLA Ops:
  7.2 53.3 %copy-start.12 = (bf16[384,192]{0,1:T(8,128)(2,1)S(1)}, bf16[384,192]{0,1:T(8,128)(2,1)}, u32[]{:S(2)}) copy-start(bf16[384,192]{0,1:T(8,128)(2,1)} %param.25) | copy-start | bytes 442372
  7.2 73.3 %all-gather.6.cloned.1.call-start = ((), (), s32[]{:S(2)}) async-start(), calls=%async_computation.8 | async-start | bytes 3981312 | tf_op jit(solution)/shard_map/all_gather | solution.py:21
  24.9 54.0 %copy-start.9 = (bf16[1024,768]{1,0:T(8,128)(2,1)S(1)}, bf16[1024,768]{1,0:T(8,128)(2,1)}, u32[]{:S(2)}) copy-start(bf16[1024,768]{1,0:T(8,128)(2,1)} %param.35) | copy-start | bytes 4718596
  26.2 129.4 %all-gather.8.cloned.1.call-start = ((), (), s32[]{:S(2)}) async-start(), calls=%async_computation.9 | async-start | bytes 1327104 | tf_op jit(solution)/shard_map/all_gather | solution.py:22
  42.2 118.9 %all-gather.10.cloned.1.call-start = ((), (), s32[]{:S(2)}) async-start(), calls=%async_computation.10 | async-start | bytes 5308416 | tf_op jit(solution)/shard_map/all_gather | solution.py:21
  60.4 138.9 %all-gather.12.cloned.1.call-start = ((), (), s32[]{:S(2)}) async-start(), calls=%async_computation.11 | async-start | bytes 5308416 | tf_op jit(solution)/shard_map/all_gather | solution.py:22
  76.2 573.0 %reduce-scatter.17.cloned.1.call-start = ((), (), s32[]{:S(2)}) async-start(), calls=%async_computation.13 | async-start | bytes 1474560 | tf_op jit(solution)/shard_map/reduce_scatter | solution.py:31
  80.5 6.7 copy-start.17
  80.5 6.7 copy-start.18
  95.2 61.6 %copy-start.24 = (f32[768]{0:T(1024)S(1)}, f32[768]{0:T(1024)}, u32[]{:S(2)}) copy-start(f32[768]{0:T(1024)} %param.28) | copy-start | bytes 9220
  155.5 1.2 copy-start.6
  155.5 5.1 copy-start.13
  156.7 4.3 copy-start.19
  156.7 4.3 copy-start.23
  156.7 4.3 copy-start.26
  160.6 38.7 %copy-start.3 = (f32[1024,768]{0,1:T(8,128)}, f32[1024,768]{0,1:T(8,128)S(1)}, u32[]{:S(2)}) copy-start(f32[1024,768]{0,1:T(8,128)S(1)} %get-tuple-element.618) | copy-start | bytes 9437188
  161.0 38.3 %copy-start.25 = (f32[768]{0:T(1024)S(1)}, f32[768]{0:T(1024)}, u32[]{:S(2)}) copy-start(f32[768]{0:T(1024)} %param.32) | copy-start | bytes 9220
  199.3 10.2 copy-start.15
  209.0 1.4 copy-start.2
  230.4 11.6 %copy-start.4 = (f32[1024,768]{0,1:T(8,128)S(1)}, f32[1024,768]{0,1:T(8,128)}, u32[]{:S(2)}) copy-start(f32[1024,768]{0,1:T(8,128)} %copy-done.3) | copy-start | bytes 9437188
  243.7 1.6 copy-start.7
  249.2 448.1 %reduce-scatter.15.cloned.1.call-start = ((), (), s32[]{:S(2)}) async-start(), calls=%async_computation.12 | async-start | bytes 4423680 | tf_op jit(solution)/shard_map/reduce_scatter | solution.py:28
  271.6 0.7 copy-start
  294.9 17.5 %copy-start.1 = (bf16[1024,128]{0,1:T(8,128)(2,1)S(1)}, bf16[1024,128]{0,1:T(8,128)(2,1)}, u32[]{:S(2)}) copy-start(bf16[1024,128]{0,1:T(8,128)(2,1)} %copy.124) | copy-start | bytes 786436 | tf_op jit(solution)/shard_map/while
  330.9 0.7 copy-start
  354.2 17.5 %copy-start.1 = (bf16[1024,128]{0,1:T(8,128)(2,1)S(1)}, bf16[1024,128]{0,1:T(8,128)(2,1)}, u32[]{:S(2)}) copy-start(bf16[1024,128]{0,1:T(8,128)(2,1)} %copy.124) | copy-start | bytes 786436 | tf_op jit(solution)/shard_map/while
  390.3 0.7 copy-start
  413.6 17.5 %copy-start.1 = (bf16[1024,128]{0,1:T(8,128)(2,1)S(1)}, bf16[1024,128]{0,1:T(8,128)(2,1)}, u32[]{:S(2)}) copy-start(bf16[1024,128]{0,1:T(8,128)(2,1)} %copy.124) | copy-start | bytes 786436 | tf_op jit(solution)/shard_map/while
  449.7 0.7 copy-start
  473.0 17.5 %copy-start.1 = (bf16[1024,128]{0,1:T(8,128)(2,1)S(1)}, bf16[1024,128]{0,1:T(8,128)(2,1)}, u32[]{:S(2)}) copy-start(bf16[1024,128]{0,1:T(8,128)(2,1)} %copy.124) | copy-start | bytes 786436 | tf_op jit(solution)/shard_map/while
  509.1 0.7 copy-start
  532.4 17.5 %copy-start.1 = (bf16[1024,128]{0,1:T(8,128)(2,1)S(1)}, bf16[1024,128]{0,1:T(8,128)(2,1)}, u32[]{:S(2)}) copy-start(bf16[1024,128]{0,1:T(8,128)(2,1)} %copy.124) | copy-start | bytes 786436 | tf_op jit(solution)/shard_map/while
  591.7 17.5 %copy-start.1 = (bf16[1024,128]{0,1:T(8,128)(2,1)S(1)}, bf16[1024,128]{0,1:T(8,128)(2,1)}, u32[]{:S(2)}) copy-start(bf16[1024,128]{0,1:T(8,128)(2,1)} %copy.124) | copy-start | bytes 786436 | tf_op jit(solution)/shard_map/while
  616.4 3.7 copy-start.5
  619.8 1.7 copy-start.8
  619.8 2.6 copy-start.10
  620.5 1.5 copy-start.11
  629.0 156.1 %reduce-scatter.23.cloned.1.call-start = ((), (), s32[]{:S(2)}) async-start(), calls=%async_computation.16 | async-start | bytes 5898240 | tf_op jit(solution)/shard_map/reduce_scatter | solution.py:31
  638.7 234.5 %reduce-scatter.19.cloned.1.call-start = ((), (), s32[]{:S(2)}) async-start(), calls=%async_computation.14 | async-start | bytes 5898240 | tf_op jit(solution)/shard_map/reduce_scatter | solution.py:28
  649.2 288.7 %reduce-scatter.27.cloned.1.call-start = ((), (), s32[]{:S(2)}) async-start(), calls=%async_computation.18 | async-start | bytes 442368
  651.2 298.5 %reduce-scatter.25.cloned.1.call-start = ((), (), s32[]{:S(2)}) async-start(), calls=%async_computation.17 | async-start | bytes 1105920
  699.6 291.8 %reduce-scatter.29.cloned.1.call-start = ((), (), s32[]{:S(2)}) async-start(), calls=%async_computation.19 | async-start | bytes 1769472
  787.6 243.5 %reduce-scatter.21.cloned.1.call-start = ((), (), s32[]{:S(2)}) async-start(), calls=%async_computation.15 | async-start | bytes 1327104 | tf_op jit(solution)/shard_map/reduce_scatter | solution.py:36
  883.1 3.8 copy-start.22
  891.1 4.7 copy-start.14
  891.1 4.8 copy-start.16
  891.1 4.8 copy-start.20
  891.1 4.8 copy-start.21
  (2 other events, 1.4 us)
Sparse Core Ops, SparseCore 0:
  26.3 35.5 all-gather.5
  64.4 23.9 all-gather.7
  90.2 38.7 all-gather.9
  130.7 39.6 all-gather.11
  249.4 30.9 reduce-scatter.16
  629.1 68.1 reduce-scatter.14
  699.6 85.4 reduce-scatter.22
  787.4 85.7 reduce-scatter.18
  876.3 34.3 reduce-scatter.26
  913.8 35.9 reduce-scatter.24
  953.0 38.2 reduce-scatter.28
  994.5 36.6 reduce-scatter.20
where the time goes:
time: 1050 us; the launch traced here: 1040 us
  matrix products  439 us (42%)
  waiting for transfers between devices  305 us (29%)
  local copies, waits for them, and re-layouts  128 us (12%)
  blocking collectives  108 us (10%)
  other arithmetic  43.5 us (4%)
  between operations  15.1 us (1%)
    reduce_scatter x2, waiting for transfers between devices, reduce_grads(): lax.psum_scatter(grads[0].astype(jnp.bfloat16), 'col', scatter_dimension=...  132 us
    dot_general x6, matrix products, back_step(): jnp.einsum('hqk,qhd->khd', grad_raw, query_part.reshape(qlen, 2, HEAD_DIM...  91.2 us
    dot_general x6, matrix products, back_step(): jnp.einsum('hqk,khd->qhd', grad_raw, key_part.reshape(LEN, 2, HEAD_DIM),...  89.8 us
    reduce_scatter x2, waiting for transfers between devices, reduce_grads(): lax.psum_scatter(grads[1].astype(jnp.bfloat16), 'col', scatter_dimension=...  85.5 us
    unnamed x15, waiting for transfers between devices  50.1 us
    dot_general x4, matrix products, dot_back(): lax.dot_general(left, right, (((1,), (1,)), ((), ())), preferred_element_...  45.4 us
    psum x1, blocking collectives, per_device(): lax.psum((grad_bias_query, grad_bias_value, grad_bias_out, grad_gain_attn...  42.1 us
    dot_general x12, matrix products, pair_scores(): jnp.einsum('qhd,khd->hqk', query_heads, key_heads, preferred_element_type...  38.5 us
  transfers between devices with their start and end apart: 12, of which 6 were waited for; matrix products, arithmetic and copies ran while one was open for 53% of the time, Pallas kernels for 0%

commit v1 on v0

v1 whole, which is shorter than its diff:
```python
import jax
import jax.numpy as jnp
from jax import lax
from jax.experimental import pallas as pl
from jax.experimental.pallas import tpu as pltpu
from jax.sharding import PartitionSpec as P

HEADS = 12
HEAD_DIM = 64
LEN = 1024


norm_eps = 1e-05
masked_score = -1e30


def gather_block(blocks):
    widened = (
        lax.all_gather(blocks[0], "col", axis=1, tiled=True),
        lax.all_gather(blocks[1], "col", axis=1, tiled=True),
    )
    return (
        lax.all_gather(widened[0], "row", axis=0, tiled=True),
        lax.all_gather(widened[1], "row", axis=0, tiled=True),
    )


def reduce_grads(grads):
    def one(grad):
        narrowed = lax.psum_scatter(
            grad.astype(jnp.bfloat16), "row", scatter_dimension=0, tiled=True
        )
        return lax.psum_scatter(narrowed, "col", scatter_dimension=1, tiled=True).astype(jnp.float32)

    return tuple(one(grad) for grad in grads)


def dot_rows(left, right):
    return lax.dot_general(
        left, right, (((0,), (0,)), ((), ())), preferred_element_type=jnp.float32
    )


def dot_back(left, right):
    return lax.dot_general(
        left, right, (((1,), (1,)), ((), ())), preferred_element_type=jnp.float32
    )


def norm_rows(resid, gain, shift):
    centre = resid - jnp.mean(resid, axis=1, keepdims=True)
    factor = lax.rsqrt(jnp.mean(centre * centre, axis=1, keepdims=True) + norm_eps)
    normed = centre * factor
    return (normed * gain + shift, normed, factor)


def norm_back(grad_result, normed, factor, gain):
    grad_normed = grad_result * gain
    grad_resid = factor * (
        grad_normed
        - jnp.mean(grad_normed, axis=1, keepdims=True)
        - normed * jnp.mean(grad_normed * normed, axis=1, keepdims=True)
    )
    return (grad_resid, jnp.sum(grad_result * normed, axis=0), jnp.sum(grad_result, axis=0))


def gelu_exact(value):
    return jax.nn.gelu(value, approximate=False)


BLOCK = 512


def contract(left, right, left_dim, right_dim):
    return lax.dot_general(
        left, right, (((left_dim,), (right_dim,)), ((), ())), preferred_element_type=jnp.float32
    )


def keep_head(field, head):
    lane = lax.broadcasted_iota(jnp.int32, field.shape, 1)
    keep = (lane < HEAD_DIM) if head == 0 else (lane >= HEAD_DIM)
    return jnp.where(keep, field, jnp.zeros_like(field))


def attend_kernel(q, k, v, seg_row, seg_col, context, logsum, bias):
    bias[...] = jnp.where(seg_col[BLOCK:, :] == seg_row[0:1, BLOCK:], 0.0, masked_score)
    for block in range(2):
        rows = slice(block * BLOCK, (block + 1) * BLOCK)

        def pair_step(pair, _, rows=rows, block=block):
            cols = pl.ds(pl.multiple_of(pair * 128, 128), 128)
            qp, kp, vp = q[rows, cols], k[rows, cols], v[rows, cols]
            total = 0.0
            for head in range(2):
                scores = contract(keep_head(qp, head), kp, 1, 1)
                if block:
                    scores = scores + bias[...]
                peak = jnp.max(scores, axis=1, keepdims=True)
                expo = jnp.exp(scores - peak)
                norm = jnp.sum(expo, axis=1, keepdims=True)
                lse = jnp.broadcast_to(peak + jnp.log(norm), (BLOCK, 128)).T
                logsum[pl.ds(pair * 2 + head, 1), rows] = lse[0:1]
                part = contract(expo.astype(jnp.bfloat16), keep_head(vp, head), 1, 0)
                total = total + part * (1.0 / norm)
            context[rows, cols] = total.astype(jnp.bfloat16)
            return 0

        lax.fori_loop(0, HEADS // 2, pair_step, 0)


def attend_back_kernel(q, k, v, grad, context, logsum, seg_row, seg_col, dq, dk, dv, bias):
    bias[...] = jnp.where(seg_col[BLOCK:, :] == seg_row[0:1, BLOCK:], 0.0, masked_score)
    for block in range(2):
        rows = slice(block * BLOCK, (block + 1) * BLOCK)

        def pair_step(pair, _, rows=rows, block=block):
            cols = pl.ds(pl.multiple_of(pair * 128, 128), 128)
            qp, kp, vp, gp = q[rows, cols], k[rows, cols], v[rows, cols], grad[rows, cols]
            prod = (gp.astype(jnp.float32) * context[rows, cols].astype(jnp.float32)).T
            sum_q = sum_k = sum_v = 0.0
            for head in range(2):
                inner = jnp.sum(prod[head * HEAD_DIM : (head + 1) * HEAD_DIM], axis=0, keepdims=True)
                qh, gh, kh = keep_head(qp, head), keep_head(gp, head), keep_head(kp, head)
                scores = contract(kp, qh, 1, 1)
                if block:
                    scores = scores + bias[...]
                prob = jnp.exp(scores - logsum[pl.ds(pair * 2 + head, 1), rows])
                raw = (prob * (contract(vp, gh, 1, 1) - inner)).astype(jnp.bfloat16)
                sum_v = sum_v + contract(prob.astype(jnp.bfloat16), gh, 1, 0)
                sum_k = sum_k + contract(raw, qh, 1, 0)
                sum_q = sum_q + contract(raw, kh, 0, 0)
            dq[rows, cols] = sum_q * HEAD_DIM ** (-0.5)
            dk[rows, cols] = sum_k
            dv[rows, cols] = sum_v
            return 0

        lax.fori_loop(0, HEADS // 2, pair_step, 0)


VMEM = pl.BlockSpec(memory_space=pltpu.VMEM)


def local_call(kernel, outs, name, *args):
    return pl.pallas_call(
        kernel,
        out_shape=outs,
        in_specs=[VMEM] * len(args),
        out_specs=[VMEM] * len(outs),
        scratch_shapes=[pltpu.VMEM((BLOCK, BLOCK), jnp.float32)],
        compiler_params=pltpu.CompilerParams(vmem_limit_bytes=48 << 20),
        name=name,
    )(*args)


def roll_rows(field, start):
    return lax.dynamic_slice_in_dim(jnp.concatenate([field, field]), start, field.shape[0], 0)


def per_device(
    tokens,
    segment,
    w_qkv,
    w_out,
    w_up,
    w_down,
    bias_query,
    bias_value,
    bias_out,
    gain_attn,
    shift_attn,
    bias_up,
    bias_down,
    gain_ffn,
    shift_ffn,
    cotangent,
):
    model = tokens.shape[1]
    tok_rows = tokens.shape[0]
    device_at = lax.axis_index("row") * lax.axis_size("col") + lax.axis_index("col")
    segrow = lax.dynamic_index_in_dim(segment, device_at * tok_rows // LEN, 0, keepdims=False)
    start = jnp.argmax(segrow[: LEN - BLOCK + 1] == segrow[BLOCK - 1 :]).astype(jnp.int32)
    back = (LEN - start).astype(jnp.int32)
    segrow = roll_rows(segrow, start)
    tokens = roll_rows(tokens, start)
    cotangent = roll_rows(cotangent, start)
    seg_row, seg_col = segrow[None, :], segrow[:, None]
    attn_qkv, attn_out = gather_block((w_qkv, w_out))
    ffn_up, ffn_down = gather_block((w_up, w_down))
    projected = jnp.dot(tokens, attn_qkv, preferred_element_type=jnp.float32)
    queries = (projected[:, :model] + bias_query).astype(jnp.bfloat16) * jnp.bfloat16(HEAD_DIM ** (-0.5))
    keys = projected[:, model : 2 * model].astype(jnp.bfloat16)
    values = (projected[:, 2 * model :] + bias_value).astype(jnp.bfloat16)
    wide = jax.ShapeDtypeStruct((tok_rows, model), jnp.bfloat16)
    context, logsum = local_call(
        attend_kernel,
        [wide, jax.ShapeDtypeStruct((HEADS, tok_rows), jnp.float32)],
        "attend",
        queries, keys, values, seg_row, seg_col,
    )
    attended = jnp.dot(context, attn_out, preferred_element_type=jnp.float32) + bias_out
    hidden, normed_one, factor_one = norm_rows(
        tokens.astype(jnp.float32) + attended, gain_attn, shift_attn
    )
    hidden_low = hidden.astype(jnp.bfloat16)
    upward = jnp.dot(hidden_low, ffn_up, preferred_element_type=jnp.float32) + bias_up
    active_low = gelu_exact(upward).astype(jnp.bfloat16)
    ffn_result = jnp.dot(active_low, ffn_down, preferred_element_type=jnp.float32) + bias_down
    output, normed_two, factor_two = norm_rows(hidden + ffn_result, gain_ffn, shift_ffn)
    grad_two, grad_gain_ffn, grad_shift_ffn = norm_back(
        cotangent.astype(jnp.float32), normed_two, factor_two, gain_ffn
    )
    grad_bias_down = jnp.sum(grad_two, axis=0)
    grad_two_low = grad_two.astype(jnp.bfloat16)
    grad_down_full = dot_rows(active_low, grad_two_low)
    grad_active = dot_back(grad_two_low, ffn_down)
    grad_upward = jax.vjp(gelu_exact, upward)[1](grad_active)[0]
    grad_bias_up = jnp.sum(grad_upward, axis=0)
    grad_up_low = grad_upward.astype(jnp.bfloat16)
    grad_up_full = dot_rows(hidden_low, grad_up_low)
    grad_hidden = grad_two + dot_back(grad_up_low, ffn_up)
    block_up, block_down = reduce_grads((grad_up_full, grad_down_full))
    grad_one, grad_gain_attn, grad_shift_attn = norm_back(
        grad_hidden, normed_one, factor_one, gain_attn
    )
    grad_bias_out = jnp.sum(grad_one, axis=0)
    grad_one_low = grad_one.astype(jnp.bfloat16)
    grad_out_full = dot_rows(context, grad_one_low)
    grad_context = dot_back(grad_one_low, attn_out).astype(jnp.bfloat16)

    full = jax.ShapeDtypeStruct((tok_rows, model), jnp.float32)
    grad_queries, grad_keys, grad_values = local_call(
        attend_back_kernel,
        [full, full, full],
        "attend_back",
        queries, keys, values, grad_context, context, logsum, seg_row, seg_col,
    )
    grad_bias_query = jnp.sum(grad_queries, axis=0)
    grad_bias_value = jnp.sum(grad_values, axis=0)
    grad_proj_low = jnp.concatenate([grad_queries, grad_keys, grad_values], axis=1).astype(jnp.bfloat16)
    grad_qkv_full = dot_rows(tokens, grad_proj_low)
    grad_tokens = grad_one + dot_back(grad_proj_low, attn_qkv)
    block_qkv, block_out = reduce_grads((grad_qkv_full, grad_out_full))
    (
        sum_query,
        sum_value,
        sum_out,
        sum_gain_attn,
        sum_shift_attn,
        sum_up,
        sum_down,
        sum_gain_ffn,
        sum_shift_ffn,
    ) = lax.psum(
        (
            grad_bias_query,
            grad_bias_value,
            grad_bias_out,
            grad_gain_attn,
            grad_shift_attn,
            grad_bias_up,
            grad_bias_down,
            grad_gain_ffn,
            grad_shift_ffn,
        ),
        ("row", "col"),
    )
    return (
        roll_rows(output.astype(jnp.bfloat16), back),
        roll_rows(grad_tokens, back),
        block_qkv,
        block_out,
        block_up,
        block_down,
        sum_query,
        sum_value,
        sum_out,
        sum_gain_attn,
        sum_shift_attn,
        sum_up,
        sum_down,
        sum_gain_ffn,
        sum_shift_ffn,
    )


def solution(mesh):
    return jax.shard_map(
        per_device,
        mesh=mesh,
        in_specs=(
            P(("row", "col"), None),
            P(),
            P("row", "col"),
            P("row", "col"),
            P("row", "col"),
            P("row", "col"),
            P(),
            P(),
            P(),
            P(),
            P(),
            P(),
            P(),
            P(),
            P(),
            P(("row", "col"), None),
        ),
        out_specs=(
            P(("row", "col"), None),
            P(("row", "col"), None),
            P("row", "col"),
            P("row", "col"),
            P("row", "col"),
            P("row", "col"),
            P(),
            P(),
            P(),
            P(),
            P(),
            P(),
            P(),
            P(),
            P(),
        ),
        check_vma=False,
    )
```

time: 1050 us -> 540 us (0.51)
  matrix products: 439 us -> 128 us
  waiting for transfers between devices: 305 us -> 175 us
  local copies, waits for them, and re-layouts: 128 us -> 26.4 us
  Pallas kernels: 0 us -> 45.5 us
  other arithmetic: 43.5 us -> 30.9 us
    dot_general x42 -> x0, matrix products: 306 us -> none  [the longest x6 91.2 us: back_step(): jnp.einsum('hqk,qhd->khd', grad_raw, query_part.reshape(qlen, 2, HEAD_DIM...]
    reduce_scatter x5, waiting for transfers between devices: 255 us -> 152 us  [the longest x4 131 us: one(): lax.psum_scatter(grad.astype(jnp.bfloat16), 'row', scatter_dimension=0, t...]
    dynamic_slice x42 -> x1, local copies, waits for them, and re-layouts: 52.9 us -> 0.77 us  [per_device(): lax.dynamic_index_in_dim(segment, device_at * tok_rows // LEN, 0, keepdim...]
    pallas_call x0 -> x2, Pallas kernels: none -> 45.5 us  [local_call(): pl.pallas_call(kernel, out_shape=outs, in_specs=[VMEM] * len(args), out_s...]
    unnamed x15, waiting for transfers between devices: 50.1 us -> 9.06 us
    dynamic_update_slice x18 -> x0, local copies, waits for them, and re-layouts: 23.2 us -> none  [the longest x6 13.8 us: back_step(): lax.dynamic_update_slice(grad_kv, grad_key.reshape(LEN, width), (key_row,...]
    eq x12 -> x1, other arithmetic: 13.6 us -> 0.89 us  [per_device(): segrow[:LEN - BLOCK + 1] == segrow[BLOCK - 1:]]
    unnamed x66 -> x79, local copies, waits for them, and re-layouts: 30.7 us -> 24.3 us
  transfers between devices with their start and end apart: 12 -> 12, of which waited for: 6 -> 7; matrix products, arithmetic and copies ran while one was open for 53% -> 23% of each run, Pallas kernels for 0% -> 9%
where the time goes in v1:
time: 540 us; the launch traced here: 531 us
  waiting for transfers between devices  175 us (32%)
  matrix products  128 us (24%)
  blocking collectives  106 us (20%)
  Pallas kernels  45.5 us (8%)
  other arithmetic  30.9 us (6%)
  local copies, waits for them, and re-layouts  26.4 us (5%)
  between operations  18.4 us (3%)
    reduce_scatter x4, waiting for transfers between devices, one(): lax.psum_scatter(grad.astype(jnp.bfloat16), 'row', scatter_dimension=0, t...  131 us
    pallas_call x2, Pallas kernels, local_call(): pl.pallas_call(kernel, out_shape=outs, in_specs=[VMEM] * len(args), out_s...  45.5 us
    dot_general x4, matrix products, dot_back(): lax.dot_general(left, right, (((1,), (1,)), ((), ())), preferred_element_...  41.4 us
    psum x1, blocking collectives, per_device(): lax.psum((grad_bias_query, grad_bias_value, grad_bias_out, grad_gain_attn...  41.1 us
    dot_general x1, matrix products, per_device(): jnp.dot(hidden_low, ffn_up, preferred_element_type=jnp.float32) + bias_up  38.4 us
    all_gather x2, blocking collectives, gather_block(): lax.all_gather(blocks[0], 'col', axis=1, tiled=True)  35 us
    all_gather x2, blocking collectives, gather_block(): lax.all_gather(blocks[1], 'col', axis=1, tiled=True)  30.2 us
    dot_general x4, matrix products, dot_rows(): lax.dot_general(left, right, (((0,), (0,)), ((), ())), preferred_element_...  28.2 us
  transfers between devices with their start and end apart: 12, of which 7 were waited for; matrix products, arithmetic and copies ran while one was open for 23% of the time, Pallas kernels for 9%

profile of v1, /device:TPU:0, one launch (start us, length us, event | category | flops | bytes accessed | tf_op | source)
XLA Modules:
  0.0 531.0 jit_solution(14469853020286659991)
XLA Ops:
  7.2 17.5 %all-gather = bf16[4,576,96]{1,2,0:T(8,128)(2,1)S(1)} all-gather(bf16[1,576,96]{1,2,0:T(8,128)(2,1)} %bitcast.40), channel_id=1, replica_groups=mesh['row'=8,'col'=4] {'col'}, dimensions={0}, use_global_device_ids=true | all-gather | bytes 552960 | tf_op jit(solution)/shard_map/all_gather | solution.py:19
  25.0 1.2 reshape.83
  27.1 14.2 %all_gather.26 = bf16[96,768]{0,1:T(8,128)(2,1)S(1)} all-gather(bf16[96,192]{0,1:T(8,128)(2,1)S(1)} %copy.43), channel_id=1, replica_groups=mesh['row'=8,'col'=4] {'col'}, dimensions={1}, use_global_device_ids=true | all-gather | bytes 184320 | tf_op jit(solution)/shard_map/all_gather | solution.py:20
  42.2 17.5 %all_gather.28 = bf16[96,3072]{1,0:T(8,128)(2,1)} all-gather(bf16[96,768]{1,0:T(8,128)(2,1)S(1)} %copy-done.24), channel_id=1, replica_groups=mesh['row'=8,'col'=4] {'col'}, dimensions={1}, use_global_device_ids=true | all-gather | bytes 737280 | tf_op jit(solution)/shard_map/all_gather | solution.py:19
  59.7 16.0 %all_gather.30 = bf16[384,768]{0,1:T(8,128)(2,1)} all-gather(bf16[384,192]{0,1:T(8,128)(2,1)S(1)} %copy-done.25), channel_id=1, replica_groups=mesh['row'=8,'col'=4] {'col'}, dimensions={1}, use_global_device_ids=true | all-gather | bytes 737280 | tf_op jit(solution)/shard_map/all_gather | solution.py:20
  80.5 3.2 fusion.27
  83.7 6.4 %fusion.50 = f32[1024,2304]{1,0:T(8,128)S(1)} fusion(bf16[1024,768]{1,0:T(8,128)(2,1)S(1)} %fusion.27, bf16[768,2304]{1,0:T(8,128)(2,1)} %all-gather.6.cloned.1.call-done), kind=kOutput, calls=%fused_computation.99 | convolution fusion | flops 3623878656 | bytes 14548992 | tf_op jit(solution)/shard_map/dot_general | solution.py:190
  90.2 1.4 fusion.14.v
  92.0 18.1 %attend.1 = (bf16[1024,768]{1,0:T(8,128)(2,1)S(1)}, f32[12,1024]{1,0:T(8,128)S(1)}) custom-call(bf16[1024,768]{1,0:T(8,128)(2,1)S(1)} %get-tuple-element.112.q, bf16[1024,768]{1,0:T(8,128)(2,1)S(1)} %get-tuple-element.111.k, bf16[1024,768]{1,0:T(8,128)(2,1)} %fusion.14.v, s32[1,1024]{1,0:T(1,128)S(1)} %bitcast.32, s32[1024,1]{1,0:T(8,128)S(1)} %copy.42.seg_col), custom_call_target="tpu_custom_call" | custom-call | tf_op jit(solution)/shard_map/attend/pallas_call | solution.py:145
  110.1 1.2 copy-done
  111.2 1.2 copy-done.2
  112.4 3.9 fusion.47
  116.4 1.6 copy-done.10
  118.5 10.5 %all-gather.10.cloned.1.call-done = bf16[768,3072]{1,0:T(8,128)(2,1)} async-done(((bf16[96,3072]{1,0:T(8,128)(2,1)}), bf16[768,3072]{1,0:T(8,128)(2,1)}) %all-gather.10.cloned.1.call-update) | async-done | bytes 4718608 | tf_op jit(solution)/shard_map/all_gather | solution.py:23
  129.0 38.4 %multiply_convert_fusion = (bf16[1024,3072]{1,0:T(8,128)(2,1)}, f32[1024,3072]{1,0:T(8,128)}, f32[1024,3072]{1,0:T(8,128)}) fusion(f32[3072]{0:T(1024)S(1)} %copy-done.31, bf16[768,3072]{1,0:T(8,128)(2,1)} %all-gather.10.cloned.1.call-done, f32[1024,768]{1,0:T(8,128)} %copy-done.10, f32[768]{0:T(1024)S(1)} %copy-done.34, f32[768]{0:T(1024)S(1)} %copy-done.29, ...), kind=kOutput, calls=%fused_computation.3 | convolution fusion | flops 5043388416 | bytes 39348224 | tf_op jit(solution)/shard_map/dot_general | solution.py:206
  167.4 3.0 all-gather.12.cloned.1.call-done
  170.4 9.4 %fusion.48 = (f32[1024]{0:T(1024)S(1)}, f32[1024,768]{1,0:T(8,128)S(1)}) fusion(f32[768]{0:T(1024)S(1)} %copy-done.33, bf16[1024,3072]{1,0:T(8,128)(2,1)} %get-tuple-element.109, bf16[3072,768]{0,1:T(8,128)(2,1)} %all-gather.12.cloned.1.call-done, f32[768]{0:T(1024)S(1)} %copy-done.34, f32[768]{0:T(1024)S(1)} %copy-done.29, f32[1024]{0:T(1024)S(1)} %add_rsqrt_fusion.1, ...), kind=kOutput, calls=%fused_computation.97 | convolution fusion | flops 4837342208 | bytes 17323008 | tf_op jit(solution)/shard_map/dot_general | solution.py:208
  181.3 3.2 fusion.12
  184.5 2.9 fusion.39
  187.4 18.7 %fusion.49 = (f32[3072]{0:T(1024)S(1)}, bf16[1024,3072]{1,0:T(8,128)(2,1)}) fusion(f32[1024,3072]{1,0:T(8,128)} %get-tuple-element.110, bf16[3072,768]{0,1:T(8,128)(2,1)} %all-gather.12.cloned.1.call-done, f32[1024,768]{1,0:T(8,128)} %get-tuple-element.105, f32[1024,3072]{1,0:T(8,128)} %get-tuple-element.120, f32[3072]{0:T(1024)S(1)} %copy-done.31), kind=kOutput, calls=%fused_computation.98 | convolution fusion | flops 4882953216 | bytes 39346176 | tf_op jit(solution)/shard_map/dot_general | solution.py:45
  206.1 10.1 %multiply_reduce_fusion = (f32[768]{0:T(1024)S(1)}, f32[1024]{0:T(1024)S(1)}, f32[1024]{0:T(1024)S(1)}, f32[768]{0:T(1024)S(1)}, f32[1024,768]{1,0:T(8,128)S(1)}) fusion(f32[1024,768]{1,0:T(8,128)S(1)} %copy-done.11, f32[1024]{0:T(1024)S(1)} %add_rsqrt_fusion.1, f32[1024]{0:T(1024)S(1)} %broadcast_multiply_fusion.5, f32[768]{0:T(1024)S(1)} %copy-done.29, ...), kind=kOutput, calls=%fused_computation.45 | convolution fusion | flops 4839698432 | bytes 20472832 | tf_op jit(solution)/shard_map/dot_general | solution.py:45
  216.2 1.1 fusion.41
  217.4 1.7 copy-done.15
  219.1 2.5 convolution_convert_fusion.4
  221.9 4.9 convolution_convert_fusion.3.grad
  226.9 27.5 %attend_back.1 = (f32[1024,768]{1,0:T(8,128)}, f32[1024,768]{1,0:T(8,128)}, f32[1024,768]{1,0:T(8,128)}) custom-call(bf16[1024,768]{1,0:T(8,128)(2,1)S(1)} %copy-done.3, bf16[1024,768]{1,0:T(8,128)(2,1)S(1)} %copy-done.1, bf16[1024,768]{1,0:T(8,128)(2,1)S(1)} %copy-done.4, bf16[1024,768]{1,0:T(8,128)(2,1)} %convolution_convert_fusion.3.grad, ...), custom_call_target="tpu_custom_call" | custom-call | tf_op jit(solution)/shard_map/attend_back/pallas_call | solution.py:145
  254.4 2.2 convert.14
  257.2 3.8 fusion.45
  261.1 1.1 copy-done.22
  262.7 6.0 %convolution_convert_fusion.2 = bf16[768,2304]{1,0:T(8,128)(2,1)} fusion(bf16[1024,768]{1,0:T(8,128)(2,1)S(1)} %copy-done.21, bf16[1024,768]{1,0:T(8,128)(2,1)S(1)} %get-tuple-element.115, bf16[1024,768]{1,0:T(8,128)(2,1)S(1)} %convert.14, bf16[1024,768]{1,0:T(8,128)(2,1)S(1)} %get-tuple-element.126), kind=kOutput, calls=%fused_computation.21 | convolution fusion | flops 3639803904 | bytes 9830400 | tf_op jit(solution)/shard_map/dot_general | solution.py:39
  268.8 1.8 copy-done.14
  270.6 9.8 %convolution_convert_fusion = bf16[3072,768]{1,0:T(8,128)(2,1)} fusion(bf16[1024,3072]{1,0:T(8,128)(2,1)} %get-tuple-element.109, f32[1024,768]{1,0:T(8,128)S(1)} %copy-done.14), kind=kOutput, calls=%fused_computation.19 | convolution fusion | flops 4834983936 | bytes 14155776 | tf_op jit(solution)/shard_map/dot_general | solution.py:39
  280.7 1.8 copy-done.12
  282.4 9.9 %convolution_convert_fusion.1 = bf16[768,3072]{1,0:T(8,128)(2,1)} fusion(bf16[1024,3072]{1,0:T(8,128)(2,1)} %get-tuple-element.125, f32[1024,768]{1,0:T(8,128)S(1)} %copy-done.12, f32[768]{0:T(1024)S(1)} %copy-done.34, f32[768]{0:T(1024)S(1)} %copy-done.29, f32[1024]{0:T(1024)S(1)} %add_rsqrt_fusion.1, f32[1024]{0:T(1024)S(1)} %broadcast_multiply_fusion.5), kind=kOutput, calls=%fused_computation.20 | convolution fusion | flops 4838129664 | bytes 14170112 | tf_op jit(solution)/shard_map/dot_general | solution.py:39
  292.4 1.8 copy.49
  294.3 22.5 %reduce-scatter.15.cloned.1.call-done = bf16[96,2304]{1,0:T(8,128)(2,1)} async-done(((bf16[768,2304]{1,0:T(8,128)(2,1)}), bf16[96,2304]{1,0:T(8,128)(2,1)}) %reduce-scatter.15.cloned.1.call-update) | async-done | bytes 442384 | tf_op jit(solution)/shard_map/reduce_scatter | solution.py:30
  316.8 2.1 copy.47
  319.0 55.1 %reduce-scatter.23.cloned.1.call-done = bf16[384,768]{1,0:T(8,128)(2,1)} async-done(((bf16[3072,768]{1,0:T(8,128)(2,1)}), bf16[384,768]{1,0:T(8,128)(2,1)}) %reduce-scatter.23.cloned.1.call-update) | async-done | bytes 589840 | tf_op jit(solution)/shard_map/reduce_scatter | solution.py:30
  374.1 2.1 copy.51
  377.6 53.8 %reduce-scatter.19.cloned.1.call-done = bf16[96,3072]{1,0:T(8,128)(2,1)} async-done(((bf16[768,3072]{1,0:T(8,128)(2,1)}), bf16[96,3072]{1,0:T(8,128)(2,1)}) %reduce-scatter.19.cloned.1.call-update) | async-done | bytes 589840 | tf_op jit(solution)/shard_map/reduce_scatter | solution.py:30
  431.4 3.8 fusion.26
  435.1 41.1 %all-reduce = (f32[768]{0:T(1024)}, f32[768]{0:T(1024)}, f32[768]{0:T(1024)}, f32[768]{0:T(1024)}, f32[768]{0:T(1024)}, /*index=5*/f32[3072]{0:T(1024)}, f32[768]{0:T(1024)}, f32[768]{0:T(1024)}, f32[768]{0:T(1024)}) all-reduce(f32[768]{0:T(1024)S(1)} %get-tuple-element.127, ...), channel_id=1, replica_groups=mesh['row'=8,'col'=4] {'row','col'}, use_global_device_ids=true, to_apply=%region_18.19 | all-reduce | flops 9216 | bytes 73728 | tf_op jit(solution)/shard_map/psum | solution.py:254
  476.3 7.7 %fusion.21 = f32[1024,768]{1,0:T(8,128)S(1)} fusion(f32[1024,768]{1,0:T(8,128)} %copy-done.15, bf16[768,2304]{1,0:T(8,128)(2,1)} %all-gather.6.cloned.1.call-done, bf16[1024,768]{1,0:T(8,128)(2,1)} %copy-done.22, bf16[1024,768]{1,0:T(8,128)(2,1)S(1)} %copy-done.19, bf16[1024,768]{1,0:T(8,128)(2,1)} %copy-done.23), kind=kOutput, calls=%fused_computation.62 | convolution fusion | flops 3638820864 | bytes 14548992 | tf_op jit(solution)/shard_map/dot_general | solution.py:45
  484.0 3.2 fusion.13
  488.7 1.0 copy.48
  490.5 8.9 %reduce-scatter.29.cloned.1.call-done = bf16[192,384]{1,0:T(8,128)(2,1)} async-done(((bf16[768,384]{1,0:T(8,128)(2,1)}), bf16[192,384]{1,0:T(8,128)(2,1)}) %reduce-scatter.29.cloned.1.call-update) | async-done | bytes 147472
  501.2 20.9 %reduce-scatter.21.cloned.1.call-done = bf16[96,768]{1,0:T(8,128)(2,1)} async-done(((bf16[96,3072]{1,0:T(8,128)(2,1)}), bf16[96,768]{1,0:T(8,128)(2,1)}) %reduce-scatter.21.cloned.1.call-update) | async-done | bytes 147472 | tf_op jit(solution)/shard_map/reduce_scatter | solution.py:33
  522.1 1.6 convert_element_type.75
  (116 shorter events, 13.5 us)
Async XLA Ops:
  7.2 35.0 %copy-start.24 = (bf16[96,768]{1,0:T(8,128)(2,1)S(1)}, bf16[96,768]{1,0:T(8,128)(2,1)}, u32[]{:S(2)}) copy-start(bf16[96,768]{1,0:T(8,128)(2,1)} %param.20) | copy-start | bytes 442372
  7.2 52.5 %copy-start.25 = (bf16[384,192]{0,1:T(8,128)(2,1)S(1)}, bf16[384,192]{0,1:T(8,128)(2,1)}, u32[]{:S(2)}) copy-start(bf16[384,192]{0,1:T(8,128)(2,1)} %param.21) | copy-start | bytes 442372
  7.2 76.5 %all-gather.6.cloned.1.call-start = ((), (), s32[]{:S(2)}) async-start(), calls=%async_computation.8 | async-start | bytes 3981312 | tf_op jit(solution)/shard_map/all_gather | solution.py:23
  26.2 86.2 %all-gather.8.cloned.1.call-start = ((), (), s32[]{:S(2)}) async-start(), calls=%async_computation.9 | async-start | bytes 1327104 | tf_op jit(solution)/shard_map/all_gather | solution.py:24
  42.1 86.9 %all-gather.10.cloned.1.call-start = ((), (), s32[]{:S(2)}) async-start(), calls=%async_computation.10 | async-start | bytes 5308416 | tf_op jit(solution)/shard_map/all_gather | solution.py:23
  59.7 110.7 %all-gather.12.cloned.1.call-start = ((), (), s32[]{:S(2)}) async-start(), calls=%async_computation.11 | async-start | bytes 5308416 | tf_op jit(solution)/shard_map/all_gather | solution.py:24
  75.8 216.6 %reduce-scatter.17.cloned.1.call-start = ((), (), s32[]{:S(2)}) async-start(), calls=%async_computation.13 | async-start | bytes 1327104 | tf_op jit(solution)/shard_map/reduce_scatter | solution.py:30
  80.2 11.8 %copy-start.8 = (s32[1024]{0:T(1024)}, s32[1024]{0:T(1024)S(1)}, u32[]{:S(2)}) copy-start(s32[1024]{0:T(1024)S(1)} %fusion.33) | copy-start | bytes 12292
  80.4 11.5 %copy-start.5 = (s32[1024,1]{1,0:T(8,128)}, s32[1024,1]{1,0:T(8,128)S(1)}, u32[]{:S(2)}) copy-start(s32[1024,1]{1,0:T(8,128)S(1)} %copy.42.seg_col) | copy-start | bytes 12292
  83.7 6.5 %copy-start.20 = (bf16[1024,768]{1,0:T(8,128)(2,1)}, bf16[1024,768]{1,0:T(8,128)(2,1)S(1)}, u32[]{:S(2)}) copy-start(bf16[1024,768]{1,0:T(8,128)(2,1)S(1)} %fusion.27) | copy-start | bytes 4718596
  83.7 6.5 %copy-start.30 = (f32[768]{0:T(1024)S(1)}, f32[768]{0:T(1024)}, u32[]{:S(2)}) copy-start(f32[768]{0:T(1024)} %param.23) | copy-start | bytes 9220
  90.2 1.4 copy-start.27
  92.0 20.4 %copy-start.32 = (f32[768]{0:T(1024)S(1)}, f32[768]{0:T(1024)}, u32[]{:S(2)}) copy-start(f32[768]{0:T(1024)} %param.24) | copy-start | bytes 9220
  110.1 1.2 copy-start
  111.2 1.2 copy-start.2
  112.4 105.0 %copy-start.7 = (bf16[1024,768]{1,0:T(8,128)(2,1)}, bf16[1024,768]{1,0:T(8,128)(2,1)S(1)}, u32[]{:S(2)}) copy-start(bf16[1024,768]{1,0:T(8,128)(2,1)S(1)} %get-tuple-element.22.context) | copy-start | bytes 4718596
  116.3 1.7 copy-start.10
  116.3 12.7 %copy-start.29 = (f32[768]{0:T(1024)S(1)}, f32[768]{0:T(1024)}, u32[]{:S(2)}) copy-start(f32[768]{0:T(1024)} %param.25) | copy-start | bytes 9220
  116.3 12.7 %copy-start.31 = (f32[3072]{0:T(1024)S(1)}, f32[3072]{0:T(1024)}, u32[]{:S(2)}) copy-start(f32[3072]{0:T(1024)} %param.27) | copy-start | bytes 36868
  116.3 12.7 %copy-start.34 = (f32[768]{0:T(1024)S(1)}, f32[768]{0:T(1024)}, u32[]{:S(2)}) copy-start(f32[768]{0:T(1024)} %param.26) | copy-start | bytes 9220
  118.5 51.9 %copy-start.33 = (f32[768]{0:T(1024)S(1)}, f32[768]{0:T(1024)}, u32[]{:S(2)}) copy-start(f32[768]{0:T(1024)} %param.28) | copy-start | bytes 9220
  179.8 1.4 copy-start.17
  179.8 1.4 copy-start.26
  181.2 3.2 copy-start.28
  187.4 18.7 %copy-start.11 = (f32[1024,768]{1,0:T(8,128)S(1)}, f32[1024,768]{1,0:T(8,128)}, u32[]{:S(2)}) copy-start(f32[1024,768]{1,0:T(8,128)} %copy-done.10) | copy-start | bytes 9437188
  217.4 1.7 copy-start.15
  221.6 5.3 copy-start.1
  221.6 5.3 copy-start.3
  221.6 5.3 copy-start.9
  221.6 95.2 %reduce-scatter.15.cloned.1.call-start = ((), (), s32[]{:S(2)}) async-start(), calls=%async_computation.12 | async-start | bytes 3981312 | tf_op jit(solution)/shard_map/reduce_scatter | solution.py:30
  221.9 5.0 copy-start.4
  221.9 5.0 copy-start.6
  254.4 2.8 copy-start.16
  256.6 4.5 copy-start.18
  257.2 5.5 %copy-start.21 = (bf16[1024,768]{1,0:T(8,128)(2,1)S(1)}, bf16[1024,768]{1,0:T(8,128)(2,1)}, u32[]{:S(2)}) copy-start(bf16[1024,768]{1,0:T(8,128)(2,1)} %copy-done.20) | copy-start | bytes 4718596
  261.0 1.1 copy-start.22
  261.0 1.6 copy-start.23
  268.7 1.9 copy-start.14
  268.7 105.4 %reduce-scatter.23.cloned.1.call-start = ((), (), s32[]{:S(2)}) async-start(), calls=%async_computation.16 | async-start | bytes 5308416 | tf_op jit(solution)/shard_map/reduce_scatter | solution.py:30
  280.4 2.1 copy-start.12
  280.4 150.9 %reduce-scatter.19.cloned.1.call-start = ((), (), s32[]{:S(2)}) async-start(), calls=%async_computation.14 | async-start | bytes 5308416 | tf_op jit(solution)/shard_map/reduce_scatter | solution.py:30
  292.3 139.0 %copy-start.13 = (bf16[1024,768]{1,0:T(8,128)(2,1)S(1)}, bf16[1024,768]{1,0:T(8,128)(2,1)}, u32[]{:S(2)}) copy-start(bf16[1024,768]{1,0:T(8,128)(2,1)} %get-tuple-element.113) | copy-start | bytes 4718596
  292.3 194.8 %reduce-scatter.27.cloned.1.call-start = ((), (), s32[]{:S(2)}) async-start(), calls=%async_computation.18 | async-start | bytes 245760
  294.3 194.4 %reduce-scatter.25.cloned.1.call-start = ((), (), s32[]{:S(2)}) async-start(), calls=%async_computation.17 | async-start | bytes 737280
  318.9 157.4 %copy-start.19 = (bf16[1024,768]{1,0:T(8,128)(2,1)S(1)}, bf16[1024,768]{1,0:T(8,128)(2,1)}, u32[]{:S(2)}) copy-start(bf16[1024,768]{1,0:T(8,128)(2,1)} %copy-done.18) | copy-start | bytes 4718596
  318.9 180.4 %reduce-scatter.29.cloned.1.call-start = ((), (), s32[]{:S(2)}) async-start(), calls=%async_computation.19 | async-start | bytes 737280
  376.2 145.8 %reduce-scatter.21.cloned.1.call-start = ((), (), s32[]{:S(2)}) async-start(), calls=%async_computation.15 | async-start | bytes 737280 | tf_op jit(solution)/shard_map/reduce_scatter | solution.py:33
Sparse Core Ops, SparseCore 0:
  26.3 35.5 all-gather.5
  64.4 23.9 all-gather.7
  90.2 38.7 all-gather.9
  130.7 39.6 all-gather.11
  221.7 36.7 reduce-scatter.16
  268.8 47.9 reduce-scatter.14
  320.3 53.7 reduce-scatter.22
  377.5 53.7 reduce-scatter.18
  434.2 19.5 reduce-scatter.26
  455.9 20.3 reduce-scatter.24
  478.6 20.6 reduce-scatter.28
  501.5 20.5 reduce-scatter.20

commit v2 on v1

--- a/solution.py
+++ b/solution.py
@@ -1,3 +1,5 @@
+import functools
+
 import jax
 import jax.numpy as jnp
 from jax import lax
@@ -14,17 +16,6 @@
 masked_score = -1e30
 
 
-def gather_block(blocks):
-    widened = (
-        lax.all_gather(blocks[0], "col", axis=1, tiled=True),
-        lax.all_gather(blocks[1], "col", axis=1, tiled=True),
-    )
-    return (
-        lax.all_gather(widened[0], "row", axis=0, tiled=True),
-        lax.all_gather(widened[1], "row", axis=0, tiled=True),
-    )
-
-
 def reduce_grads(grads):
     def one(grad):
         narrowed = lax.psum_scatter(
@@ -47,13 +38,6 @@
     )
 
 
-def norm_rows(resid, gain, shift):
-    centre = resid - jnp.mean(resid, axis=1, keepdims=True)
-    factor = lax.rsqrt(jnp.mean(centre * centre, axis=1, keepdims=True) + norm_eps)
-    normed = centre * factor
-    return (normed * gain + shift, normed, factor)
-
-
 def norm_back(grad_result, normed, factor, gain):
     grad_normed = grad_result * gain
     grad_resid = factor * (
@@ -64,10 +48,6 @@
     return (grad_resid, jnp.sum(grad_result * normed, axis=0), jnp.sum(grad_result, axis=0))
 
 
-def gelu_exact(value):
-    return jax.nn.gelu(value, approximate=False)
-
-
 BLOCK = 512
 
 
@@ -83,30 +63,431 @@
     return jnp.where(keep, field, jnp.zeros_like(field))
 
 
-def attend_kernel(q, k, v, seg_row, seg_col, context, logsum, bias):
-    bias[...] = jnp.where(seg_col[BLOCK:, :] == seg_row[0:1, BLOCK:], 0.0, masked_score)
-    for block in range(2):
-        rows = slice(block * BLOCK, (block + 1) * BLOCK)
-
-        def pair_step(pair, _, rows=rows, block=block):
-            cols = pl.ds(pl.multiple_of(pair * 128, 128), 128)
-            qp, kp, vp = q[rows, cols], k[rows, cols], v[rows, cols]
-            total = 0.0
-            for head in range(2):
-                scores = contract(keep_head(qp, head), kp, 1, 1)
-                if block:
-                    scores = scores + bias[...]
-                peak = jnp.max(scores, axis=1, keepdims=True)
-                expo = jnp.exp(scores - peak)
-                norm = jnp.sum(expo, axis=1, keepdims=True)
-                lse = jnp.broadcast_to(peak + jnp.log(norm), (BLOCK, 128)).T
-                logsum[pl.ds(pair * 2 + head, 1), rows] = lse[0:1]
-                part = contract(expo.astype(jnp.bfloat16), keep_head(vp, head), 1, 0)
-                total = total + part * (1.0 / norm)
-            context[rows, cols] = total.astype(jnp.bfloat16)
+MESH = pl.DeviceIdType.MESH
+ANY = pl.BlockSpec(memory_space=pl.ANY)
+CHUNK = 256
+
+
+class Place:
+    def __init__(self, chips, depth):
+        self.chips, self.depth, self.hops = chips, depth, chips // 2
+        self.row, self.z = lax.axis_index("row"), lax.axis_index("col")
+        self.chip, self.core = self.row // 2, self.row % 2
+        across = self.chip % 2
+        self.pos = self.chip // 2 + across * (chips - 1 - 2 * (self.chip // 2))
+
+    def chip_at(self, pos):
+        pos = (pos + self.chips) % self.chips
+        far = pos // (self.chips // 2)
+        return 2 * (pos + far * (self.chips - 1 - 2 * pos)) + far
+
+    def right(self):
+        return (2 * self.chip_at(self.pos + 1) + self.core, self.z)
+
+    def left(self):
+        return (2 * self.chip_at(self.pos - 1) + self.core, self.z)
+
+    def mate(self):
+        return (self.row + 1 - 2 * self.core, self.z)
+
+    def up(self):
+        return (self.row, self.z + 1)
+
+    def down(self):
+        return (self.row, self.z - 1)
+
+    def meet(self):
+        barrier = pltpu.get_barrier_semaphore()
+        for device in (self.right(), self.left(), self.mate()):
+            pl.semaphore_signal(barrier, inc=1, device_id=device, device_id_type=MESH)
+
+        @pl.when(self.z < self.depth - 1)
+        def _():
+            pl.semaphore_signal(barrier, inc=1, device_id=self.up(), device_id_type=MESH)
+
+        @pl.when(self.z > 0)
+        def _():
+            pl.semaphore_signal(barrier, inc=1, device_id=self.down(), device_id_type=MESH)
+
+        ends = jnp.where(self.z == 0, 1, 0) + jnp.where(self.z == self.depth - 1, 1, 0)
+        pl.semaphore_wait(barrier, 5 - ends)
+
+
+class Gather:
+    def __init__(self, place, index, staged, full, sems):
+        self.p, self.i, self.staged, self.full = place, index, staged, full
+        self.z_send, self.z_recv, self.ring_sent, self.ring_recv, self.core_sent, self.core_recv = sems
+        self.rows, self.half = staged.shape[1], full.shape[1] // 2
+
+    def line(self, source, way, step):
+        block = self.staged.at[source]
+        return pltpu.make_async_remote_copy(
+            block, block, self.z_send.at[self.i, way, step], self.z_recv.at[self.i, source],
+            device_id=self.p.down() if way else self.p.up(), device_id_type=MESH,
+        )
+
+    def open(self):
+        p = self.p
+
+        @pl.when(p.z < p.depth - 1)
+        def _():
+            self.line(p.z, 0, 0).start()
+
+        @pl.when(p.z > 0)
+        def _():
+            self.line(p.z, 1, 0).start()
+
+    def relay(self):
+        p = self.p
+        for step in range(1, p.depth):
+
+            @pl.when(p.z - step >= 0)
+            def _(step=step):
+                self.line(p.z - step, 0, step).wait_recv()
+
+                @pl.when(p.z < p.depth - 1)
+                def _():
+                    self.line(p.z - step, 0, step).start()
+
+            @pl.when(p.z + step < p.depth)
+            def _(step=step):
+                self.line(p.z + step, 1, step).wait_recv()
+
+                @pl.when(p.z > 0)
+                def _():
+                    self.line(p.z + step, 1, step).start()
+
+        rows = pl.ds(pl.multiple_of(p.row * self.rows, self.rows), self.rows)
+        self.full[rows, :] = jnp.concatenate([self.staged[z] for z in range(p.depth)], axis=1)
+
+    def line_sent(self):
+        p = self.p
+        for step in range(p.depth):
+
+            @pl.when((p.z - step >= 0) & (p.z < p.depth - 1))
+            def _(step=step):
+                self.line(p.z - step, 0, step).wait_send()
+
+            @pl.when((p.z + step < p.depth) & (p.z > 0))
+            def _(step=step):
+                self.line(p.z + step, 1, step).wait_send()
+
+    def piece(self, hop, way, core):
+        p = self.p
+        pos = p.pos + hop if way else p.pos - hop
+        row = 2 * p.chip_at(pos) + core
+        rows = pl.ds(pl.multiple_of(row * self.rows, self.rows), self.rows)
+        if hop == p.hops:
+            return self.full.at[rows, pl.ds(way * self.half, self.half)]
+        return self.full.at[rows, :]
+
+    def ring(self, hop, way):
+        p = self.p
+        pos = p.pos + hop - 1 if way else p.pos - hop + 1
+        row = 2 * p.chip_at(pos) + p.core
+        rows = pl.ds(pl.multiple_of(row * self.rows, self.rows), self.rows)
+        cols = pl.ds(way * self.half, self.half) if hop == p.hops else slice(None)
+        block = self.full.at[rows, cols]
+        return pltpu.make_async_remote_copy(
+            block, block, self.ring_sent.at[self.i, way, hop - 1], self.ring_recv.at[self.i, way, hop - 1],
+            device_id=p.left() if way else p.right(), device_id_type=MESH,
+        )
+
+    def landed(self, hop, way):
+        block = self.piece(hop, way, self.p.core)
+        return pltpu.make_async_remote_copy(
+            block, block, self.ring_sent.at[self.i, way, hop - 1], self.ring_recv.at[self.i, way, hop - 1],
+            device_id=self.p.left() if way else self.p.right(), device_id_type=MESH,
+        )
+
+    def pair(self, hop, way, core):
+        block = self.piece(hop, way, core)
+        slot = 0 if hop == 0 else 2 * hop - 1 + way
+        return pltpu.make_async_remote_copy(
+            block, block, self.core_sent.at[self.i, slot], self.core_recv.at[self.i, slot],
+            device_id=self.p.mate(), device_id_type=MESH,
+        )
+
+    def start_ring(self):
+        self.ring(1, 0).start()
+        self.ring(1, 1).start()
+        self.pair(0, 0, self.p.core).start()
+
+    def advance(self, hop):
+        for way in range(2):
+            self.landed(hop, way).wait_recv()
+            if hop < self.p.hops:
+                self.ring(hop + 1, way).start()
+            self.pair(hop, way, self.p.core).start()
+
+    def mate_has(self, hop):
+        for way in range(1 if hop == 0 else 2):
+            self.pair(hop, way, 1 - self.p.core).wait_recv()
+
+    def finish(self):
+        self.line_sent()
+        self.pair(0, 0, self.p.core).wait_send()
+        for hop in range(1, self.p.hops + 1):
+            for way in range(2):
+                self.ring(hop, way).wait_send()
+                self.pair(hop, way, self.p.core).wait_send()
+
+
+def gelu_parts(value):
+    part = 1.0 / (1.0 + jnp.abs(value) * (0.3275911 * 0.5**0.5))
+    bell = jnp.exp(value * value * -0.5)
+    tail = part * (0.127414796 + part * (-0.142248368 + part * (0.7107068705 + part * (-0.7265760135 + part * 0.5307027145))))
+    tail = tail * bell
+    below = jnp.where(value >= 0, 1.0 - tail, tail)
+    return value * below, below + value * bell * 0.3989422804014327
+
+
+def row_mean(field):
+    return jnp.mean(field, axis=1, keepdims=True)
+
+
+def fill_bias(seg_row, bias):
+    seg_key = seg_row[0:1, BLOCK:]
+    seg_query = jnp.broadcast_to(seg_key, (128, BLOCK)).T[:, 0:1]
+    bias[...] = jnp.where(seg_query == seg_key, 0.0, masked_score)
+
+
+def attend_pair(qkv, bias, context, logsum, model, block, pair):
+    rows = slice(block * BLOCK, (block + 1) * BLOCK)
+    cols = [pl.ds(pl.multiple_of(part * model + pair * 128, 128), 128) for part in range(3)]
+    qp, kp, vp = (qkv[rows, col] for col in cols)
+    total = 0.0
+    for head in range(2):
+        scores = contract(keep_head(qp, head), kp, 1, 1)
+        if block:
+            scores = scores + bias[...]
+        peak = jnp.max(scores, axis=1, keepdims=True)
+        expo = jnp.exp(scores - peak)
+        norm = jnp.sum(expo, axis=1, keepdims=True)
+        lse = jnp.broadcast_to(peak + jnp.log(norm), (BLOCK, 128)).T
+        logsum[pl.ds(pair * 2 + head, 1), rows] = lse[0:1]
+        part = contract(expo.astype(jnp.bfloat16), keep_head(vp, head), 1, 0)
+        total = total + part * (1.0 / norm)
+    context[rows, cols[0]] = total.astype(jnp.bfloat16)
+
+
+def forward_kernel(
+    chips, depth,
+    tokens_in, cot_in, qkv_in, out_in, up_in, down_in, seg_row, vecs,
+    output_o, two_o, two_low_o, qkv_o, context_o, normed_o, hidden_low_o, active_o, slope_o,
+    wqkv_o, wout_o, wup_o, wdown_o, logsum, factor, sums,
+    tokens, cot, s_qkv, s_out, s_up, s_down, w_qkv, w_out, w_up, w_down,
+    qkv, context, bias, hidden, hidden_low, normed, active, slope, two_low, output,
+    load, store, z_send, z_recv, ring_sent, ring_recv, core_sent, core_recv,
+):
+    p = Place(chips, depth)
+    rows, model = tokens.shape
+    pairs = HEADS // 2
+    loads = [
+        pltpu.make_async_copy(src, dst, load.at[i])
+        for i, (src, dst) in enumerate(
+            ((qkv_in, s_qkv.at[p.z]), (out_in, s_out.at[p.z]), (up_in, s_up.at[p.z]), (down_in, s_down.at[p.z]), (tokens_in, tokens), (cot_in, cot))
+        )
+    ]
+    for item in loads:
+        item.start()
+    sems = (z_send, z_recv, ring_sent, ring_recv, core_sent, core_recv)
+    g_qkv, g_out, g_up, g_down = (
+        Gather(p, i, staged, full, sems)
+        for i, (staged, full) in enumerate(((s_qkv, w_qkv), (s_out, w_out), (s_up, w_up), (s_down, w_down)))
+    )
+    stores = []
+
+    def put(src, dst):
+        copy = pltpu.make_async_copy(src, dst, store.at[len(stores)])
+        copy.start()
+        stores.append(copy)
+
+    p.meet()
+    for item, gather in zip(loads, (g_qkv, g_out, g_up, g_down)):
+        item.wait()
+        gather.open()
+    g_qkv.relay()
+    g_qkv.start_ring()
+    g_out.relay()
+    fill_bias(seg_row, bias)
+    for hop in range(1, p.hops):
+        g_qkv.advance(hop)
+    g_out.start_ring()
+    g_up.relay()
+    g_qkv.advance(p.hops)
+    g_up.start_ring()
+    loads[4].wait()
+    loads[5].wait()
+    for hop in range(p.hops + 1):
+        g_qkv.mate_has(hop)
+    put(w_qkv, wqkv_o)
+
+    def project(step, _):
+        tile, at = step % 3, pl.ds(pl.multiple_of(step // 3 * CHUNK, CHUNK), CHUNK)
+        cols = pl.ds(pl.multiple_of(tile * model, model), model)
+        got = contract(tokens[at, :], w_qkv[:, cols], 1, 0) + vecs[pl.ds(tile, 1), :]
+        got = got * jnp.where(tile == 0, HEAD_DIM ** (-0.5), 1.0)
+        qkv[at, cols] = got.astype(jnp.bfloat16)
+        return 0
+
+    lax.fori_loop(0, 3 * (rows // CHUNK), project, 0)
+    put(qkv, qkv_o)
+    for hop in range(1, p.hops):
+        g_out.advance(hop)
+
+    def attend_first(pair, _):
+        attend_pair(qkv, bias, context, logsum, model, 0, pair)
+        return 0
+
+    lax.fori_loop(0, pairs, attend_first, 0)
+    g_down.relay()
+
+    def attend_second(pair, _):
+        attend_pair(qkv, bias, context, logsum, model, 1, pair)
+
+        @pl.when(pair == pairs // 2 - 1)
+        def _():
+            for hop in range(1, p.hops):
+                g_up.advance(hop)
+            g_down.start_ring()
+
+        return 0
+
+    lax.fori_loop(0, pairs, attend_second, 0)
+    g_out.advance(p.hops)
+    put(context, context_o)
+    for hop in range(p.hops + 1):
+        g_out.mate_has(hop)
+    put(w_out, wout_o)
+
+    def first_norm(step, _):
+        at = pl.ds(pl.multiple_of(step * CHUNK, CHUNK), CHUNK)
+        resid = contract(context[at, :], w_out[...], 1, 0) + vecs[3:4, :] + tokens[at, :].astype(jnp.float32)
+        centre = resid - row_mean(resid)
+        scale = lax.rsqrt(row_mean(centre * centre) + norm_eps)
+        unit = centre * scale
+        normed[at, :] = unit
+        factor[at, :] = jnp.broadcast_to(scale, (CHUNK, 128))
+        value = unit * vecs[4:5, :] + vecs[5:6, :]
+        hidden[at, :] = value + vecs[6:7, :]
+        hidden_low[at, :] = value.astype(jnp.bfloat16)
+        return 0
+
+    lax.fori_loop(0, rows // CHUNK, first_norm, 0)
+    put(normed, normed_o)
+    put(hidden_low, hidden_low_o)
+    g_up.advance(p.hops)
+    for hop in range(p.hops + 1):
+        g_up.mate_has(hop)
+    put(w_up, wup_o)
+    tiles = active.shape[1] // model
+    steps = tiles * (rows // CHUNK)
+
+    def widen(step, _):
+        tile, at = step % tiles, pl.ds(pl.multiple_of(step // tiles * CHUNK, CHUNK), CHUNK)
+        cols = pl.ds(pl.multiple_of(tile * model, model), model)
+        value = contract(hidden_low[at, :], w_up[:, cols], 1, 0) + vecs[pl.ds(9 + tile, 1), :]
+        act, grade = gelu_parts(value)
+        active[at, cols] = act.astype(jnp.bfloat16)
+        slope[at, cols] = grade.astype(jnp.bfloat16)
+
+        @pl.when(step == steps * 3 // 4)
+        def _():
+            for hop in range(1, p.hops):
+                g_down.advance(hop)
+
+        return 0
+
+    lax.fori_loop(0, steps, widen, 0)
+    put(active, active_o)
+    put(slope, slope_o)
+    deep = 2 * g_down.rows
+
+    def narrow(chip):
+        span = pl.ds(pl.multiple_of(chip * deep, deep), deep)
+
+        def step_rows(step, _):
+            at = pl.ds(pl.multiple_of(step * CHUNK, CHUNK), CHUNK)
+            hidden[at, :] += contract(active[at, span], w_down[span, :], 1, 0)
             return 0
 
-        lax.fori_loop(0, HEADS // 2, pair_step, 0)
+        lax.fori_loop(0, rows // CHUNK, step_rows, 0)
+
+    for hop in range(p.hops):
+        g_down.mate_has(hop)
+        if hop == p.hops - 1:
+            g_down.advance(p.hops)
+        for way in range(1 if hop == 0 else 2):
+            narrow(p.chip_at(p.pos + hop if way else p.pos - hop))
+    g_down.mate_has(p.hops)
+    put(w_down, wdown_o)
+    narrow(p.chip_at(p.pos + p.hops))
+    sums[...] = jnp.zeros_like(sums)
+
+    def second_norm(step, _):
+        at = pl.ds(pl.multiple_of(step * CHUNK, CHUNK), CHUNK)
+        resid = hidden[at, :]
+        centre = resid - row_mean(resid)
+        scale = lax.rsqrt(row_mean(centre * centre) + norm_eps)
+        unit = centre * scale
+        output[at, :] = (unit * vecs[7:8, :] + vecs[8:9, :]).astype(jnp.bfloat16)
+        coming = cot[at, :].astype(jnp.float32)
+        inner = coming * vecs[7:8, :]
+        both = scale * (inner - row_mean(inner) - unit * row_mean(inner * unit))
+        hidden[at, :] = both
+        two_low[at, :] = both.astype(jnp.bfloat16)
+        sums[0:1, :] += jnp.sum(coming * unit, axis=0, keepdims=True)
+        sums[1:2, :] += jnp.sum(coming, axis=0, keepdims=True)
+        sums[2:3, :] += jnp.sum(both, axis=0, keepdims=True)
+        return 0
+
+    lax.fori_loop(0, rows // CHUNK, second_norm, 0)
+    put(output, output_o)
+    put(hidden, two_o)
+    put(two_low, two_low_o)
+    for gather in (g_qkv, g_out, g_up, g_down):
+        gather.finish()
+    for copy in stores:
+        copy.wait()
+
+
+def forward(chips, depth, tokens, cotangent, w_qkv, w_out, w_up, w_down, seg_row, vecs):
+    rows, model = tokens.shape
+    low, full = jnp.bfloat16, jnp.float32
+    weights = (w_qkv, w_out, w_up, w_down)
+    whole = [(2 * chips * w.shape[0], depth * w.shape[1]) for w in weights]
+    wide = whole[2][1]
+    shape = jax.ShapeDtypeStruct
+    outs = [
+        shape((rows, model), low), shape((rows, model), full), shape((rows, model), low),
+        shape((rows, 3 * model), low), shape((rows, model), low), shape((rows, model), full),
+        shape((rows, model), low), shape((rows, wide), low), shape((rows, wide), low),
+        *(shape(size, low) for size in whole),
+        shape((HEADS, rows), full), shape((rows, 128), full), shape((8, model), full),
+    ]
+    hops = chips // 2
+    return pl.pallas_call(
+        functools.partial(forward_kernel, chips, depth),
+        out_shape=outs,
+        in_specs=[ANY] * 6 + [VMEM] * 2,
+        out_specs=[ANY] * 13 + [VMEM] * 3,
+        scratch_shapes=[
+            pltpu.VMEM((rows, model), low), pltpu.VMEM((rows, model), low),
+            *(pltpu.VMEM((depth, *w.shape), low) for w in weights),
+            *(pltpu.VMEM(size, low) for size in whole),
+            pltpu.VMEM((rows, 3 * model), low), pltpu.VMEM((rows, model), low), pltpu.VMEM((BLOCK, BLOCK), full),
+            pltpu.VMEM((rows, model), full), pltpu.VMEM((rows, model), low), pltpu.VMEM((rows, model), full),
+            pltpu.VMEM((rows, wide), low), pltpu.VMEM((rows, wide), low),
+            pltpu.VMEM((rows, model), low), pltpu.VMEM((rows, model), low),
+            pltpu.SemaphoreType.DMA((6,)), pltpu.SemaphoreType.DMA((13,)),
+            pltpu.SemaphoreType.DMA((4, 2, depth)), pltpu.SemaphoreType.DMA((4, depth)),
+            pltpu.SemaphoreType.DMA((4, 2, hops)), pltpu.SemaphoreType.DMA((4, 2, hops)),
+            pltpu.SemaphoreType.DMA((4, 2 * hops + 1)), pltpu.SemaphoreType.DMA((4, 2 * hops + 1)),
+        ],
+        compiler_params=pltpu.CompilerParams(collective_id=0, has_side_effects=True, vmem_limit_bytes=67043328),
+        name="forward",
+    )(tokens, cotangent, *weights, seg_row, vecs)
 
 
 def attend_back_kernel(q, k, v, grad, context, logsum, seg_row, seg_col, dq, dk, dv, bias):
@@ -185,36 +566,23 @@
     tokens = roll_rows(tokens, start)
     cotangent = roll_rows(cotangent, start)
     seg_row, seg_col = segrow[None, :], segrow[:, None]
-    attn_qkv, attn_out = gather_block((w_qkv, w_out))
-    ffn_up, ffn_down = gather_block((w_up, w_down))
-    projected = jnp.dot(tokens, attn_qkv, preferred_element_type=jnp.float32)
-    queries = (projected[:, :model] + bias_query).astype(jnp.bfloat16) * jnp.bfloat16(HEAD_DIM ** (-0.5))
-    keys = projected[:, model : 2 * model].astype(jnp.bfloat16)
-    values = (projected[:, 2 * model :] + bias_value).astype(jnp.bfloat16)
-    wide = jax.ShapeDtypeStruct((tok_rows, model), jnp.bfloat16)
-    context, logsum = local_call(
-        attend_kernel,
-        [wide, jax.ShapeDtypeStruct((HEADS, tok_rows), jnp.float32)],
-        "attend",
-        queries, keys, values, seg_row, seg_col,
-    )
-    attended = jnp.dot(context, attn_out, preferred_element_type=jnp.float32) + bias_out
-    hidden, normed_one, factor_one = norm_rows(
-        tokens.astype(jnp.float32) + attended, gain_attn, shift_attn
-    )
-    hidden_low = hidden.astype(jnp.bfloat16)
-    upward = jnp.dot(hidden_low, ffn_up, preferred_element_type=jnp.float32) + bias_up
-    active_low = gelu_exact(upward).astype(jnp.bfloat16)
-    ffn_result = jnp.dot(active_low, ffn_down, preferred_element_type=jnp.float32) + bias_down
-    output, normed_two, factor_two = norm_rows(hidden + ffn_result, gain_ffn, shift_ffn)
-    grad_two, grad_gain_ffn, grad_shift_ffn = norm_back(
-        cotangent.astype(jnp.float32), normed_two, factor_two, gain_ffn
-    )
-    grad_bias_down = jnp.sum(grad_two, axis=0)
-    grad_two_low = grad_two.astype(jnp.bfloat16)
+    vecs = jnp.concatenate(
+        [
+            jnp.stack([bias_query, jnp.zeros_like(bias_query), bias_value, bias_out, gain_attn, shift_attn, bias_down, gain_ffn, shift_ffn]),
+            bias_up.reshape(-1, model),
+        ]
+    )
+    chips, depth = lax.axis_size("row") // 2, lax.axis_size("col")
+    (
+        output, grad_two, grad_two_low, projected, context, normed_one, hidden_low, active_low, slope,
+        attn_qkv, attn_out, ffn_up, ffn_down, logsum, factor_one, sums,
+    ) = forward(chips, depth, tokens, cotangent, w_qkv, w_out, w_up, w_down, seg_row, vecs)
+    factor_one = factor_one[:, :1]
+    queries, keys, values = (projected[:, i * model : (i + 1) * model] for i in range(3))
+    grad_gain_ffn, grad_shift_ffn, grad_bias_down = sums[0], sums[1], sums[2]
     grad_down_full = dot_rows(active_low, grad_two_low)
     grad_active = dot_back(grad_two_low, ffn_down)
-    grad_upward = jax.vjp(gelu_exact, upward)[1](grad_active)[0]
+    grad_upward = grad_active * slope.astype(jnp.float32)
     grad_bias_up = jnp.sum(grad_upward, axis=0)
     grad_up_low = grad_upward.astype(jnp.bfloat16)
     grad_up_full = dot_rows(hidden_low, grad_up_low)

time: 540 us -> 488 us (0.904)
  Pallas kernels: 45.5 us -> 143 us
  blocking collectives: 106 us -> 40.8 us
  matrix products: 128 us -> 65 us
  waiting for transfers between devices: 175 us -> 157 us
  local copies, waits for them, and re-layouts: 26.4 us -> 36.1 us
  other arithmetic: 30.9 us -> 22.7 us
    pallas_call x0 -> x1, Pallas kernels: none -> 115 us  [forward(): pl.pallas_call(functools.partial(forward_kernel, chips, depth), out_shape...]
    all_gather x4 -> x0, blocking collectives: 65.1 us -> none  [the longest x2 35 us: gather_block(): lax.all_gather(blocks[0], 'col', axis=1, tiled=True)]
    dot_general x4 -> x0, matrix products: 58.1 us -> none  [the longest x1 38.4 us: per_device(): jnp.dot(hidden_low, ffn_up, preferred_element_type=jnp.float32) + bias_up]
    pallas_call x2 -> x1, Pallas kernels: 45.5 us -> 27.4 us  [local_call(): pl.pallas_call(kernel, out_shape=outs, in_specs=[VMEM] * len(args), out_s...]
    all_gather x4 -> x0, waiting for transfers between devices: 13.5 us -> none  [the longest x2 10.5 us: gather_block(): lax.all_gather(widened[0], 'row', axis=0, tiled=True)]
    dot_general x4, matrix products: 41.4 us -> 33.1 us  [dot_back(): lax.dot_general(left, right, (((1,), (1,)), ((), ())), preferred_element_...]
    reduce_scatter x4, waiting for transfers between devices: 131 us -> 124 us  [one(): lax.psum_scatter(grad.astype(jnp.bfloat16), 'row', scatter_dimension=0, t...]
    reduce_sum x4 -> x1, other arithmetic: 7.14 us -> 0.37 us  [per_device(): grad_bias_query = jnp.sum(grad_queries, axis=0)]
  transfers between devices with their start and end apart: 12 -> 8, of which waited for: 7 -> 5; matrix products, arithmetic and copies ran while one was open for 23% -> 14% of each run, Pallas kernels for 9% -> 6%
where the time goes in v2:
time: 488 us; the launch traced here: 483 us
  waiting for transfers between devices  157 us (32%)
  Pallas kernels  143 us (29%)
  matrix products  65 us (13%)
  blocking collectives  40.8 us (8%)
  local copies, waits for them, and re-layouts  36.1 us (7%)
  other arithmetic  22.7 us (5%)
  between operations  18.1 us (4%)
    reduce_scatter x4, waiting for transfers between devices, one(): lax.psum_scatter(grad.astype(jnp.bfloat16), 'row', scatter_dimension=0, t...  124 us
    pallas_call x1, Pallas kernels, forward(): pl.pallas_call(functools.partial(forward_kernel, chips, depth), out_shape...  115 us
    psum x1, blocking collectives, per_device(): lax.psum((grad_bias_query, grad_bias_value, grad_bias_out, grad_gain_attn...  40.8 us
    dot_general x4, matrix products, dot_back(): lax.dot_general(left, right, (((1,), (1,)), ((), ())), preferred_element_...  33.1 us
    dot_general x4, matrix products, dot_rows(): lax.dot_general(left, right, (((0,), (0,)), ((), ())), preferred_element_...  32 us
    pallas_call x1, Pallas kernels, local_call(): pl.pallas_call(kernel, out_shape=outs, in_specs=[VMEM] * len(args), out_s...  27.4 us
    reduce_scatter x1, waiting for transfers between devices, one(): lax.psum_scatter(narrowed, 'col', scatter_dimension=1, tiled=True)  21 us
    unnamed x44, local copies, waits for them, and re-layouts  20.8 us
  transfers between devices with their start and end apart: 8, of which 5 were waited for; matrix products, arithmetic and copies ran while one was open for 14% of the time, Pallas kernels for 6%

profile of v2, /device:TPU:0, one launch (start us, length us, event | category | flops | bytes accessed | tf_op | source)
XLA Modules:
  0.0 483.1 jit_solution(10670742216268772731)
XLA Ops:
  7.2 0.8 constant_dynamic-slice_fusion
  8.0 0.9 compare_reduce_fusion
  10.9 0.7 stack.24
  11.6 0.7 stack.25
  12.2 0.7 stack.26
  16.4 0.7 reshape.45
  17.1 1.7 copy.36.down_in
  20.2 6.0 %fusion.6 = (bf16[1024,768]{1,0:T(8,128)(2,1)}, bf16[1024,768]{1,0:T(8,128)(2,1)}) fusion(s32[]{:T(128)S(6)} %select_n.24, bf16[1024,768]{1,0:T(8,128)(2,1)} %param.31, bf16[1024,768]{1,0:T(8,128)(2,1)} %param.16), kind=kLoop, calls=%fused_computation.25 | loop fusion | flops 6291456 | bytes 6291460 | tf_op jit(solution)/shard_map/concatenate | solution.py:538
  26.2 1.3 concatenate.25.vecs
  27.4 115.3 %forward.1 = (bf16[1024,768]{1,0:T(8,128)(2,1)}, f32[1024,768]{1,0:T(8,128)}, bf16[1024,768]{1,0:T(8,128)(2,1)}, bf16[1024,2304]{1,0:T(8,128)(2,1)}, bf16[1024,7...) custom-call(bf16[1024,768]{1,0:T(8,128)(2,1)} %get-tuple-element.129, ...), custom_call_target="tpu_custom_call" | custom-call | tf_op jit(solution)/shard_map/forward/pallas_call | solution.py:470
  142.8 1.2 slice_reduce_fusion
  144.0 11.2 %fusion = (f32[3072]{0:T(1024)S(1)}, f32[1024,3072]{1,0:T(8,128)}) fusion(bf16[1024,3072]{1,0:T(8,128)(2,1)} %get-tuple-element.41, bf16[1024,768]{1,0:T(8,128)(2,1)} %get-tuple-element.39, bf16[3072,768]{1,0:T(8,128)(2,1)} %get-tuple-element.40), kind=kOutput, calls=%fused_computation.1 | convolution fusion | flops 4841272320 | bytes 25178112 | tf_op jit(solution)/shard_map/dot_general | solution.py:36
  155.3 11.2 %multiply_reduce_fusion = (f32[768]{0:T(1024)S(1)}, f32[1024]{0:T(1024)S(1)}, f32[1024]{0:T(1024)S(1)}, f32[768]{0:T(1024)S(1)}, f32[1024,768]{1,0:T(8,128)S(1)}) fusion(f32[1024,768]{1,0:T(8,128)S(1)} %copy-done.7, f32[768]{0:T(1024)S(1)} %copy-done.14, f32[1024,768]{1,0:T(8,128)S(1)} %copy-done.15, bf16[768,3072]{1,0:T(8,128)(2,1)} %get-tuple-element.42, ...), kind=kOutput, calls=%fused_computation.16 | convolution fusion | flops 4847562752 | bytes 33047552 | tf_op jit(solution)/shard_map/dot_general | solution.py:36
  166.5 1.3 fusion.15
  167.9 2.5 convolution_convert_fusion.4
  170.5 3.8 convolution_convert_fusion.3.grad
  174.3 3.9 fusion.16
  178.2 1.0 copy.37.seg_col
  179.3 1.5 copy-done
  180.7 1.0 copy-done.1
  181.8 27.4 %attend_back.1 = (f32[1024,768]{1,0:T(8,128)}, f32[1024,768]{1,0:T(8,128)}, f32[1024,768]{1,0:T(8,128)}) custom-call(bf16[1024,768]{1,0:T(8,128)(2,1)S(1)} %copy-done, bf16[1024,768]{1,0:T(8,128)(2,1)S(1)} %get-tuple-element.119.k, bf16[1024,768]{1,0:T(8,128)(2,1)S(1)} %get-tuple-element.118.v, bf16[1024,768]{1,0:T(8,128)(2,1)} %convolution_convert_fusion.3.grad, ...), custom_call_target="tpu_custom_call" | custom-call | tf_op jit(solution)/shard_map/attend_back/pallas_call | solution.py:526
  209.2 2.2 convert.10
  212.4 2.2 copy-done.8
  215.0 1.2 copy-done.12
  216.2 6.1 %convolution_convert_fusion.2 = bf16[768,2304]{1,0:T(8,128)(2,1)} fusion(bf16[1024,768]{1,0:T(8,128)(2,1)S(1)} %copy-done.4, bf16[1024,768]{1,0:T(8,128)(2,1)S(1)} %get-tuple-element.122, bf16[1024,768]{1,0:T(8,128)(2,1)S(1)} %convert.10, bf16[1024,768]{1,0:T(8,128)(2,1)S(1)} %get-tuple-element.124), kind=kOutput, calls=%fused_computation.7 | convolution fusion | flops 3639803904 | bytes 9830400 | tf_op jit(solution)/shard_map/dot_general | solution.py:30
  222.3 1.3 copy-done.17
  223.7 10.0 %convolution_convert_fusion = bf16[3072,768]{1,0:T(8,128)(2,1)} fusion(bf16[1024,3072]{1,0:T(8,128)(2,1)} %get-tuple-element.53, bf16[1024,768]{1,0:T(8,128)(2,1)S(1)} %copy-done.17), kind=kOutput, calls=%fused_computation.5 | convolution fusion | flops 4834197504 | bytes 12582912 | tf_op jit(solution)/shard_map/dot_general | solution.py:30
  233.7 1.4 copy-done.16
  235.1 13.4 %convolution_convert_fusion.1 = bf16[768,3072]{1,0:T(8,128)(2,1)} fusion(bf16[1024,768]{1,0:T(8,128)(2,1)S(1)} %copy-done.16, f32[1024,3072]{1,0:T(8,128)} %get-tuple-element.127, bf16[1024,3072]{1,0:T(8,128)(2,1)} %get-tuple-element.41), kind=kOutput, calls=%fused_computation.6 | convolution fusion | flops 4843634688 | bytes 25165824 | tf_op jit(solution)/shard_map/dot_general | solution.py:30
  248.6 1.7 copy.41
  250.4 18.8 %reduce-scatter.15.cloned.1.call-done = bf16[96,2304]{1,0:T(8,128)(2,1)} async-done(((bf16[768,2304]{1,0:T(8,128)(2,1)}), bf16[96,2304]{1,0:T(8,128)(2,1)}) %reduce-scatter.15.cloned.1.call-update) | async-done | bytes 442384 | tf_op jit(solution)/shard_map/reduce_scatter | solution.py:21
  269.2 2.1 copy.39
  271.3 55.2 %reduce-scatter.23.cloned.1.call-done = bf16[384,768]{1,0:T(8,128)(2,1)} async-done(((bf16[3072,768]{1,0:T(8,128)(2,1)}), bf16[384,768]{1,0:T(8,128)(2,1)}) %reduce-scatter.23.cloned.1.call-update) | async-done | bytes 589840 | tf_op jit(solution)/shard_map/reduce_scatter | solution.py:21
  326.5 2.1 copy.43
  330.0 4.0 fusion.5
  334.0 49.6 %reduce-scatter.19.cloned.1.call-done = bf16[96,3072]{1,0:T(8,128)(2,1)} async-done(((bf16[768,3072]{1,0:T(8,128)(2,1)}), bf16[96,3072]{1,0:T(8,128)(2,1)}) %reduce-scatter.19.cloned.1.call-update) | async-done | bytes 589840 | tf_op jit(solution)/shard_map/reduce_scatter | solution.py:21
  383.6 0.9 slice_reduce_fusion.1
  384.5 40.8 %all-reduce = (f32[768]{0:T(1024)}, f32[768]{0:T(1024)}, f32[768]{0:T(1024)}, f32[768]{0:T(1024)}, f32[768]{0:T(1024)}, /*index=5*/f32[3072]{0:T(1024)}, f32[768]{0:T(1024)}, f32[768]{0:T(1024)}, f32[768]{0:T(1024)}) all-reduce(f32[768]{0:T(1024)S(1)} %get-tuple-element.123, ...), channel_id=1, replica_groups=mesh['row'=8,'col'=4] {'row','col'}, use_global_device_ids=true, to_apply=%region_12.13 | all-reduce | flops 9216 | bytes 73728 | tf_op jit(solution)/shard_map/psum | solution.py:622
  425.3 6.9 %fusion.4 = f32[1024,768]{1,0:T(8,128)S(1)} fusion(f32[1024,768]{1,0:T(8,128)S(1)} %copy-done.6, bf16[768,2304]{1,0:T(8,128)(2,1)} %get-tuple-element.51, bf16[1024,768]{1,0:T(8,128)(2,1)} %copy-done.12, bf16[1024,768]{1,0:T(8,128)(2,1)} %copy-done.10, bf16[1024,768]{1,0:T(8,128)(2,1)} %copy-done.11), kind=kOutput, calls=%fused_computation.22 | convolution fusion | flops 3638820864 | bytes 14548992 | tf_op jit(solution)/shard_map/dot_general | solution.py:36
  432.2 3.2 fusion.2
  435.4 0.9 copy.42
  436.9 1.0 copy.40
  438.0 0.7 convert_element_type.42
  438.7 12.6 %reduce-scatter.29.cloned.1.call-done = bf16[192,384]{1,0:T(8,128)(2,1)} async-done(((bf16[768,384]{1,0:T(8,128)(2,1)}), bf16[192,384]{1,0:T(8,128)(2,1)}) %reduce-scatter.29.cloned.1.call-update) | async-done | bytes 147472
  451.3 1.0 copy.44
  452.4 0.8 copy.38
  453.2 21.0 %reduce-scatter.21.cloned.1.call-done = bf16[96,768]{1,0:T(8,128)(2,1)} async-done(((bf16[96,3072]{1,0:T(8,128)(2,1)}), bf16[96,768]{1,0:T(8,128)(2,1)}) %reduce-scatter.21.cloned.1.call-update) | async-done | bytes 147472 | tf_op jit(solution)/shard_map/reduce_scatter | solution.py:24
  474.2 1.6 convert_element_type.46
  (62 shorter events, 7.4 us)
Async XLA Ops:
  7.2 241.4 %reduce-scatter.17.cloned.1.call-start = ((), (), s32[]{:S(2)}) async-start(), calls=%async_computation.9 | async-start | bytes 1327104 | tf_op jit(solution)/shard_map/reduce_scatter | solution.py:21
  144.0 11.2 %copy-start.7 = (f32[1024,768]{1,0:T(8,128)S(1)}, f32[1024,768]{1,0:T(8,128)}, u32[]{:S(2)}) copy-start(f32[1024,768]{1,0:T(8,128)} %get-tuple-element.43) | copy-start | bytes 9437188
  144.0 11.2 %copy-start.14 = (f32[768]{0:T(1024)S(1)}, f32[768]{0:T(1024)}, u32[]{:S(2)}) copy-start(f32[768]{0:T(1024)} %param.25) | copy-start | bytes 9220
  144.0 11.2 %copy-start.15 = (f32[1024,768]{1,0:T(8,128)S(1)}, f32[1024,768]{1,0:T(8,128)}, u32[]{:S(2)}) copy-start(f32[1024,768]{1,0:T(8,128)} %get-tuple-element.38) | copy-start | bytes 9437188
  166.5 1.4 copy-start.13
  167.8 2.7 copy-start.5
  170.4 98.8 %reduce-scatter.15.cloned.1.call-start = ((), (), s32[]{:S(2)}) async-start(), calls=%async_computation.8 | async-start | bytes 3981312 | tf_op jit(solution)/shard_map/reduce_scatter | solution.py:21
  174.3 3.9 copy-start.3
  174.3 5.0 %copy-start.2 = (f32[12,1024]{1,0:T(8,128)S(1)}, f32[12,1024]{1,0:T(8,128)}, u32[]{:S(2)}) copy-start(f32[12,1024]{1,0:T(8,128)} %get-tuple-element.47.logsum) | copy-start | bytes 147460
  179.3 1.5 copy-start
  180.7 1.0 copy-start.1
  209.2 2.8 copy-start.9
  211.4 3.6 copy-start.10
  211.4 3.2 copy-start.8
  212.4 2.6 copy-start.11
  212.4 3.8 copy-start.4
  215.0 1.2 copy-start.12
  222.3 1.4 copy-start.17
  222.3 104.2 %reduce-scatter.23.cloned.1.call-start = ((), (), s32[]{:S(2)}) async-start(), calls=%async_computation.12 | async-start | bytes 5308416 | tf_op jit(solution)/shard_map/reduce_scatter | solution.py:21
  233.7 1.5 copy-start.16
  233.7 149.9 %reduce-scatter.19.cloned.1.call-start = ((), (), s32[]{:S(2)}) async-start(), calls=%async_computation.10 | async-start | bytes 5308416 | tf_op jit(solution)/shard_map/reduce_scatter | solution.py:21
  248.5 186.9 %reduce-scatter.27.cloned.1.call-start = ((), (), s32[]{:S(2)}) async-start(), calls=%async_computation.14 | async-start | bytes 245760
  250.3 186.6 %reduce-scatter.25.cloned.1.call-start = ((), (), s32[]{:S(2)}) async-start(), calls=%async_computation.13 | async-start | bytes 737280
  271.3 154.0 %copy-start.6 = (f32[1024,768]{1,0:T(8,128)S(1)}, f32[1024,768]{1,0:T(8,128)}, u32[]{:S(2)}) copy-start(f32[1024,768]{1,0:T(8,128)} %copy-done.5) | copy-start | bytes 9437188
  271.3 180.0 %reduce-scatter.29.cloned.1.call-start = ((), (), s32[]{:S(2)}) async-start(), calls=%async_computation.15 | async-start | bytes 737280
  328.6 145.5 %reduce-scatter.21.cloned.1.call-start = ((), (), s32[]{:S(2)}) async-start(), calls=%async_computation.11 | async-start | bytes 737280 | tf_op jit(solution)/shard_map/reduce_scatter | solution.py:24
Sparse Core Ops, SparseCore 0:
  170.5 35.4 reduce-scatter.16
  222.4 46.7 reduce-scatter.14
  272.7 53.7 reduce-scatter.22
  329.8 53.7 reduce-scatter.18
  386.3 19.5 reduce-scatter.26
  408.1 20.4 reduce-scatter.24
  430.9 20.3 reduce-scatter.28
  453.6 20.5 reduce-scatter.20

commit v3 on v2

--- a/solution.py
+++ b/solution.py
@@ -14,38 +14,6 @@
 
 norm_eps = 1e-05
 masked_score = -1e30
-
-
-def reduce_grads(grads):
-    def one(grad):
-        narrowed = lax.psum_scatter(
-            grad.astype(jnp.bfloat16), "row", scatter_dimension=0, tiled=True
-        )
-        return lax.psum_scatter(narrowed, "col", scatter_dimension=1, tiled=True).astype(jnp.float32)
-
-    return tuple(one(grad) for grad in grads)
-
-
-def dot_rows(left, right):
-    return lax.dot_general(
-        left, right, (((0,), (0,)), ((), ())), preferred_element_type=jnp.float32
-    )
-
-
-def dot_back(left, right):
-    return lax.dot_general(
-        left, right, (((1,), (1,)), ((), ())), preferred_element_type=jnp.float32
-    )
-
-
-def norm_back(grad_result, normed, factor, gain):
-    grad_normed = grad_result * gain
-    grad_resid = factor * (
-        grad_normed
-        - jnp.mean(grad_normed, axis=1, keepdims=True)
-        - normed * jnp.mean(grad_normed * normed, axis=1, keepdims=True)
-    )
-    return (grad_resid, jnp.sum(grad_result * normed, axis=0), jnp.sum(grad_result, axis=0))
 
 
 BLOCK = 512
@@ -111,6 +79,14 @@
 
         ends = jnp.where(self.z == 0, 1, 0) + jnp.where(self.z == self.depth - 1, 1, 0)
         pl.semaphore_wait(barrier, 5 - ends)
+
+    def meet_all(self):
+        barrier = pltpu.get_barrier_semaphore()
+        others = [(2 * self.chip_at(self.pos + apart) + self.core, self.z) for apart in range(1, self.chips)]
+        others += [(self.row, (self.z + apart) % self.depth) for apart in range(1, self.depth)]
+        for device in [*others, self.mate()]:
+            pl.semaphore_signal(barrier, inc=1, device_id=device, device_id_type=MESH)
+        pl.semaphore_wait(barrier, self.chips + self.depth - 1)
 
 
 class Gather:
@@ -367,7 +343,7 @@
         centre = resid - row_mean(resid)
         scale = lax.rsqrt(row_mean(centre * centre) + norm_eps)
         unit = centre * scale
-        normed[at, :] = unit
+        normed[at, :] = unit.astype(jnp.bfloat16)
         factor[at, :] = jnp.broadcast_to(scale, (CHUNK, 128))
         value = unit * vecs[4:5, :] + vecs[5:6, :]
         hidden[at, :] = value + vecs[6:7, :]
@@ -461,7 +437,7 @@
     shape = jax.ShapeDtypeStruct
     outs = [
         shape((rows, model), low), shape((rows, model), full), shape((rows, model), low),
-        shape((rows, 3 * model), low), shape((rows, model), low), shape((rows, model), full),
+        shape((rows, 3 * model), low), shape((rows, model), low), shape((rows, model), low),
         shape((rows, model), low), shape((rows, wide), low), shape((rows, wide), low),
         *(shape(size, low) for size in whole),
         shape((HEADS, rows), full), shape((rows, 128), full), shape((8, model), full),
@@ -477,7 +453,7 @@
             *(pltpu.VMEM((depth, *w.shape), low) for w in weights),
             *(pltpu.VMEM(size, low) for size in whole),
             pltpu.VMEM((rows, 3 * model), low), pltpu.VMEM((rows, model), low), pltpu.VMEM((BLOCK, BLOCK), full),
-            pltpu.VMEM((rows, model), full), pltpu.VMEM((rows, model), low), pltpu.VMEM((rows, model), full),
+            pltpu.VMEM((rows, model), full), pltpu.VMEM((rows, model), low), pltpu.VMEM((rows, model), low),
             pltpu.VMEM((rows, wide), low), pltpu.VMEM((rows, wide), low),
             pltpu.VMEM((rows, model), low), pltpu.VMEM((rows, model), low),
             pltpu.SemaphoreType.DMA((6,)), pltpu.SemaphoreType.DMA((13,)),
@@ -490,48 +466,479 @@
     )(tokens, cotangent, *weights, seg_row, vecs)
 
 
-def attend_back_kernel(q, k, v, grad, context, logsum, seg_row, seg_col, dq, dk, dv, bias):
-    bias[...] = jnp.where(seg_col[BLOCK:, :] == seg_row[0:1, BLOCK:], 0.0, masked_score)
-    for block in range(2):
-        rows = slice(block * BLOCK, (block + 1) * BLOCK)
-
-        def pair_step(pair, _, rows=rows, block=block):
-            cols = pl.ds(pl.multiple_of(pair * 128, 128), 128)
-            qp, kp, vp, gp = q[rows, cols], k[rows, cols], v[rows, cols], grad[rows, cols]
-            prod = (gp.astype(jnp.float32) * context[rows, cols].astype(jnp.float32)).T
-            sum_q = sum_k = sum_v = 0.0
-            for head in range(2):
-                inner = jnp.sum(prod[head * HEAD_DIM : (head + 1) * HEAD_DIM], axis=0, keepdims=True)
-                qh, gh, kh = keep_head(qp, head), keep_head(gp, head), keep_head(kp, head)
-                scores = contract(kp, qh, 1, 1)
-                if block:
-                    scores = scores + bias[...]
-                prob = jnp.exp(scores - logsum[pl.ds(pair * 2 + head, 1), rows])
-                raw = (prob * (contract(vp, gh, 1, 1) - inner)).astype(jnp.bfloat16)
-                sum_v = sum_v + contract(prob.astype(jnp.bfloat16), gh, 1, 0)
-                sum_k = sum_k + contract(raw, qh, 1, 0)
-                sum_q = sum_q + contract(raw, kh, 0, 0)
-            dq[rows, cols] = sum_q * HEAD_DIM ** (-0.5)
-            dk[rows, cols] = sum_k
-            dv[rows, cols] = sum_v
+VMEM = pl.BlockSpec(memory_space=pltpu.VMEM)
+
+
+class Reduce:
+    def __init__(self, place, index, bufs, result, sems):
+        self.p, self.i, self.result = place, index, result
+        self.grad, self.other, self.halves, self.fulls, self.parts, self.came, self.total = bufs
+        self.core_sent, self.core_recv, self.ring_sent, self.ring_recv, self.z_sent, self.z_recv, self.res_sem = sems
+        self.half = self.grad.shape[3] // 2
+
+    def pair(self):
+        return pltpu.make_async_remote_copy(
+            self.grad.at[:, 1 - self.p.core], self.other, self.core_sent.at[self.i], self.core_recv.at[self.i],
+            device_id=self.p.mate(), device_id_type=MESH,
+        )
+
+    def swap(self):
+        self.pair().start()
+
+    def absorb(self):
+        self.pair().wait_recv()
+
+        def step(chip, _):
+            both = self.grad[chip, self.p.core].astype(jnp.float32) + self.other[chip].astype(jnp.float32)
+            self.grad[chip, self.p.core] = both.astype(jnp.bfloat16)
             return 0
 
-        lax.fori_loop(0, HEADS // 2, pair_step, 0)
-
-
-VMEM = pl.BlockSpec(memory_space=pltpu.VMEM)
-
-
-def local_call(kernel, outs, name, *args):
+        lax.fori_loop(0, self.p.chips, step, 0)
+
+    def span(self, hop, way):
+        return pl.ds((1 - way) * self.half, self.half) if hop == 1 else slice(None)
+
+    def ring(self, hop, way):
+        p = self.p
+        dest = p.pos - p.hops + hop - 1 if way else p.pos + p.hops - hop + 1
+        return pltpu.make_async_remote_copy(
+            self.grad.at[p.chip_at(dest), p.core, :, self.span(hop, way)],
+            self.halves.at[way] if hop == 1 else self.fulls.at[way, hop - 2],
+            self.ring_sent.at[self.i, way, hop - 1], self.ring_recv.at[self.i, way, hop - 1],
+            device_id=p.left() if way else p.right(), device_id_type=MESH,
+        )
+
+    def go(self, hop):
+        self.ring(hop, 0).start()
+        self.ring(hop, 1).start()
+
+    def take(self, hop):
+        p = self.p
+        for way in range(2):
+            self.ring(hop, way).wait_recv()
+            chip = p.chip_at(p.pos - p.hops + hop if way else p.pos + p.hops - hop)
+            got = self.halves[way] if hop == 1 else self.fulls[way, hop - 2]
+            cols = self.span(hop, way)
+            both = self.grad[chip, p.core, :, cols].astype(jnp.float32) + got.astype(jnp.float32)
+            self.grad[chip, p.core, :, cols] = both.astype(jnp.bfloat16)
+
+    def split(self):
+        p = self.p
+        self.ring(p.hops, 0).wait_recv()
+        self.ring(p.hops, 1).wait_recv()
+        last = p.hops - 2
+        low = (
+            self.grad[p.chip, p.core].astype(jnp.float32)
+            + self.fulls[0, last].astype(jnp.float32)
+            + self.fulls[1, last].astype(jnp.float32)
+        ).astype(jnp.bfloat16)
+        wide = self.parts.shape[2]
+        for z in range(p.depth):
+            self.parts[z] = low[:, z * wide : (z + 1) * wide]
+
+    def line(self, block, way):
+        return pltpu.make_async_remote_copy(
+            self.parts.at[block], self.came.at[block + 1 - way],
+            self.z_sent.at[self.i, way, block], self.z_recv.at[self.i, way, block],
+            device_id=self.p.down() if way else self.p.up(), device_id_type=MESH,
+        )
+
+    def round(self, turn):
+        p = self.p
+        for way in range(2):
+            far = p.depth - 1 - p.z if way else p.z
+            block = turn - far if way else p.depth - 1 - turn + far
+
+            @pl.when(far <= turn)
+            def _(far=far, block=block, way=way):
+                @pl.when(far > 0)
+                def _():
+                    self.line(block, way).wait_recv()
+                    both = self.parts[block].astype(jnp.float32) + self.came[block + 1 - way].astype(jnp.float32)
+                    self.parts[block] = both.astype(jnp.bfloat16)
+
+                self.line(block, way).start()
+
+    def write(self):
+        return pltpu.make_async_copy(self.total, self.result, self.res_sem.at[self.i])
+
+    def land(self):
+        p = self.p
+        self.total[...] = self.parts[p.z].astype(jnp.float32)
+
+        @pl.when(p.z > 0)
+        def _():
+            self.line(p.z, 0).wait_recv()
+            self.total[...] += self.came[p.z + 1].astype(jnp.float32)
+
+        @pl.when(p.z < p.depth - 1)
+        def _():
+            self.line(p.z, 1).wait_recv()
+            self.total[...] += self.came[p.z].astype(jnp.float32)
+
+        self.write().start()
+
+    def finish(self):
+        p = self.p
+        self.pair().wait_send()
+        for hop in range(1, p.hops + 1):
+            for way in range(2):
+                self.ring(hop, way).wait_send()
+        for turn in range(p.depth - 1):
+            for way in range(2):
+                far = p.depth - 1 - p.z if way else p.z
+                block = turn - far if way else p.depth - 1 - turn + far
+
+                @pl.when(far <= turn)
+                def _(block=block, way=way):
+                    self.line(block, way).wait_send()
+
+        self.write().wait()
+
+    def stages(self):
+        def first():
+            self.absorb()
+            self.go(1)
+
+        def along(hop):
+            self.take(hop)
+            self.go(hop + 1)
+
+        def begin():
+            self.split()
+            self.round(0)
+
+        p = self.p
+        return [
+            [first, *(functools.partial(along, hop) for hop in range(1, p.hops)), begin],
+            [*(functools.partial(self.round, turn) for turn in range(1, p.depth - 1)), self.land],
+        ]
+
+
+class Sums:
+    def __init__(self, place, sums, mine, pair, plane, line, sems):
+        self.p, self.sums, self.mine, self.other, self.plane, self.col = place, sums, mine, pair, plane, line
+        self.pair_sent, self.pair_recv, self.plane_sent, self.plane_recv, self.col_sent, self.col_recv = sems
+
+    def pair(self):
+        return pltpu.make_async_remote_copy(
+            self.mine, self.other, self.pair_sent, self.pair_recv, device_id=self.p.mate(), device_id_type=MESH
+        )
+
+    def chip(self, apart, source):
+        target = (2 * self.p.chip_at(self.p.pos + apart) + self.p.core, self.p.z)
+        return pltpu.make_async_remote_copy(
+            self.plane.at[source], self.plane.at[source], self.plane_sent.at[apart], self.plane_recv.at[source],
+            device_id=target, device_id_type=MESH,
+        )
+
+    def level(self, apart, source):
+        target = (self.p.row, (self.p.z + apart) % self.p.depth)
+        return pltpu.make_async_remote_copy(
+            self.col.at[source], self.col.at[source], self.col_sent.at[apart], self.col_recv.at[source],
+            device_id=target, device_id_type=MESH,
+        )
+
+    def start(self):
+        self.mine[...] = self.sums[...]
+        self.pair().start()
+
+    def across(self):
+        p = self.p
+        self.pair().wait_recv()
+        self.plane[p.chip] = self.mine[...] + self.other[...]
+        for apart in range(1, p.chips):
+            self.chip(apart, p.chip).start()
+
+    def along(self):
+        p = self.p
+        for apart in range(1, p.chips):
+            self.chip(apart, p.chip_at(p.pos + apart)).wait_recv()
+        total = self.plane[0]
+        for chip in range(1, p.chips):
+            total = total + self.plane[chip]
+        self.col[p.z] = total
+        for apart in range(1, p.depth):
+            self.level(apart, p.z).start()
+
+    def land(self, result):
+        p = self.p
+        for apart in range(1, p.depth):
+            self.level(apart, (p.z + apart) % p.depth).wait_recv()
+        total = self.col[0]
+        for z in range(1, p.depth):
+            total = total + self.col[z]
+        result[...] = total
+
+    def finish(self):
+        p = self.p
+        self.pair().wait_send()
+        for apart in range(1, p.chips):
+            self.chip(apart, p.chip).wait_send()
+        for apart in range(1, p.depth):
+            self.level(apart, p.z).wait_send()
+
+
+def backward_kernel(
+    chips, depth,
+    two_low_in, active_in, wdown_in, slope_in, hidden_low_in, wup_in, two_in, normed_in, factor_in, wout_in, context_in,
+    qkv_in, tokens_in, wqkv_in, seg_row, vecs, logsum, sums_in,
+    tokens_o, qkv_o, out_o, up_o, down_o, sums_o,
+    two_low, active, slope, hidden_low, tiles, acc, normed, factor, w_out, bias, sums,
+    *rest,
+):
+    p = Place(chips, depth)
+    groups = [rest[7 * i : 7 * i + 7] for i in range(4)]
+    mine, other, plane, col = rest[28:32]
+    load, store, core_sent, core_recv, ring_sent, ring_recv, z_sent, z_recv, res_sem = rest[32:41]
+    sum_sems = rest[41:47]
+    rows, model = two_low.shape
+    wide = active.shape[1]
+    count = wide // model
+    pairs = HEADS // 2
+    sems = (core_sent, core_recv, ring_sent, ring_recv, z_sent, z_recv, res_sem)
+    r_qkv, r_out, r_up, r_down = (
+        Reduce(p, i, bufs, result, sems) for i, (bufs, result) in enumerate(zip(groups, (qkv_o, out_o, up_o, down_o)))
+    )
+    used = []
+
+    def fetch(src, dst):
+        copy = pltpu.make_async_copy(src, dst, load.at[len(used)])
+        copy.start()
+        used.append(copy)
+        return copy
+
+    def col_tile(ref, tile):
+        return ref.at[:, pl.ds(tile * model, model)]
+
+    got_two_low = fetch(two_low_in, two_low)
+    got_active = [fetch(col_tile(active_in, t), col_tile(active, t)) for t in range(count)]
+    got_down = [fetch(wdown_in.at[pl.ds(t * model, model), :], tiles.at[t]) for t in range(count)]
+    got_slope = [fetch(col_tile(slope_in, t), col_tile(slope, t)) for t in range(count)]
+    got_rest = [
+        fetch(src, dst)
+        for src, dst in ((hidden_low_in, hidden_low), (two_in, acc), (normed_in, normed), (factor_in, factor), (wout_in, w_out))
+    ]
+    p.meet_all()
+
+    def weight_grad(reduce, left, right, left_at, tile, skip=0):
+        piece = 384
+        cols = pl.ds(pl.multiple_of(tile * model, model), model)
+        got = contract(left[:, pl.ds(pl.multiple_of(skip + left_at * piece, 128), piece)], right[:, cols], 0, 0)
+        high = reduce.grad.shape[2]
+        for s in range(piece // high):
+            row = left_at * (piece // high) + s
+            reduce.grad[row // 2, row % 2, :, cols] = got[s * high : (s + 1) * high].astype(jnp.bfloat16)
+
+    got_two_low.wait()
+    for t in range(count):
+        got_active[t].wait()
+
+        def down_grad(step, _, t=t):
+            weight_grad(r_down, active, two_low, t * (model // 384) + step, 0)
+            return 0
+
+        lax.fori_loop(0, model // 384, down_grad, 0)
+    r_down.swap()
+    got_qkv = fetch(qkv_in, active.at[:, pl.ds(0, 3 * model)])
+    sums[...] = jnp.zeros_like(sums)
+    sums[9:10, :] = sums_in[2:3, :]
+    sums[10:12, :] = sums_in[0:2, :]
+    got_up = []
+    for t in range(count):
+        got_down[t].wait()
+        got_slope[t].wait()
+        cols = pl.ds(t * model, model)
+
+        def upward_grad(step, _, t=t, cols=cols):
+            at = pl.ds(pl.multiple_of(step * CHUNK, CHUNK), CHUNK)
+            got = contract(two_low[at, :], tiles[t], 1, 1) * slope[at, cols].astype(jnp.float32)
+            slope[at, cols] = got.astype(jnp.bfloat16)
+            sums[5 + t : 6 + t, :] += jnp.sum(got, axis=0, keepdims=True)
+            return 0
+
+        lax.fori_loop(0, rows // CHUNK, upward_grad, 0)
+        got_up.append(fetch(col_tile(wup_in, t), tiles.at[t]))
+    down_one, down_two = r_down.stages()
+    down_one[0]()
+    got_rest[0].wait()
+
+    def up_grad(step, _):
+        weight_grad(r_up, hidden_low, slope, step // count, step % count)
+        return 0
+
+    lax.fori_loop(0, count * (model // 384), up_grad, 0)
+    r_up.swap()
+    got_tokens = fetch(tokens_in, hidden_low)
+    for stage in down_one[1:-1]:
+        stage()
+    for item in got_rest[1:] + got_up:
+        item.wait()
+
+    def first_norm(step, _):
+        at = pl.ds(pl.multiple_of(step * CHUNK, CHUNK), CHUNK)
+        whole = acc[at, :]
+        for t in range(count):
+            whole = whole + contract(slope[at, t * model : (t + 1) * model], tiles[t], 1, 1)
+        unit, scale = normed[at, :].astype(jnp.float32), factor[at, 0:1]
+        inner = whole * vecs[4:5, :]
+        both = scale * (inner - row_mean(inner) - unit * row_mean(inner * unit))
+        acc[at, :] = both
+        low = both.astype(jnp.bfloat16)
+        two_low[at, :] = low
+        sums[2:3, :] += jnp.sum(both, axis=0, keepdims=True)
+        sums[3:4, :] += jnp.sum(whole * unit, axis=0, keepdims=True)
+        sums[4:5, :] += jnp.sum(whole, axis=0, keepdims=True)
+        active[at, pl.ds(3 * model, model)] = contract(low, w_out[...], 1, 1).astype(jnp.bfloat16)
+        return 0
+
+    lax.fori_loop(0, rows // CHUNK, first_norm, 0)
+    got_context = fetch(context_in, slope.at[:, pl.ds(3 * model, model)])
+    got_wqkv = [fetch(col_tile(wqkv_in, t), tiles.at[t]) for t in range(3)]
+    up_one, up_two = r_up.stages()
+    up_one[0]()
+
+    got_context.wait()
+
+    def out_grad(step, _):
+        weight_grad(r_out, slope, two_low, step, 0, 3 * model)
+        return 0
+
+    lax.fori_loop(0, model // 384, out_grad, 0)
+    r_out.swap()
+    fill_bias(seg_row, bias)
+    got_qkv.wait()
+    out_one, out_two = r_out.stages()
+
+    def pair_back(pair, block):
+        at = slice(block * BLOCK, (block + 1) * BLOCK)
+        cols = [pl.ds(pl.multiple_of(part * model + pair * 128, 128), 128) for part in range(4)]
+        qp, kp, vp, gp = (active[at, col] for col in cols)
+        prod = (gp.astype(jnp.float32) * slope[at, cols[3]].astype(jnp.float32)).T
+        sum_q = sum_k = sum_v = 0.0
+        for head in range(2):
+            inner = jnp.sum(prod[head * HEAD_DIM : (head + 1) * HEAD_DIM], axis=0, keepdims=True)
+            qh, gh, kh = keep_head(qp, head), keep_head(gp, head), keep_head(kp, head)
+            scores = contract(kp, qh, 1, 1)
+            if block:
+                scores = scores + bias[...]
+            prob = jnp.exp(scores - logsum[pl.ds(pair * 2 + head, 1), at])
+            raw = (prob * (contract(vp, gh, 1, 1) - inner)).astype(jnp.bfloat16)
+            sum_v = sum_v + contract(prob.astype(jnp.bfloat16), gh, 1, 0)
+            sum_k = sum_k + contract(raw, qh, 1, 0)
+            sum_q = sum_q + contract(raw, kh, 0, 0)
+        sum_q = sum_q * HEAD_DIM ** (-0.5)
+        for col, got in zip(cols, (sum_q, sum_k, sum_v)):
+            slope[at, col] = got.astype(jnp.bfloat16)
+        sums[0:1, cols[0]] += jnp.sum(sum_q, axis=0, keepdims=True)
+        sums[1:2, cols[0]] += jnp.sum(sum_v, axis=0, keepdims=True)
+
+    hooks = {
+        (0, 0): [out_one[0]],
+        (0, 1): [down_one[-1]],
+        (1, 1): down_two[:1],
+        (2, 0): up_one[1:-1],
+        (2, 1): down_two[1:-1],
+        (3, 0): out_one[1:-1],
+        (3, 1): down_two[-1:],
+    }
+
+    def attend_back(pair, _):
+        for block in range(2):
+            pair_back(pair, block)
+            for (when, part), todo in hooks.items():
+                if part == block:
+
+                    @pl.when(pair == when)
+                    def _(todo=todo):
+                        for stage in todo:
+                            stage()
+
+        return 0
+
+    lax.fori_loop(0, pairs, attend_back, 0)
+    got_tokens.wait()
+    for item in got_wqkv:
+        item.wait()
+
+    def qkv_grad(step, _):
+        weight_grad(r_qkv, hidden_low, slope, step // 3, step % 3)
+        return 0
+
+    lax.fori_loop(0, 3 * (model // 384), qkv_grad, 0)
+    r_qkv.swap()
+    small = Sums(p, sums, mine, other, plane, col, sum_sems)
+    small.start()
+    up_one[-1]()
+
+    def token_grad(step, _):
+        at = pl.ds(pl.multiple_of(step * CHUNK, CHUNK), CHUNK)
+        whole = acc[at, :]
+        for t in range(3):
+            whole = whole + contract(slope[at, t * model : (t + 1) * model], tiles[t], 1, 1)
+        acc[at, :] = whole
+        return 0
+
+    half = rows // CHUNK // 2
+    lax.fori_loop(0, half, token_grad, 0)
+    qkv_one, qkv_two = r_qkv.stages()
+    qkv_one[0]()
+    small.across()
+    out_one[-1]()
+    lax.fori_loop(half, rows // CHUNK, token_grad, 0)
+    tokens_out = pltpu.make_async_copy(acc, tokens_o, store.at[0])
+    tokens_out.start()
+    small.along()
+    up_two[0]()
+    for stage in qkv_one[1:-1]:
+        stage()
+    out_two[0]()
+    small.land(sums_o)
+    for stage in up_two[1:] + out_two[1:]:
+        stage()
+    qkv_one[-1]()
+    for stage in qkv_two:
+        stage()
+    small.finish()
+    for reduce in (r_down, r_up, r_out, r_qkv):
+        reduce.finish()
+    tokens_out.wait()
+
+
+def backward(chips, depth, blocks, ins, vmem_ins):
+    rows, model = ins[0].shape
+    wide = ins[1].shape[1]
+    hops = chips // 2
+    low, full = jnp.bfloat16, jnp.float32
+    shape, dma = jax.ShapeDtypeStruct, pltpu.SemaphoreType.DMA
+    bufs = []
+    for high, across in blocks:
+        whole = depth * across
+        bufs += [
+            pltpu.VMEM((chips, 2, high, whole), low), pltpu.VMEM((chips, high, whole), low),
+            pltpu.VMEM((2, high, whole // 2), low), pltpu.VMEM((2, hops - 1, high, whole), low),
+            pltpu.VMEM((depth, high, across), low), pltpu.VMEM((depth + 1, high, across), low),
+            pltpu.VMEM((high, across), full),
+        ]
     return pl.pallas_call(
-        kernel,
-        out_shape=outs,
-        in_specs=[VMEM] * len(args),
-        out_specs=[VMEM] * len(outs),
-        scratch_shapes=[pltpu.VMEM((BLOCK, BLOCK), jnp.float32)],
-        compiler_params=pltpu.CompilerParams(vmem_limit_bytes=48 << 20),
-        name=name,
-    )(*args)
+        functools.partial(backward_kernel, chips, depth),
+        out_shape=[shape((rows, model), full), *(shape(size, full) for size in blocks), shape((16, model), full)],
+        in_specs=[ANY] * len(ins) + [VMEM] * len(vmem_ins),
+        out_specs=[ANY] * 5 + [VMEM],
+        scratch_shapes=[
+            pltpu.VMEM((rows, model), low), pltpu.VMEM((rows, wide), low), pltpu.VMEM((rows, wide), low),
+            pltpu.VMEM((rows, model), low), pltpu.VMEM((wide // model, model, model), low), pltpu.VMEM((rows, model), full),
+            pltpu.VMEM((rows, model), low), pltpu.VMEM((rows, 128), full), pltpu.VMEM((model, model), low),
+            pltpu.VMEM((BLOCK, BLOCK), full), pltpu.VMEM((16, model), full),
+            *bufs,
+            pltpu.VMEM((16, model), full), pltpu.VMEM((16, model), full),
+            pltpu.VMEM((chips, 16, model), full), pltpu.VMEM((depth, 16, model), full),
+            dma((32,)), dma((1,)), dma((4,)), dma((4,)), dma((4, 2, hops)), dma((4, 2, hops)), dma((4, 2, depth)), dma((4, 2, depth)), dma((4,)),
+            dma, dma, dma((chips,)), dma((chips,)), dma((depth,)), dma((depth,)),
+        ],
+        compiler_params=pltpu.CompilerParams(collective_id=1, has_side_effects=True, vmem_limit_bytes=67043328),
+        name="backward",
+    )(*ins, *vmem_ins)
 
 
 def roll_rows(field, start):
@@ -565,7 +972,7 @@
     segrow = roll_rows(segrow, start)
     tokens = roll_rows(tokens, start)
     cotangent = roll_rows(cotangent, start)
-    seg_row, seg_col = segrow[None, :], segrow[:, None]
+    seg_row = segrow[None, :]
     vecs = jnp.concatenate(
         [
             jnp.stack([bias_query, jnp.zeros_like(bias_query), bias_value, bias_out, gain_attn, shift_attn, bias_down, gain_ffn, shift_ffn]),
@@ -577,78 +984,32 @@
         output, grad_two, grad_two_low, projected, context, normed_one, hidden_low, active_low, slope,
         attn_qkv, attn_out, ffn_up, ffn_down, logsum, factor_one, sums,
     ) = forward(chips, depth, tokens, cotangent, w_qkv, w_out, w_up, w_down, seg_row, vecs)
-    factor_one = factor_one[:, :1]
-    queries, keys, values = (projected[:, i * model : (i + 1) * model] for i in range(3))
-    grad_gain_ffn, grad_shift_ffn, grad_bias_down = sums[0], sums[1], sums[2]
-    grad_down_full = dot_rows(active_low, grad_two_low)
-    grad_active = dot_back(grad_two_low, ffn_down)
-    grad_upward = grad_active * slope.astype(jnp.float32)
-    grad_bias_up = jnp.sum(grad_upward, axis=0)
-    grad_up_low = grad_upward.astype(jnp.bfloat16)
-    grad_up_full = dot_rows(hidden_low, grad_up_low)
-    grad_hidden = grad_two + dot_back(grad_up_low, ffn_up)
-    block_up, block_down = reduce_grads((grad_up_full, grad_down_full))
-    grad_one, grad_gain_attn, grad_shift_attn = norm_back(
-        grad_hidden, normed_one, factor_one, gain_attn
+    grad_tokens, block_qkv, block_out, block_up, block_down, sums = backward(
+        chips, depth,
+        (w_qkv.shape, w_out.shape, w_up.shape, w_down.shape),
+        (
+            grad_two_low, active_low, ffn_down, slope, hidden_low, ffn_up, grad_two, normed_one, factor_one, attn_out, context,
+            projected, tokens, attn_qkv,
+        ),
+        (seg_row, vecs, logsum, sums),
     )
-    grad_bias_out = jnp.sum(grad_one, axis=0)
-    grad_one_low = grad_one.astype(jnp.bfloat16)
-    grad_out_full = dot_rows(context, grad_one_low)
-    grad_context = dot_back(grad_one_low, attn_out).astype(jnp.bfloat16)
-
-    full = jax.ShapeDtypeStruct((tok_rows, model), jnp.float32)
-    grad_queries, grad_keys, grad_values = local_call(
-        attend_back_kernel,
-        [full, full, full],
-        "attend_back",
-        queries, keys, values, grad_context, context, logsum, seg_row, seg_col,
-    )
-    grad_bias_query = jnp.sum(grad_queries, axis=0)
-    grad_bias_value = jnp.sum(grad_values, axis=0)
-    grad_proj_low = jnp.concatenate([grad_queries, grad_keys, grad_values], axis=1).astype(jnp.bfloat16)
-    grad_qkv_full = dot_rows(tokens, grad_proj_low)
-    grad_tokens = grad_one + dot_back(grad_proj_low, attn_qkv)
-    block_qkv, block_out = reduce_grads((grad_qkv_full, grad_out_full))
-    (
-        sum_query,
-        sum_value,
-        sum_out,
-        sum_gain_attn,
-        sum_shift_attn,
-        sum_up,
-        sum_down,
-        sum_gain_ffn,
-        sum_shift_ffn,
-    ) = lax.psum(
-        (
-            grad_bias_query,
-            grad_bias_value,
-            grad_bias_out,
-            grad_gain_attn,
-            grad_shift_attn,
-            grad_bias_up,
-            grad_bias_down,
-            grad_gain_ffn,
-            grad_shift_ffn,
-        ),
-        ("row", "col"),
-    )
+    wide = bias_up.shape[0] // model
     return (
-        roll_rows(output.astype(jnp.bfloat16), back),
+        roll_rows(output, back),
         roll_rows(grad_tokens, back),
         block_qkv,
         block_out,
         block_up,
         block_down,
-        sum_query,
-        sum_value,
-        sum_out,
-        sum_gain_attn,
-        sum_shift_attn,
-        sum_up,
-        sum_down,
-        sum_gain_ffn,
-        sum_shift_ffn,
+        sums[0],
+        sums[1],
+        sums[2],
+        sums[3],
+        sums[4],
+        sums[5 : 5 + wide].reshape(-1),
+        sums[9],
+        sums[10],
+        sums[11],
     )
 
 

time: 488 us -> 271 us (0.56)
  waiting for transfers between devices: 157 us -> 0 us
  Pallas kernels: 143 us -> 235 us
  matrix products: 65 us -> 0 us
  blocking collectives: 40.8 us -> 0 us
  local copies, waits for them, and re-layouts: 36.1 us -> 14.2 us
  between operations: 18.1 us -> 3.98 us
  other arithmetic: 22.7 us -> 17.1 us
    reduce_scatter x5 -> x0, waiting for transfers between devices: 145 us -> none  [the longest x4 124 us: one(): lax.psum_scatter(grad.astype(jnp.bfloat16), 'row', scatter_dimension=0, t...]
    pallas_call x1, Pallas kernels: 27.4 us -> 120 us  [backward(): pl.pallas_call(functools.partial(backward_kernel, chips, depth), out_shap...]
    dot_general x8 -> x0, matrix products: 65 us -> none  [the longest x4 33.1 us: dot_back(): lax.dot_general(left, right, (((1,), (1,)), ((), ())), preferred_element_...]
    psum x1 -> x0, blocking collectives: 40.8 us -> none  [per_device(): lax.psum((grad_bias_query, grad_bias_value, grad_bias_out, grad_gain_attn...]
    unnamed x44 -> x15, local copies, waits for them, and re-layouts: 20.8 us -> 4.66 us
    unnamed x11 -> x0, waiting for transfers between devices: 12.8 us -> none
    slice x3 -> x2, local copies, waits for them, and re-layouts: 6.06 us -> 0.67 us  [the longest x1 0.66 us: per_device(): sums[11]]
  transfers between devices with their start and end apart: 8 -> 0, of which waited for: 5 -> 0; matrix products, arithmetic and copies ran while one was open for 14% -> 0% of each run, Pallas kernels for 6% -> 0%
where the time goes in v3:
time: 271 us; the launch traced here: 270 us
  Pallas kernels  235 us (87%)
  other arithmetic  17.1 us (6%)
  local copies, waits for them, and re-layouts  14.2 us (5%)
  between operations  3.98 us (1%)
    pallas_call x1, Pallas kernels, backward(): pl.pallas_call(functools.partial(backward_kernel, chips, depth), out_shap...  120 us
    pallas_call x1, Pallas kernels, forward(): pl.pallas_call(functools.partial(forward_kernel, chips, depth), out_shape...  115 us
    concatenate x4, other arithmetic, roll_rows(): jnp.concatenate([field, field])  15.6 us
    another operation x9, local copies, waits for them, and re-layouts, per_device(): jnp.stack([bias_query, jnp.zeros_like(bias_query), bias_value, bias_out,...  5.52 us

profile of v3, /device:TPU:0, one launch (start us, length us, event | category | flops | bytes accessed | tf_op | source)
XLA Modules:
  0.0 270.4 jit_solution(9764006953795567013)
XLA Ops:
  0.7 0.9 compare_reduce_fusion
  1.6 0.7 iota_reduce_fusion
  5.5 0.7 stack.24
  6.2 0.7 stack.25
  6.8 0.7 stack.26
  7.5 0.7 stack.27
  8.2 0.7 stack.28
  8.9 0.7 stack.29
  9.6 0.7 stack.30
  10.3 0.7 stack.31
  11.0 0.8 constant_dynamic-slice_fusion
  11.7 0.7 fusion.4
  12.4 0.7 reshape.39
  13.1 1.3 concatenate.21.vecs
  14.4 1.7 copy.31.down_in
  16.1 6.0 %fusion.2 = (bf16[1024,768]{1,0:T(8,128)(2,1)}, bf16[1024,768]{1,0:T(8,128)(2,1)}) fusion(s32[]{:T(128)S(6)} %select_n.24, bf16[1024,768]{1,0:T(8,128)(2,1)} %param.31, bf16[1024,768]{1,0:T(8,128)(2,1)} %param.16), kind=kLoop, calls=%fused_computation.10 | loop fusion | flops 6291456 | bytes 6291460 | tf_op jit(solution)/shard_map/concatenate | solution.py:945
  22.1 114.9 %forward.1 = (bf16[1024,768]{1,0:T(8,128)(2,1)}, f32[1024,768]{1,0:T(8,128)}, bf16[1024,768]{1,0:T(8,128)(2,1)}, bf16[1024,2304]{1,0:T(8,128)(2,1)}, bf16[1024,7...) custom-call(bf16[1024,768]{1,0:T(8,128)(2,1)} %get-tuple-element.85., ...), custom_call_target="tpu_custom_call" | custom-call | tf_op jit(solution)/shard_map/forward/pallas_call | solution.py:446
  137.1 4.1 %fusion.1 = bf16[1024,768]{1,0:T(8,128)(2,1)} fusion(s32[]{:T(128)S(6)} %select_n.25, bf16[1024,768]{1,0:T(8,128)(2,1)} %get-tuple-element.39), kind=kLoop, calls=%fused_computation.9 | loop fusion | flops 3145728 | bytes 3145732 | tf_op jit(solution)/shard_map/concatenate | solution.py:945
  141.1 120.1 %backward.1 = (f32[1024,768]{1,0:T(8,128)}, f32[96,576]{1,0:T(8,128)}, f32[96,192]{1,0:T(8,128)}, f32[96,768]{1,0:T(8,128)}, f32[384,192]{1,0:T(8,128)}, /*index=5*/f32[16,768]{1,0:T(8,128)}) custom-call(bf16[1024,768]{1,0:T(8,128)(2,1)} %get-tuple-element.40.two_low_in, bf16[1024,3072]{1,0:T(8,128)(2,1)} %get-tuple-element.41.active_in, ...), custom_call_target="tpu_custom_call" | custom-call | tf_op jit(solution)/shard_map/backward/pallas_call | solution.py:923
  261.2 0.0 copy-start.4
  261.2 0.0 copy-start
  261.3 0.0 copy-start.2
  261.3 0.0 copy-start.3
  261.3 0.0 copy-start.1
  261.3 4.9 %fusion = f32[1024,768]{1,0:T(8,128)} fusion(s32[]{:T(128)S(6)} %select_n.25, f32[1024,768]{1,0:T(8,128)} %get-tuple-element.55), kind=kLoop, calls=%fused_computation.2 | loop fusion | flops 786432 | bytes 6291460 | tf_op jit(solution)/shard_map/concatenate | solution.py:945
  266.2 0.0 copy-done.4
  266.2 0.7 slice_reduce_fusion
  266.8 0.6 reshape.40
  267.4 0.0 copy-done
  267.5 0.9 copy.32
  268.3 0.0 copy-done.2
  268.3 0.7 copy.36
  269.0 0.0 copy-done.3
  269.0 0.6 copy.37
  269.7 0.0 copy-done.1
  269.7 0.7 copy.38
  (2 shorter events, 0.0 us)
Async XLA Ops:
  261.2 4.9 %copy-start.4 = (f32[16,768]{1,0:T(8,128)S(1)}, f32[16,768]{1,0:T(8,128)}, u32[]{:S(2)}) copy-start(f32[16,768]{1,0:T(8,128)} %get-tuple-element.60) | copy-start | bytes 147460
  261.2 6.2 %copy-start = (f32[384,192]{1,0:T(8,128)S(1)}, f32[384,192]{1,0:T(8,128)}, u32[]{:S(2)}) copy-start(f32[384,192]{1,0:T(8,128)} %get-tuple-element.66) | copy-start | bytes 884740
  261.3 7.1 %copy-start.2 = (f32[96,576]{1,0:T(8,128)S(1)}, f32[96,576]{1,0:T(8,128)}, u32[]{:S(2)}) copy-start(f32[96,576]{1,0:T(8,128)} %get-tuple-element.103) | copy-start | bytes 663556
  261.3 7.8 %copy-start.3 = (f32[96,192]{1,0:T(8,128)S(1)}, f32[96,192]{1,0:T(8,128)}, u32[]{:S(2)}) copy-start(f32[96,192]{1,0:T(8,128)} %get-tuple-element.104) | copy-start | bytes 221188
  261.3 8.4 %copy-start.1 = (f32[96,768]{1,0:T(8,128)S(1)}, f32[96,768]{1,0:T(8,128)}, u32[]{:S(2)}) copy-start(f32[96,768]{1,0:T(8,128)} %get-tuple-element.105) | copy-start | bytes 884740

commit v4 on v3

--- a/solution.py
+++ b/solution.py
@@ -247,13 +247,42 @@
     context[rows, cols[0]] = total.astype(jnp.bfloat16)
 
 
+def find_rows(p, segment, turn, seg_row, start_o):
+    own = jnp.broadcast_to(segment[pl.ds(p.row * p.depth + p.z, 1), :].astype(jnp.float32), (16, LEN))
+    lane = lax.broadcasted_iota(jnp.int32, (16, LEN), 1)
+    ahead = pltpu.roll(own, LEN - BLOCK + 1, 1)
+    found = (own == ahead) & (lane <= LEN - BLOCK)
+    start = jnp.min(jnp.where(found, lane.astype(jnp.float32), 2.0 * LEN), axis=1, keepdims=True)
+    start_o[...] = jnp.broadcast_to(start[:8].astype(jnp.int32), start_o.shape)
+
+    def step(i, _):
+        at = pl.ds(pl.multiple_of(i * CHUNK, CHUNK), CHUNK)
+        apart = lax.broadcasted_iota(jnp.int32, (CHUNK, LEN), 1) - lax.broadcasted_iota(jnp.int32, (CHUNK, LEN), 0) - i * CHUNK
+        apart = apart.astype(jnp.float32) - start[0:1, 0:1]
+        turn[at, 0:LEN] = jnp.where((apart == 0.0) | (apart == -1.0 * LEN), 1.0, 0.0).astype(jnp.bfloat16)
+        return 0
+
+    lax.fori_loop(0, LEN // CHUNK, step, 0)
+    seg_row[...] = contract(own.astype(jnp.bfloat16), turn[:, 0:LEN], 1, 1)
+
+
+def turn_rows(turn, source, result):
+    def step(i, _):
+        at = pl.ds(pl.multiple_of(i * CHUNK, CHUNK), CHUNK)
+        result[at, :] = contract(turn[at, 0:LEN], source[...], 1, 0).astype(jnp.bfloat16)
+        return 0
+
+    lax.fori_loop(0, LEN // CHUNK, step, 0)
+
+
 def forward_kernel(
     chips, depth,
-    tokens_in, cot_in, qkv_in, out_in, up_in, down_in, seg_row, vecs,
+    tokens_in, cot_in, qkv_in, out_in, up_in, down_in, segment,
+    bias_query, bias_value, bias_out, gain_attn, shift_attn, bias_down, gain_ffn, shift_ffn, bias_up,
     output_o, two_o, two_low_o, qkv_o, context_o, normed_o, hidden_low_o, active_o, slope_o,
-    wqkv_o, wout_o, wup_o, wdown_o, logsum, factor, sums,
+    wqkv_o, wout_o, wup_o, wdown_o, tokens_o, logsum, factor, sums, seg_row, vecs, start_o,
     tokens, cot, s_qkv, s_out, s_up, s_down, w_qkv, w_out, w_up, w_down,
-    qkv, context, bias, hidden, hidden_low, normed, active, slope, two_low, output,
+    qkv, context, bias, hidden, hidden_low, normed, active, slope, two_low, output, down_flat,
     load, store, z_send, z_recv, ring_sent, ring_recv, core_sent, core_recv,
 ):
     p = Place(chips, depth)
@@ -262,7 +291,7 @@
     loads = [
         pltpu.make_async_copy(src, dst, load.at[i])
         for i, (src, dst) in enumerate(
-            ((qkv_in, s_qkv.at[p.z]), (out_in, s_out.at[p.z]), (up_in, s_up.at[p.z]), (down_in, s_down.at[p.z]), (tokens_in, tokens), (cot_in, cot))
+            ((qkv_in, s_qkv.at[p.z]), (out_in, s_out.at[p.z]), (up_in, s_up.at[p.z]), (down_in, down_flat), (tokens_in, two_low), (cot_in, output))
         )
     ]
     for item in loads:
@@ -280,21 +309,33 @@
         stores.append(copy)
 
     p.meet()
-    for item, gather in zip(loads, (g_qkv, g_out, g_up, g_down)):
-        item.wait()
-        gather.open()
+    loads[0].wait()
+    g_qkv.open()
+    find_rows(p, segment, active, seg_row, start_o)
+    loads[4].wait()
+    turn_rows(active, two_low, tokens)
+    put(tokens, tokens_o)
+    for i in (1, 2, 3, 5):
+        loads[i].wait()
     g_qkv.relay()
     g_qkv.start_ring()
+    g_out.open()
+    g_up.open()
+    s_down[p.z] = down_flat[...].astype(jnp.float32).T.astype(jnp.bfloat16)
+    turn_rows(active, output, cot)
+    for i, vector in enumerate((bias_query, None, bias_value, bias_out, gain_attn, shift_attn, bias_down, gain_ffn, shift_ffn)):
+        vecs[i : i + 1, :] = jnp.zeros((1, model), jnp.float32) if vector is None else vector[...].reshape(1, model)
+    for i in range(active.shape[1] // model):
+        vecs[9 + i : 10 + i, :] = bias_up[i * model : (i + 1) * model].reshape(1, model)
+    fill_bias(seg_row, bias)
     g_out.relay()
-    fill_bias(seg_row, bias)
     for hop in range(1, p.hops):
         g_qkv.advance(hop)
+    g_down.open()
     g_out.start_ring()
     g_up.relay()
+    g_up.start_ring()
     g_qkv.advance(p.hops)
-    g_up.start_ring()
-    loads[4].wait()
-    loads[5].wait()
     for hop in range(p.hops + 1):
         g_qkv.mate_has(hop)
     put(w_qkv, wqkv_o)
@@ -305,24 +346,36 @@
         got = contract(tokens[at, :], w_qkv[:, cols], 1, 0) + vecs[pl.ds(tile, 1), :]
         got = got * jnp.where(tile == 0, HEAD_DIM ** (-0.5), 1.0)
         qkv[at, cols] = got.astype(jnp.bfloat16)
+
+        @pl.when(step == 2 * (rows // CHUNK))
+        def _():
+            for hop in range(1, p.hops):
+                g_out.advance(hop)
+
         return 0
 
     lax.fori_loop(0, 3 * (rows // CHUNK), project, 0)
     put(qkv, qkv_o)
-    for hop in range(1, p.hops):
-        g_out.advance(hop)
 
     def attend_first(pair, _):
         attend_pair(qkv, bias, context, logsum, model, 0, pair)
+
+        @pl.when(pair == 0)
+        def _():
+            g_out.advance(p.hops)
+
+        @pl.when(pair == pairs - 1)
+        def _():
+            g_down.relay()
+
         return 0
 
     lax.fori_loop(0, pairs, attend_first, 0)
-    g_down.relay()
 
     def attend_second(pair, _):
         attend_pair(qkv, bias, context, logsum, model, 1, pair)
 
-        @pl.when(pair == pairs // 2 - 1)
+        @pl.when(pair == 1)
         def _():
             for hop in range(1, p.hops):
                 g_up.advance(hop)
@@ -331,7 +384,6 @@
         return 0
 
     lax.fori_loop(0, pairs, attend_second, 0)
-    g_out.advance(p.hops)
     put(context, context_o)
     for hop in range(p.hops + 1):
         g_out.mate_has(hop)
@@ -428,7 +480,7 @@
         copy.wait()
 
 
-def forward(chips, depth, tokens, cotangent, w_qkv, w_out, w_up, w_down, seg_row, vecs):
+def forward(chips, depth, tokens, cotangent, w_qkv, w_out, w_up, w_down, segment, vectors):
     rows, model = tokens.shape
     low, full = jnp.bfloat16, jnp.float32
     weights = (w_qkv, w_out, w_up, w_down)
@@ -440,14 +492,15 @@
         shape((rows, 3 * model), low), shape((rows, model), low), shape((rows, model), low),
         shape((rows, model), low), shape((rows, wide), low), shape((rows, wide), low),
         *(shape(size, low) for size in whole),
-        shape((HEADS, rows), full), shape((rows, 128), full), shape((8, model), full),
+        shape((rows, model), low), shape((HEADS, rows), full), shape((rows, 128), full), shape((8, model), full),
+        shape((16, rows), full), shape((16, model), full), shape((8, 128), jnp.int32),
     ]
     hops = chips // 2
     return pl.pallas_call(
         functools.partial(forward_kernel, chips, depth),
         out_shape=outs,
-        in_specs=[ANY] * 6 + [VMEM] * 2,
-        out_specs=[ANY] * 13 + [VMEM] * 3,
+        in_specs=[ANY] * 6 + [VMEM] * (1 + len(vectors)),
+        out_specs=[ANY] * 14 + [VMEM] * 6,
         scratch_shapes=[
             pltpu.VMEM((rows, model), low), pltpu.VMEM((rows, model), low),
             *(pltpu.VMEM((depth, *w.shape), low) for w in weights),
@@ -455,15 +508,15 @@
             pltpu.VMEM((rows, 3 * model), low), pltpu.VMEM((rows, model), low), pltpu.VMEM((BLOCK, BLOCK), full),
             pltpu.VMEM((rows, model), full), pltpu.VMEM((rows, model), low), pltpu.VMEM((rows, model), low),
             pltpu.VMEM((rows, wide), low), pltpu.VMEM((rows, wide), low),
-            pltpu.VMEM((rows, model), low), pltpu.VMEM((rows, model), low),
-            pltpu.SemaphoreType.DMA((6,)), pltpu.SemaphoreType.DMA((13,)),
+            pltpu.VMEM((rows, model), low), pltpu.VMEM((rows, model), low), pltpu.VMEM(w_down.shape[::-1], low),
+            pltpu.SemaphoreType.DMA((6,)), pltpu.SemaphoreType.DMA((14,)),
             pltpu.SemaphoreType.DMA((4, 2, depth)), pltpu.SemaphoreType.DMA((4, depth)),
             pltpu.SemaphoreType.DMA((4, 2, hops)), pltpu.SemaphoreType.DMA((4, 2, hops)),
             pltpu.SemaphoreType.DMA((4, 2 * hops + 1)), pltpu.SemaphoreType.DMA((4, 2 * hops + 1)),
         ],
         compiler_params=pltpu.CompilerParams(collective_id=0, has_side_effects=True, vmem_limit_bytes=67043328),
         name="forward",
-    )(tokens, cotangent, *weights, seg_row, vecs)
+    )(tokens, cotangent, w_qkv, w_out, w_up, w_down.T, segment, *vectors)
 
 
 VMEM = pl.BlockSpec(memory_space=pltpu.VMEM)
@@ -941,8 +994,98 @@
     )(*ins, *vmem_ins)
 
 
-def roll_rows(field, start):
-    return lax.dynamic_slice_in_dim(jnp.concatenate([field, field]), start, field.shape[0], 0)
+def finish_kernel(
+    start_in, output_in, tokens_in, qkv_in, out_in, up_in, down_in, sums,
+    output_o, tokens_o, qkv_o, out_o, up_o, down_o, *rest,
+):
+    vectors, (low, wide, grad, done_low, done, qkv, out, up, down, load, store) = rest[:9], rest[9:]
+    rows, model = low.shape
+    loads = [
+        pltpu.make_async_copy(src, dst, load.at[i])
+        for i, (src, dst) in enumerate(
+            ((output_in, low), (tokens_in, grad.at[pl.ds(0, rows), :]), (tokens_in.at[pl.ds(0, 32), :], grad.at[pl.ds(rows, 32), :]), (qkv_in, qkv), (out_in, out), (up_in, up), (down_in, down))
+        )
+    ]
+    for item in loads:
+        item.start()
+    stores = []
+
+    def put(src, dst):
+        copy = pltpu.make_async_copy(src, dst, store.at[len(stores)])
+        copy.start()
+        stores.append(copy)
+
+    for i, vector in enumerate(vectors):
+        row = i if i < 6 else i + 3
+        for j in range(vector.shape[0] // model):
+            vector[j * model : (j + 1) * model] = sums[row + j : row + j + 1, :].reshape(model)
+    start = start_in[0, 0]
+    loads[0].wait()
+
+    def widen(i, _):
+        at = pl.ds(pl.multiple_of(i * 64, 64), 64)
+        wide[at, :] = low[at, :].astype(jnp.float32)
+        return 0
+
+    lax.fori_loop(0, rows // 64, widen, 0)
+    wide[rows:, :] = wide[0:32, :]
+
+    over = lax.rem(rows - start, 8)
+    early = lax.broadcasted_iota(jnp.int32, (8, model), 0) < 8 - over
+
+    def turn(source, result, i):
+        for j in range(2):
+            at = i * 64 + j * 32
+            came = pl.multiple_of(lax.rem(at + rows - start - over, rows), 8)
+            field = source[pl.ds(came, 40), :]
+            parts = [pltpu.roll(field[8 * k : 8 * k + 8], lax.rem(8 - over, 8), 0) for k in range(5)]
+            whole = jnp.concatenate([jnp.where(early, parts[k], parts[k + 1]) for k in range(4)])
+            result[pl.ds(pl.multiple_of(at, 32), 32), :] = whole.astype(result.dtype)
+
+    for source, result, dst, waits in ((wide, done_low, output_o, ()), (grad, done, tokens_o, (1, 2))):
+        for i in waits:
+            loads[i].wait()
+        for part in range(4):
+            deep = rows // 4
+
+            def step(i, _, source=source, result=result):
+                turn(source, result, i)
+                return 0
+
+            lax.fori_loop(part * (deep // 64), (part + 1) * (deep // 64), step, 0)
+            at = pl.ds(part * deep, deep)
+            put(result.at[at, :], dst.at[at, :])
+        if not waits:
+            for i, (src, dst) in enumerate(((qkv, qkv_o), (out, out_o), (up, up_o))):
+                loads[3 + i].wait()
+                put(src, dst)
+    loads[6].wait()
+    down_o[...] = down[...].T
+    for copy in stores:
+        copy.wait()
+
+
+def finish(start, output, grad_tokens, grads, sums, wide):
+    rows, model = output.shape
+    low, full = jnp.bfloat16, jnp.float32
+    shape = jax.ShapeDtypeStruct
+    flipped = grads[3].shape[::-1]
+    return pl.pallas_call(
+        finish_kernel,
+        out_shape=[
+            shape((rows, model), low), shape((rows, model), full), *(shape(g.shape, full) for g in grads[:3]), shape(flipped, full),
+            *(shape((model,), full) for _ in range(5)), shape((wide,), full), *(shape((model,), full) for _ in range(3)),
+        ],
+        in_specs=[pl.BlockSpec(memory_space=pltpu.SMEM)] + [ANY] * 6 + [VMEM],
+        out_specs=[ANY] * 5 + [VMEM] * 10,
+        scratch_shapes=[
+            pltpu.VMEM((rows, model), low), pltpu.VMEM((rows + 32, model), full), pltpu.VMEM((rows + 32, model), full),
+            pltpu.VMEM((rows, model), low), pltpu.VMEM((rows, model), full), *(pltpu.VMEM(g.shape, full) for g in grads),
+            pltpu.SemaphoreType.DMA((7,)), pltpu.SemaphoreType.DMA((11,)),
+        ],
+        compiler_params=pltpu.CompilerParams(vmem_limit_bytes=67043328),
+        name="finish",
+    )(start, output, grad_tokens, *grads, sums)
 
 
 def per_device(
@@ -963,54 +1106,25 @@
     shift_ffn,
     cotangent,
 ):
-    model = tokens.shape[1]
-    tok_rows = tokens.shape[0]
-    device_at = lax.axis_index("row") * lax.axis_size("col") + lax.axis_index("col")
-    segrow = lax.dynamic_index_in_dim(segment, device_at * tok_rows // LEN, 0, keepdims=False)
-    start = jnp.argmax(segrow[: LEN - BLOCK + 1] == segrow[BLOCK - 1 :]).astype(jnp.int32)
-    back = (LEN - start).astype(jnp.int32)
-    segrow = roll_rows(segrow, start)
-    tokens = roll_rows(tokens, start)
-    cotangent = roll_rows(cotangent, start)
-    seg_row = segrow[None, :]
-    vecs = jnp.concatenate(
-        [
-            jnp.stack([bias_query, jnp.zeros_like(bias_query), bias_value, bias_out, gain_attn, shift_attn, bias_down, gain_ffn, shift_ffn]),
-            bias_up.reshape(-1, model),
-        ]
-    )
     chips, depth = lax.axis_size("row") // 2, lax.axis_size("col")
     (
         output, grad_two, grad_two_low, projected, context, normed_one, hidden_low, active_low, slope,
-        attn_qkv, attn_out, ffn_up, ffn_down, logsum, factor_one, sums,
-    ) = forward(chips, depth, tokens, cotangent, w_qkv, w_out, w_up, w_down, seg_row, vecs)
-    grad_tokens, block_qkv, block_out, block_up, block_down, sums = backward(
+        attn_qkv, attn_out, ffn_up, ffn_down, turned, logsum, factor_one, sums, seg_row, vecs, start,
+    ) = forward(
+        chips, depth, tokens, cotangent, w_qkv, w_out, w_up, w_down, segment,
+        (bias_query, bias_value, bias_out, gain_attn, shift_attn, bias_down, gain_ffn, shift_ffn, bias_up),
+    )
+    grad_tokens, *grads, sums = backward(
         chips, depth,
         (w_qkv.shape, w_out.shape, w_up.shape, w_down.shape),
         (
             grad_two_low, active_low, ffn_down, slope, hidden_low, ffn_up, grad_two, normed_one, factor_one, attn_out, context,
-            projected, tokens, attn_qkv,
+            projected, turned, attn_qkv,
         ),
         (seg_row, vecs, logsum, sums),
     )
-    wide = bias_up.shape[0] // model
-    return (
-        roll_rows(output, back),
-        roll_rows(grad_tokens, back),
-        block_qkv,
-        block_out,
-        block_up,
-        block_down,
-        sums[0],
-        sums[1],
-        sums[2],
-        sums[3],
-        sums[4],
-        sums[5 : 5 + wide].reshape(-1),
-        sums[9],
-        sums[10],
-        sums[11],
-    )
+    done = finish(start, output, grad_tokens, grads, sums, bias_up.shape[0])
+    return (*done[:5], done[5].T, *done[6:])
 
 
 def solution(mesh):

time: 271 us -> 237 us (0.87)
  other arithmetic: 17.1 us -> 0 us
  local copies, waits for them, and re-layouts: 14.2 us -> 0 us
  between operations: 3.98 us -> 0.85 us
    concatenate x4 -> x0, other arithmetic: 15.6 us -> none  [roll_rows(): jnp.concatenate([field, field])]
    pallas_call x0 -> x1, Pallas kernels: none -> 6.65 us  [finish(): pl.pallas_call(finish_kernel, out_shape=[shape((rows, model), low), shape...]
    another operation x9 -> x0, local copies, waits for them, and re-layouts: 5.52 us -> none  [per_device(): jnp.stack([bias_query, jnp.zeros_like(bias_query), bias_value, bias_out,...]
    pallas_call x1, Pallas kernels: 115 us -> 110 us  [forward(): pl.pallas_call(functools.partial(forward_kernel, chips, depth), out_shape...]
    unnamed x15 -> x0, local copies, waits for them, and re-layouts: 4.66 us -> none
where the time goes in v4:
time: 237 us
  Pallas kernels  236 us (100%)
    pallas_call x1, Pallas kernels, backward(): pl.pallas_call(functools.partial(backward_kernel, chips, depth), out_shap...  120 us
    pallas_call x1, Pallas kernels, forward(): pl.pallas_call(functools.partial(forward_kernel, chips, depth), out_shape...  110 us
    pallas_call x1, Pallas kernels, finish(): pl.pallas_call(finish_kernel, out_shape=[shape((rows, model), low), shape...  6.65 us

profile of v4, /device:TPU:0, one launch (start us, length us, event | category | flops | bytes accessed | tf_op | source)
XLA Modules:
  0.0 237.2 jit_solution(9617422052693651374)
XLA Ops:
  0.7 109.9 %forward.1 = (bf16[1024,768]{1,0:T(8,128)(2,1)}, f32[1024,768]{1,0:T(8,128)}, bf16[1024,768]{1,0:T(8,128)(2,1)}, bf16[1024,2304]{1,0:T(8,128)(2,1)}, bf16[1024,7...) custom-call(bf16[1024,768]{1,0:T(8,128)(2,1)} %tokens_in.1, ...), custom_call_target="tpu_custom_call" | custom-call | tf_op jit(solution)/shard_map/forward/pallas_call | solution.py:499
  110.6 119.8 %backward.1 = (f32[1024,768]{1,0:T(8,128)}, f32[96,576]{1,0:T(8,128)}, f32[96,192]{1,0:T(8,128)}, f32[96,768]{1,0:T(8,128)}, f32[384,192]{1,0:T(8,128)}, /*index=5*/f32[16,768]{1,0:T(8,128)}) custom-call(bf16[1024,768]{1,0:T(8,128)(2,1)} %get-tuple-element.58.two_low_in, bf16[1024,3072]{1,0:T(8,128)(2,1)} %get-tuple-element.59.active_in, ...), custom_call_target="tpu_custom_call" | custom-call | tf_op jit(solution)/shard_map/backward/pallas_call | solution.py:976
  230.4 6.7 %finish.1 = (bf16[1024,768]{1,0:T(8,128)(2,1)}, f32[1024,768]{1,0:T(8,128)}, f32[96,576]{1,0:T(8,128)}, f32[96,192]{1,0:T(8,128)}, f32[96,768]{1,0:T(8,128)}, /*...) custom-call(s32[8,128]{1,0:T(8,128)} %get-tuple-element.56.start_in,, ...), custom_call_target="tpu_custom_call" | custom-call | tf_op jit(solution)/shard_map/finish/pallas_call | solution.py:1073

commit v5 on v4

--- a/solution.py
+++ b/solution.py
@@ -34,6 +34,13 @@
 MESH = pl.DeviceIdType.MESH
 ANY = pl.BlockSpec(memory_space=pl.ANY)
 CHUNK = 256
+EARLY = 512
+UP_AT = 6
+DOWN_AT = 12
+DT = 2
+FN = 0
+H_UP = 2
+H_OUT = 5
 
 
 class Place:
@@ -49,6 +56,10 @@
         far = pos // (self.chips // 2)
         return 2 * (pos + far * (self.chips - 1 - 2 * pos)) + far
 
+    def order(self):
+        apart = [self.hops] + [way * hop for hop in range(self.hops - 1, 0, -1) for way in (1, -1)] + [0]
+        return [self.chip_at(self.pos + hop) for hop in apart]
+
     def right(self):
         return (2 * self.chip_at(self.pos + 1) + self.core, self.z)
 
@@ -113,9 +124,9 @@
         def _():
             self.line(p.z, 1, 0).start()
 
-    def relay(self):
-        p = self.p
-        for step in range(1, p.depth):
+    def relay(self, part):
+        p = self.p
+        for step in (range(1, 2), range(2, p.depth - 1), range(max(2, p.depth - 1), p.depth))[part]:
 
             @pl.when(p.z - step >= 0)
             def _(step=step):
@@ -133,8 +144,9 @@
                 def _():
                     self.line(p.z + step, 1, step).start()
 
-        rows = pl.ds(pl.multiple_of(p.row * self.rows, self.rows), self.rows)
-        self.full[rows, :] = jnp.concatenate([self.staged[z] for z in range(p.depth)], axis=1)
+        if part == 2:
+            rows = pl.ds(pl.multiple_of(p.row * self.rows, self.rows), self.rows)
+            self.full[rows, :] = jnp.concatenate([self.staged[z] for z in range(p.depth)], axis=1)
 
     def line_sent(self):
         p = self.p
@@ -317,23 +329,29 @@
     put(tokens, tokens_o)
     for i in (1, 2, 3, 5):
         loads[i].wait()
-    g_qkv.relay()
-    g_qkv.start_ring()
+    s_down[p.z] = down_flat[...].astype(jnp.float32).T.astype(jnp.bfloat16)
+    g_qkv.relay(0)
+    g_qkv.relay(1)
     g_out.open()
     g_up.open()
-    s_down[p.z] = down_flat[...].astype(jnp.float32).T.astype(jnp.bfloat16)
-    turn_rows(active, output, cot)
+    g_qkv.relay(2)
+    g_qkv.start_ring()
+    for i in range(active.shape[1] // model):
+        vecs[9 + i : 10 + i, :] = bias_up[i * model : (i + 1) * model].reshape(1, model)
     for i, vector in enumerate((bias_query, None, bias_value, bias_out, gain_attn, shift_attn, bias_down, gain_ffn, shift_ffn)):
         vecs[i : i + 1, :] = jnp.zeros((1, model), jnp.float32) if vector is None else vector[...].reshape(1, model)
-    for i in range(active.shape[1] // model):
-        vecs[9 + i : 10 + i, :] = bias_up[i * model : (i + 1) * model].reshape(1, model)
+    g_out.relay(0)
+    g_up.relay(0)
     fill_bias(seg_row, bias)
-    g_out.relay()
+    g_out.relay(1)
+    g_up.relay(1)
+    g_down.open()
+    g_out.relay(2)
     for hop in range(1, p.hops):
         g_qkv.advance(hop)
-    g_down.open()
     g_out.start_ring()
-    g_up.relay()
+    turn_rows(active, output, cot)
+    g_up.relay(2)
     g_up.start_ring()
     g_qkv.advance(p.hops)
     for hop in range(p.hops + 1):
@@ -357,16 +375,25 @@
     lax.fori_loop(0, 3 * (rows // CHUNK), project, 0)
     put(qkv, qkv_o)
 
+    def up_next():
+        for hop in range(1, p.hops):
+            g_up.advance(hop)
+        g_down.start_ring()
+
     def attend_first(pair, _):
         attend_pair(qkv, bias, context, logsum, model, 0, pair)
 
-        @pl.when(pair == 0)
-        def _():
-            g_out.advance(p.hops)
-
-        @pl.when(pair == pairs - 1)
-        def _():
-            g_down.relay()
+        for part in range(3):
+
+            @pl.when(pair == part)
+            def _(part=part):
+                g_down.relay(part)
+
+        if UP_AT < pairs:
+
+            @pl.when(pair == UP_AT)
+            def _():
+                up_next()
 
         return 0
 
@@ -375,16 +402,17 @@
     def attend_second(pair, _):
         attend_pair(qkv, bias, context, logsum, model, 1, pair)
 
-        @pl.when(pair == 1)
-        def _():
-            for hop in range(1, p.hops):
-                g_up.advance(hop)
-            g_down.start_ring()
+        if UP_AT >= pairs:
+
+            @pl.when(pair == UP_AT - pairs)
+            def _():
+                up_next()
 
         return 0
 
     lax.fori_loop(0, pairs, attend_second, 0)
     put(context, context_o)
+    g_out.advance(p.hops)
     for hop in range(p.hops + 1):
         g_out.mate_has(hop)
     put(w_out, wout_o)
@@ -420,7 +448,7 @@
         active[at, cols] = act.astype(jnp.bfloat16)
         slope[at, cols] = grade.astype(jnp.bfloat16)
 
-        @pl.when(step == steps * 3 // 4)
+        @pl.when(step == steps * DOWN_AT // 16)
         def _():
             for hop in range(1, p.hops):
                 g_down.advance(hop)
@@ -444,9 +472,9 @@
 
     for hop in range(p.hops):
         g_down.mate_has(hop)
-        if hop == p.hops - 1:
-            g_down.advance(p.hops)
         for way in range(1 if hop == 0 else 2):
+            if hop == p.hops - 1 and way == 1:
+                g_down.advance(p.hops)
             narrow(p.chip_at(p.pos + hop if way else p.pos - hop))
     g_down.mate_has(p.hops)
     put(w_down, wdown_o)
@@ -523,30 +551,29 @@
 
 
 class Reduce:
-    def __init__(self, place, index, bufs, result, sems):
-        self.p, self.i, self.result = place, index, result
-        self.grad, self.other, self.halves, self.fulls, self.parts, self.came, self.total = bufs
+    def __init__(self, place, index, ring_bufs, line_bufs, result, sems, spans=None, last=True):
+        self.p, self.i, self.result, self.last = place, index, result, last
+        self.grad, self.other, self.halves, self.fulls = ring_bufs
+        self.parts, self.came, self.total = line_bufs
+        self.spans = spans or [(0, 0, self.grad.shape[3])]
         self.core_sent, self.core_recv, self.ring_sent, self.ring_recv, self.z_sent, self.z_recv, self.res_sem = sems
         self.half = self.grad.shape[3] // 2
 
-    def pair(self):
+    def pair(self, chip):
         return pltpu.make_async_remote_copy(
-            self.grad.at[:, 1 - self.p.core], self.other, self.core_sent.at[self.i], self.core_recv.at[self.i],
+            self.grad.at[chip, 1 - self.p.core], self.other.at[chip], self.core_sent.at[self.i, chip], self.core_recv.at[self.i, chip],
             device_id=self.p.mate(), device_id_type=MESH,
         )
 
     def swap(self):
-        self.pair().start()
-
-    def absorb(self):
-        self.pair().wait_recv()
-
-        def step(chip, _):
+        for chip in self.p.order():
+            self.pair(chip).start()
+
+    def absorb(self, chips):
+        for chip in chips:
+            self.pair(chip).wait_recv()
             both = self.grad[chip, self.p.core].astype(jnp.float32) + self.other[chip].astype(jnp.float32)
             self.grad[chip, self.p.core] = both.astype(jnp.bfloat16)
-            return 0
-
-        lax.fori_loop(0, self.p.chips, step, 0)
 
     def span(self, hop, way):
         return pl.ds((1 - way) * self.half, self.half) if hop == 1 else slice(None)
@@ -587,7 +614,10 @@
         ).astype(jnp.bfloat16)
         wide = self.parts.shape[2]
         for z in range(p.depth):
-            self.parts[z] = low[:, z * wide : (z + 1) * wide]
+            for at, real, count in self.spans:
+                left, right = max(real, z * wide), min(real + count, (z + 1) * wide)
+                if left < right:
+                    self.parts[z, :, left - z * wide : right - z * wide] = low[:, at + left - real : at + right - real]
 
     def line(self, block, way):
         return pltpu.make_async_remote_copy(
@@ -633,10 +663,13 @@
 
     def finish(self):
         p = self.p
-        self.pair().wait_send()
+        for chip in range(p.chips):
+            self.pair(chip).wait_send()
         for hop in range(1, p.hops + 1):
             for way in range(2):
                 self.ring(hop, way).wait_send()
+        if not self.last:
+            return
         for turn in range(p.depth - 1):
             for way in range(2):
                 far = p.depth - 1 - p.z if way else p.z
@@ -650,8 +683,11 @@
 
     def stages(self):
         def first():
-            self.absorb()
+            self.absorb(self.p.order()[:1])
             self.go(1)
+
+        def others():
+            self.absorb(self.p.order()[1:])
 
         def along(hop):
             self.take(hop)
@@ -659,11 +695,12 @@
 
         def begin():
             self.split()
-            self.round(0)
+            if self.last:
+                self.round(0)
 
         p = self.p
         return [
-            [first, *(functools.partial(along, hop) for hop in range(1, p.hops)), begin],
+            [first, others, *(functools.partial(along, hop) for hop in range(1, p.hops)), begin],
             [*(functools.partial(self.round, turn) for turn in range(1, p.depth - 1)), self.land],
         ]
 
@@ -741,18 +778,22 @@
     *rest,
 ):
     p = Place(chips, depth)
-    groups = [rest[7 * i : 7 * i + 7] for i in range(4)]
-    mine, other, plane, col = rest[28:32]
-    load, store, core_sent, core_recv, ring_sent, ring_recv, z_sent, z_recv, res_sem = rest[32:41]
-    sum_sems = rest[41:47]
+    rings = [rest[4 * i : 4 * i + 4] for i in range(5)]
+    lines = [rest[20 + 3 * i : 23 + 3 * i] for i in range(4)]
+    mine, other, plane, col = rest[32:36]
+    load, store, core_sent, core_recv, ring_sent, ring_recv, z_sent, z_recv, res_sem = rest[36:45]
+    sum_sems = rest[45:51]
     rows, model = two_low.shape
     wide = active.shape[1]
     count = wide // model
     pairs = HEADS // 2
     sems = (core_sent, core_recv, ring_sent, ring_recv, z_sent, z_recv, res_sem)
+    late = model - EARLY
     r_qkv, r_out, r_up, r_down = (
-        Reduce(p, i, bufs, result, sems) for i, (bufs, result) in enumerate(zip(groups, (qkv_o, out_o, up_o, down_o)))
+        Reduce(p, i, rings[i], lines[i], result, sems, [(t * late, t * model + EARLY, late) for t in range(3)] if i == 0 else None)
+        for i, result in enumerate((qkv_o, out_o, up_o, down_o))
     )
+    r_early = Reduce(p, 4, rings[4], lines[0], qkv_o, sems, [(t * EARLY, t * model, EARLY) for t in range(3)], False)
     used = []
 
     def fetch(src, dst):
@@ -765,7 +806,10 @@
         return ref.at[:, pl.ds(tile * model, model)]
 
     got_two_low = fetch(two_low_in, two_low)
-    got_active = [fetch(col_tile(active_in, t), col_tile(active, t)) for t in range(count)]
+    order = p.order()
+    deep = wide // p.chips
+    spans = [pl.ds(pl.multiple_of(chip * deep, 128), deep) for chip in order]
+    got_active = [fetch(active_in.at[:, span], active.at[:, span]) for span in spans]
     got_down = [fetch(wdown_in.at[pl.ds(t * model, model), :], tiles.at[t]) for t in range(count)]
     got_slope = [fetch(col_tile(slope_in, t), col_tile(slope, t)) for t in range(count)]
     got_rest = [
@@ -774,25 +818,29 @@
     ]
     p.meet_all()
 
-    def weight_grad(reduce, left, right, left_at, tile, skip=0):
+    def weight_grad(reduce, left, right, left_at, tile, skip=0, start=0, width=model):
         piece = 384
-        cols = pl.ds(pl.multiple_of(tile * model, model), model)
+        cols = pl.ds(pl.multiple_of(tile * model + start, 128), width)
         got = contract(left[:, pl.ds(pl.multiple_of(skip + left_at * piece, 128), piece)], right[:, cols], 0, 0)
         high = reduce.grad.shape[2]
+        cols = pl.ds(pl.multiple_of(tile * width, 128), width)
         for s in range(piece // high):
             row = left_at * (piece // high) + s
             reduce.grad[row // 2, row % 2, :, cols] = got[s * high : (s + 1) * high].astype(jnp.bfloat16)
 
     got_two_low.wait()
-    for t in range(count):
-        got_active[t].wait()
-
-        def down_grad(step, _, t=t):
-            weight_grad(r_down, active, two_low, t * (model // 384) + step, 0)
+    down_one, down_two = r_down.stages()
+    for n, chip in enumerate(order):
+        got_active[n].wait()
+
+        def down_grad(step, _, chip=chip):
+            weight_grad(r_down, active, two_low, chip * (deep // 384) + step, 0)
             return 0
 
-        lax.fori_loop(0, model // 384, down_grad, 0)
-    r_down.swap()
+        lax.fori_loop(0, deep // 384, down_grad, 0)
+        r_down.pair(chip).start()
+        if n == 1:
+            down_one[0]()
     got_qkv = fetch(qkv_in, active.at[:, pl.ds(0, 3 * model)])
     sums[...] = jnp.zeros_like(sums)
     sums[9:10, :] = sums_in[2:3, :]
@@ -812,8 +860,11 @@
 
         lax.fori_loop(0, rows // CHUNK, upward_grad, 0)
         got_up.append(fetch(col_tile(wup_in, t), tiles.at[t]))
-    down_one, down_two = r_down.stages()
-    down_one[0]()
+        if t == 0:
+            down_one[1]()
+        if t == DT:
+            for stage in down_one[2:-1]:
+                stage()
     got_rest[0].wait()
 
     def up_grad(step, _):
@@ -823,8 +874,6 @@
     lax.fori_loop(0, count * (model // 384), up_grad, 0)
     r_up.swap()
     got_tokens = fetch(tokens_in, hidden_low)
-    for stage in down_one[1:-1]:
-        stage()
     for item in got_rest[1:] + got_up:
         item.wait()
 
@@ -843,14 +892,20 @@
         sums[3:4, :] += jnp.sum(whole * unit, axis=0, keepdims=True)
         sums[4:5, :] += jnp.sum(whole, axis=0, keepdims=True)
         active[at, pl.ds(3 * model, model)] = contract(low, w_out[...], 1, 1).astype(jnp.bfloat16)
+
+        @pl.when(step == FN)
+        def _():
+            r_up.stages()[0][0]()
+
+        @pl.when(step == rows // CHUNK - 1)
+        def _():
+            r_up.stages()[0][1]()
+
         return 0
 
     lax.fori_loop(0, rows // CHUNK, first_norm, 0)
     got_context = fetch(context_in, slope.at[:, pl.ds(3 * model, model)])
     got_wqkv = [fetch(col_tile(wqkv_in, t), tiles.at[t]) for t in range(3)]
-    up_one, up_two = r_up.stages()
-    up_one[0]()
-
     got_context.wait()
 
     def out_grad(step, _):
@@ -886,43 +941,58 @@
         sums[0:1, cols[0]] += jnp.sum(sum_q, axis=0, keepdims=True)
         sums[1:2, cols[0]] += jnp.sum(sum_v, axis=0, keepdims=True)
 
+    early_one = r_early.stages()[0]
+    qkv_one, qkv_two = r_qkv.stages()
+    up_one, up_two = r_up.stages()
     hooks = {
-        (0, 0): [out_one[0]],
-        (0, 1): [down_one[-1]],
+        (0, 0): out_one[:2],
+        (0, 1): down_one[-1:],
+        (H_UP // 2, H_UP % 2): up_one[2:-1],
         (1, 1): down_two[:1],
-        (2, 0): up_one[1:-1],
-        (2, 1): down_two[1:-1],
-        (3, 0): out_one[1:-1],
+        (2, 0): down_two[1:-1],
+        (H_OUT // 2, H_OUT % 2): out_one[2:-1],
         (3, 1): down_two[-1:],
+        (4, 0): early_one[:2],
+        (4, 1): up_one[-1:],
+        (5, 0): [*early_one[2:-1], *out_one[-1:]],
+        (5, 1): up_two[:1],
     }
 
-    def attend_back(pair, _):
-        for block in range(2):
-            pair_back(pair, block)
-            for (when, part), todo in hooks.items():
-                if part == block:
-
-                    @pl.when(pair == when)
-                    def _(todo=todo):
-                        for stage in todo:
-                            stage()
-
-        return 0
-
-    lax.fori_loop(0, pairs, attend_back, 0)
+    def attend_back(first, stop):
+        def step(pair, _):
+            for block in range(2):
+                pair_back(pair, block)
+                for (when, part), todo in hooks.items():
+                    if part == block and first <= when < stop:
+
+                        @pl.when(pair == when)
+                        def _(todo=todo):
+                            for stage in todo:
+                                stage()
+
+            return 0
+
+        lax.fori_loop(first, stop, step, 0)
+
+    def early_grad(step, _):
+        weight_grad(r_early, hidden_low, slope, step // 3, step % 3, 0, 0, EARLY)
+        return 0
+
+    def late_grad(step, _):
+        weight_grad(r_qkv, hidden_low, slope, step // 3, step % 3, 0, EARLY, late)
+        return 0
+
+    attend_back(0, EARLY // 128)
     got_tokens.wait()
-    for item in got_wqkv:
-        item.wait()
-
-    def qkv_grad(step, _):
-        weight_grad(r_qkv, hidden_low, slope, step // 3, step % 3)
-        return 0
-
-    lax.fori_loop(0, 3 * (model // 384), qkv_grad, 0)
+    lax.fori_loop(0, 3 * (model // 384), early_grad, 0)
+    r_early.swap()
+    attend_back(EARLY // 128, pairs)
+    lax.fori_loop(0, 3 * (model // 384), late_grad, 0)
     r_qkv.swap()
     small = Sums(p, sums, mine, other, plane, col, sum_sems)
     small.start()
-    up_one[-1]()
+    for item in got_wqkv:
+        item.wait()
 
     def token_grad(step, _):
         at = pl.ds(pl.multiple_of(step * CHUNK, CHUNK), CHUNK)
@@ -932,28 +1002,31 @@
         acc[at, :] = whole
         return 0
 
-    half = rows // CHUNK // 2
+    half = rows // CHUNK // 4
     lax.fori_loop(0, half, token_grad, 0)
-    qkv_one, qkv_two = r_qkv.stages()
     qkv_one[0]()
+    qkv_one[1]()
     small.across()
-    out_one[-1]()
-    lax.fori_loop(half, rows // CHUNK, token_grad, 0)
+    for stage in out_two[:1] + up_two[1:-1]:
+        stage()
+    lax.fori_loop(half, 2 * half, token_grad, 0)
+    for stage in qkv_one[2:-1]:
+        stage()
+    early_one[-1]()
+    small.along()
+    lax.fori_loop(2 * half, rows // CHUNK, token_grad, 0)
     tokens_out = pltpu.make_async_copy(acc, tokens_o, store.at[0])
     tokens_out.start()
-    small.along()
-    up_two[0]()
-    for stage in qkv_one[1:-1]:
-        stage()
-    out_two[0]()
-    small.land(sums_o)
-    for stage in up_two[1:] + out_two[1:]:
+    for stage in out_two[1:-1]:
         stage()
     qkv_one[-1]()
+    up_two[-1]()
+    out_two[-1]()
+    small.land(sums_o)
     for stage in qkv_two:
         stage()
     small.finish()
-    for reduce in (r_down, r_up, r_out, r_qkv):
+    for reduce in (r_down, r_up, r_out, r_early, r_qkv):
         reduce.finish()
     tokens_out.wait()
 
@@ -965,14 +1038,14 @@
     low, full = jnp.bfloat16, jnp.float32
     shape, dma = jax.ShapeDtypeStruct, pltpu.SemaphoreType.DMA
     bufs = []
-    for high, across in blocks:
-        whole = depth * across
+    early = 3 * EARLY
+    for high, whole in [(high, depth * across - (0 if i else early)) for i, (high, across) in enumerate(blocks)] + [(blocks[0][0], early)]:
         bufs += [
             pltpu.VMEM((chips, 2, high, whole), low), pltpu.VMEM((chips, high, whole), low),
             pltpu.VMEM((2, high, whole // 2), low), pltpu.VMEM((2, hops - 1, high, whole), low),
-            pltpu.VMEM((depth, high, across), low), pltpu.VMEM((depth + 1, high, across), low),
-            pltpu.VMEM((high, across), full),
         ]
+    for high, across in blocks:
+        bufs += [pltpu.VMEM((depth, high, across), low), pltpu.VMEM((depth + 1, high, across), low), pltpu.VMEM((high, across), full)]
     return pl.pallas_call(
         functools.partial(backward_kernel, chips, depth),
         out_shape=[shape((rows, model), full), *(shape(size, full) for size in blocks), shape((16, model), full)],
@@ -986,7 +1059,7 @@
             *bufs,
             pltpu.VMEM((16, model), full), pltpu.VMEM((16, model), full),
             pltpu.VMEM((chips, 16, model), full), pltpu.VMEM((depth, 16, model), full),
-            dma((32,)), dma((1,)), dma((4,)), dma((4,)), dma((4, 2, hops)), dma((4, 2, hops)), dma((4, 2, depth)), dma((4, 2, depth)), dma((4,)),
+            dma((32,)), dma((1,)), dma((5, chips)), dma((5, chips)), dma((5, 2, hops)), dma((5, 2, hops)), dma((4, 2, depth)), dma((4, 2, depth)), dma((4,)),
             dma, dma, dma((chips,)), dma((chips,)), dma((depth,)), dma((depth,)),
         ],
         compiler_params=pltpu.CompilerParams(collective_id=1, has_side_effects=True, vmem_limit_bytes=67043328),
@@ -995,15 +1068,16 @@
 
 
 def finish_kernel(
-    start_in, output_in, tokens_in, qkv_in, out_in, up_in, down_in, sums,
+    start_in, output_in, tokens_in, qkv_in, out_in, up_in, down_in, sums_in,
     output_o, tokens_o, qkv_o, out_o, up_o, down_o, *rest,
 ):
-    vectors, (low, wide, grad, done_low, done, qkv, out, up, down, load, store) = rest[:9], rest[9:]
+    vectors, lines = rest[:9], rest[9:18]
+    low, wide, grad, done_low, done, qkv, out, up, down, flipped, sums, load, store = rest[18:]
     rows, model = low.shape
     loads = [
         pltpu.make_async_copy(src, dst, load.at[i])
         for i, (src, dst) in enumerate(
-            ((output_in, low), (tokens_in, grad.at[pl.ds(0, rows), :]), (tokens_in.at[pl.ds(0, 32), :], grad.at[pl.ds(rows, 32), :]), (qkv_in, qkv), (out_in, out), (up_in, up), (down_in, down))
+            ((output_in, low), (tokens_in, grad.at[pl.ds(0, rows), :]), (tokens_in.at[pl.ds(0, 32), :], grad.at[pl.ds(rows, 32), :]), (qkv_in, qkv), (out_in, out), (up_in, up), (down_in, down), (sums_in, sums))
         )
     ]
     for item in loads:
@@ -1015,10 +1089,6 @@
         copy.start()
         stores.append(copy)
 
-    for i, vector in enumerate(vectors):
-        row = i if i < 6 else i + 3
-        for j in range(vector.shape[0] // model):
-            vector[j * model : (j + 1) * model] = sums[row + j : row + j + 1, :].reshape(model)
     start = start_in[0, 0]
     loads[0].wait()
 
@@ -1059,8 +1129,15 @@
             for i, (src, dst) in enumerate(((qkv, qkv_o), (out, out_o), (up, up_o))):
                 loads[3 + i].wait()
                 put(src, dst)
-    loads[6].wait()
-    down_o[...] = down[...].T
+            loads[6].wait()
+            flipped[...] = down[...].T
+            put(flipped, down_o)
+            loads[7].wait()
+            for i, (line, vector) in enumerate(zip(lines, vectors)):
+                row = i if i < 6 else i + 3
+                for j in range(vector.shape[0] // model):
+                    line[j * model : (j + 1) * model] = sums[row + j : row + j + 1, :].reshape(model)
+                put(line, vector)
     for copy in stores:
         copy.wait()
 
@@ -1076,12 +1153,13 @@
             shape((rows, model), low), shape((rows, model), full), *(shape(g.shape, full) for g in grads[:3]), shape(flipped, full),
             *(shape((model,), full) for _ in range(5)), shape((wide,), full), *(shape((model,), full) for _ in range(3)),
         ],
-        in_specs=[pl.BlockSpec(memory_space=pltpu.SMEM)] + [ANY] * 6 + [VMEM],
-        out_specs=[ANY] * 5 + [VMEM] * 10,
+        in_specs=[pl.BlockSpec(memory_space=pltpu.SMEM)] + [ANY] * 7,
+        out_specs=[ANY] * 15,
         scratch_shapes=[
+            *(pltpu.VMEM((wide if i == 5 else model,), full) for i in range(9)),
             pltpu.VMEM((rows, model), low), pltpu.VMEM((rows + 32, model), full), pltpu.VMEM((rows + 32, model), full),
             pltpu.VMEM((rows, model), low), pltpu.VMEM((rows, model), full), *(pltpu.VMEM(g.shape, full) for g in grads),
-            pltpu.SemaphoreType.DMA((7,)), pltpu.SemaphoreType.DMA((11,)),
+            pltpu.VMEM(flipped, full), pltpu.VMEM(sums.shape, full), pltpu.SemaphoreType.DMA((8,)), pltpu.SemaphoreType.DMA((21,)),
         ],
         compiler_params=pltpu.CompilerParams(vmem_limit_bytes=67043328),
         name="finish",

time: 237 us -> 219 us (0.924)
  Pallas kernels: 236 us -> 218 us
    pallas_call x1, Pallas kernels: 120 us -> 107 us  [backward(): pl.pallas_call(functools.partial(backward_kernel, chips, depth), out_shap...]
    pallas_call x1, Pallas kernels: 110 us -> 105 us  [forward(): pl.pallas_call(functools.partial(forward_kernel, chips, depth), out_shape...]
where the time goes in v5:
time: 219 us; the launch traced here: 218 us
  Pallas kernels  218 us (100%)
    pallas_call x1, Pallas kernels, backward(): pl.pallas_call(functools.partial(backward_kernel, chips, depth), out_shap...  107 us
    pallas_call x1, Pallas kernels, forward(): pl.pallas_call(functools.partial(forward_kernel, chips, depth), out_shape...  105 us
    pallas_call x1, Pallas kernels, finish(): pl.pallas_call(finish_kernel, out_shape=[shape((rows, model), low), shape...  5.98 us

profile of v5, /device:TPU:0, one launch (start us, length us, event | category | flops | bytes accessed | tf_op | source)
XLA Modules:
  0.0 218.4 jit_solution(4479518517807784858)
XLA Ops:
  0.7 104.8 %forward.1 = (bf16[1024,768]{1,0:T(8,128)(2,1)}, f32[1024,768]{1,0:T(8,128)}, bf16[1024,768]{1,0:T(8,128)(2,1)}, bf16[1024,2304]{1,0:T(8,128)(2,1)}, bf16[1024,7...) custom-call(bf16[1024,768]{1,0:T(8,128)(2,1)} %tokens_in.1, ...), custom_call_target="tpu_custom_call" | custom-call | tf_op jit(solution)/shard_map/forward/pallas_call | solution.py:527
  105.5 106.7 %backward.1 = (f32[1024,768]{1,0:T(8,128)}, f32[96,576]{1,0:T(8,128)}, f32[96,192]{1,0:T(8,128)}, f32[96,768]{1,0:T(8,128)}, f32[384,192]{1,0:T(8,128)}, /*index=5*/f32[16,768]{1,0:T(8,128)}) custom-call(bf16[1024,768]{1,0:T(8,128)(2,1)} %get-tuple-element.58.two_low_in, bf16[1024,3072]{1,0:T(8,128)(2,1)} %get-tuple-element.59.active_in, ...), custom_call_target="tpu_custom_call" | custom-call | tf_op jit(solution)/shard_map/backward/pallas_call | solution.py:1049
  212.2 6.0 %finish.1 = (bf16[1024,768]{1,0:T(8,128)(2,1)}, f32[1024,768]{1,0:T(8,128)}, f32[96,576]{1,0:T(8,128)}, f32[96,192]{1,0:T(8,128)}, f32[96,768]{1,0:T(8,128)}, /*...) custom-call(s32[8,128]{1,0:T(8,128)} %get-tuple-element.56.start_in,, ...), custom_call_target="tpu_custom_call" | custom-call | tf_op jit(solution)/shard_map/finish/pallas_call | solution.py:1150

commit v6 on v5

--- a/solution.py
+++ b/solution.py
@@ -36,9 +36,10 @@
 CHUNK = 256
 EARLY = 512
 UP_AT = 6
-DOWN_AT = 12
+UP_START = 2
+DOWN_AT = 8
 DT = 2
-FN = 0
+FN = 1
 H_UP = 2
 H_OUT = 5
 
@@ -342,17 +343,15 @@
         vecs[i : i + 1, :] = jnp.zeros((1, model), jnp.float32) if vector is None else vector[...].reshape(1, model)
     g_out.relay(0)
     g_up.relay(0)
+    turn_rows(active, output, cot)
     fill_bias(seg_row, bias)
     g_out.relay(1)
-    g_up.relay(1)
-    g_down.open()
-    g_out.relay(2)
     for hop in range(1, p.hops):
         g_qkv.advance(hop)
+    g_up.relay(1)
+    g_out.relay(2)
     g_out.start_ring()
-    turn_rows(active, output, cot)
-    g_up.relay(2)
-    g_up.start_ring()
+    g_down.open()
     g_qkv.advance(p.hops)
     for hop in range(p.hops + 1):
         g_qkv.mate_has(hop)
@@ -364,6 +363,11 @@
         got = contract(tokens[at, :], w_qkv[:, cols], 1, 0) + vecs[pl.ds(tile, 1), :]
         got = got * jnp.where(tile == 0, HEAD_DIM ** (-0.5), 1.0)
         qkv[at, cols] = got.astype(jnp.bfloat16)
+
+        @pl.when(step == UP_START)
+        def _():
+            g_up.relay(2)
+            g_up.start_ring()
 
         @pl.when(step == 2 * (rows // CHUNK))
         def _():
@@ -944,28 +948,28 @@
     early_one = r_early.stages()[0]
     qkv_one, qkv_two = r_qkv.stages()
     up_one, up_two = r_up.stages()
-    hooks = {
-        (0, 0): out_one[:2],
-        (0, 1): down_one[-1:],
-        (H_UP // 2, H_UP % 2): up_one[2:-1],
-        (1, 1): down_two[:1],
-        (2, 0): down_two[1:-1],
-        (H_OUT // 2, H_OUT % 2): out_one[2:-1],
-        (3, 1): down_two[-1:],
-        (4, 0): early_one[:2],
-        (4, 1): up_one[-1:],
-        (5, 0): [*early_one[2:-1], *out_one[-1:]],
-        (5, 1): up_two[:1],
-    }
+    hooks = [
+        (0, out_one[:2]),
+        (1, down_one[-1:]),
+        (H_UP, up_one[2:-1]),
+        (3, down_two[:1]),
+        (4, down_two[1:-1]),
+        (H_OUT, out_one[2:-1]),
+        (7, down_two[-1:]),
+        (8, early_one[:2]),
+        (9, up_one[-1:]),
+        (10, [*early_one[2:-1], *out_one[-1:]]),
+        (11, up_two[:1]),
+    ]
 
     def attend_back(first, stop):
         def step(pair, _):
             for block in range(2):
                 pair_back(pair, block)
-                for (when, part), todo in hooks.items():
-                    if part == block and first <= when < stop:
-
-                        @pl.when(pair == when)
+                for when, todo in hooks:
+                    if when % 2 == block and first <= when // 2 < stop:
+
+                        @pl.when(pair == when // 2)
                         def _(todo=todo):
                             for stage in todo:
                                 stage()

time: 219 us -> 215 us (0.982)
  Pallas kernels: 218 us -> 214 us
    pallas_call x1, Pallas kernels: 105 us -> 102 us  [forward(): pl.pallas_call(functools.partial(forward_kernel, chips, depth), out_shape...]
where the time goes in v6:
time: 215 us
  Pallas kernels  214 us (100%)
    pallas_call x1, Pallas kernels, backward(): pl.pallas_call(functools.partial(backward_kernel, chips, depth), out_shap...  106 us
    pallas_call x1, Pallas kernels, forward(): pl.pallas_call(functools.partial(forward_kernel, chips, depth), out_shape...  102 us
    pallas_call x1, Pallas kernels, finish(): pl.pallas_call(finish_kernel, out_shape=[shape((rows, model), low), shape...  5.98 us

profile of v6, /device:TPU:0, one launch (start us, length us, event | category | flops | bytes accessed | tf_op | source)
XLA Modules:
  0.0 215.2 jit_solution(16427059302247707679)
XLA Ops:
  0.7 102.1 %forward.1 = (bf16[1024,768]{1,0:T(8,128)(2,1)}, f32[1024,768]{1,0:T(8,128)}, bf16[1024,768]{1,0:T(8,128)(2,1)}, bf16[1024,2304]{1,0:T(8,128)(2,1)}, bf16[1024,7...) custom-call(bf16[1024,768]{1,0:T(8,128)(2,1)} %tokens_in.1, ...), custom_call_target="tpu_custom_call" | custom-call | tf_op jit(solution)/shard_map/forward/pallas_call | solution.py:531
  102.8 106.3 %backward.1 = (f32[1024,768]{1,0:T(8,128)}, f32[96,576]{1,0:T(8,128)}, f32[96,192]{1,0:T(8,128)}, f32[96,768]{1,0:T(8,128)}, f32[384,192]{1,0:T(8,128)}, /*index=5*/f32[16,768]{1,0:T(8,128)}) custom-call(bf16[1024,768]{1,0:T(8,128)(2,1)} %get-tuple-element.58.two_low_in, bf16[1024,3072]{1,0:T(8,128)(2,1)} %get-tuple-element.59.active_in, ...), custom_call_target="tpu_custom_call" | custom-call | tf_op jit(solution)/shard_map/backward/pallas_call | solution.py:1053
  209.1 6.0 %finish.1 = (bf16[1024,768]{1,0:T(8,128)(2,1)}, f32[1024,768]{1,0:T(8,128)}, f32[96,576]{1,0:T(8,128)}, f32[96,192]{1,0:T(8,128)}, f32[96,768]{1,0:T(8,128)}, /*...) custom-call(s32[8,128]{1,0:T(8,128)} %get-tuple-element.56.start_in,, ...), custom_call_target="tpu_custom_call" | custom-call | tf_op jit(solution)/shard_map/finish/pallas_call | solution.py:1154
